TPU v7x, 32 devices: a whole 2x2x4 slice. The times are simulated.
32 devices in a mesh: chan: 8 (over z, core), win: 4 (over y, x).
Axes of the slice: x: 2, y: 2, z: 4, core: 2. Of those that a mesh axis runs over, the one named last changes fastest.
Arguments:
- traces: bfloat16 [4, 1024, 768], P('win', 'chan')
- pairing: int32 [2, 8], replicated, may hold values from 0 to 7, as said below
- aux_owners: int32 [1], replicated, may hold values from 0 to 7
- coda_start: int32 [1, 128], replicated, may hold values from 0 to 31
- coda_end: int32 [1, 128], replicated, may hold values from 96 to 128
Outputs:
- pair_coherence: bfloat16 [2, 1024, 256, 128], P(None, 'chan', 'win')
- coda_coherence: bfloat16 [1024, 128, 128], P('chan', 'win')
Inputs may be any that keep to these rules, and one draw needn't show every extreme that they name: `pairing`: each row is a round of a round-robin plan: it pairs every block with another block, and the block's partner names it back; the rows are different rounds.
All inputs are finite; a program needn't handle non-finite values.
Results may differ from a plain program's by a relative error of at most 0.0075.
Values may be sent and summed in bfloat16 or wider, within the bound.
No kernel may reach another device: no remote copies, remote signals or barrier semaphores. Data moves between devices by JAX's collectives and lax.ppermute only.
A program may use at most 384 MiB of HBM per device.

v0:
```python
import math

import jax
import jax.numpy as jnp
from jax import lax
from jax.sharding import PartitionSpec as P

LAGS = 256
CODA = 128
CODA_LO = 128
LAGS3 = 128


EPS = 1e-05


def whiten(traces):
    samples = traces.astype(jnp.float32)
    energy_mean = jnp.mean(samples * samples, axis=-1, keepdims=True)
    return (samples * lax.rsqrt(energy_mean + EPS)).astype(jnp.bfloat16)


def correlate(sources, receivers, lag_first, lag_count, lag_group, margin, form, join_axis):
    length = receivers.shape[2]
    padded = jnp.pad(receivers, ((0, 0), (0, 0), (0, margin)))
    window = lax.dynamic_slice_in_dim(padded, lag_first, length + lag_count, 2)
    pieces = []
    for offset in range(0, lag_count, lag_group):
        shifted = jnp.stack(
            [
                window[:, :, offset + lag_value : offset + lag_value + length]
                for lag_value in range(lag_group)
            ]
        )
        pieces.append(
            jnp.einsum("wit,lwjt->" + form, sources, shifted, preferred_element_type=jnp.float32)
        )
    return jnp.concatenate(pieces, axis=join_axis)


def per_device(traces, pairing, aux_owners, coda_start, coda_end):
    win_size = lax.axis_size("win")
    chan_size = lax.axis_size("chan")
    win_index = lax.axis_index("win")
    chan_index = lax.axis_index("chan")
    window_count, block_width, window_length = traces.shape
    rows_dev = window_count * block_width
    rounds = pairing.shape[0]
    aux_count = aux_owners.shape[0]
    whitened = whiten(traces).reshape(rows_dev, window_length)
    partners = lax.dynamic_index_in_dim(pairing, chan_index, 1, keepdims=False)
    gathered = lax.all_gather(whitened, ("chan", "win"), axis=0, tiled=True)
    every_block = gathered.reshape(chan_size, win_size * window_count, block_width, window_length)
    own_all = lax.dynamic_index_in_dim(every_block, chan_index, 0, keepdims=False)
    partner_all = jnp.take(every_block, partners, axis=0)
    aux_every = jnp.take(every_block, aux_owners, axis=0)
    aux_mine = lax.dynamic_slice_in_dim(aux_every, win_index * window_count, window_count, 1)
    scale_two = 1.0 / math.sqrt(win_size * window_count * window_length)
    lag_share = LAGS // win_size
    lag_first = win_index * lag_share
    pair_group = math.gcd(lag_share, 16)
    collected = []
    for round_index in range(rounds):
        collected.append(
            correlate(
                own_all, partner_all[round_index], lag_first, lag_share, pair_group, LAGS, "ilj", 1
            )
        )
    pair_out = (jnp.stack(collected) * scale_two).astype(jnp.bfloat16)
    coda_group = math.gcd(CODA, 32)
    own_mine = whitened.reshape(window_count, block_width, window_length)
    partials = (
        jnp.stack(
            [correlate(aux_mine[0], own_mine, CODA_LO, CODA, coda_group, CODA_LO + CODA, "jil", 2)],
            axis=1,
        )
        * scale_two
    )
    summed = lax.psum(partials.astype(jnp.bfloat16), "win").astype(jnp.float32)
    lag_axis = jnp.arange(CODA, dtype=jnp.int32)
    live = (lag_axis[None, None, :] >= coda_start[:, :, None]) & (
        lag_axis[None, None, :] < coda_end[:, :, None]
    )
    coda = jnp.where(live[None], summed, 0.0).astype(jnp.bfloat16)
    three_share = LAGS3 // win_size
    three_first = win_index * three_share
    three_group = math.gcd(three_share, 8)
    padded = jnp.pad(coda, ((0, 0), (0, 0), (0, 0), (0, LAGS3)))
    window = lax.dynamic_slice_in_dim(padded, three_first, CODA + three_share, 3)
    pieces = []
    for offset in range(0, three_share, three_group):
        shifted = jnp.stack(
            [
                window[:, :, :, offset + lag_value : offset + lag_value + CODA]
                for lag_value in range(three_group)
            ]
        )
        pieces.append(
            jnp.einsum("iksu,ljksu->ilj", coda, shifted, preferred_element_type=jnp.float32)
        )
    three_out = jnp.concatenate(pieces, axis=1)
    scale_three = 1.0 / math.sqrt(aux_count * block_width * CODA)
    return (pair_out, (three_out * scale_three).astype(jnp.bfloat16))


def solution(mesh):
    in_specs = (P("win", "chan", None), P(), P(), P(), P())
    out_specs = (P(None, "chan", "win", None), P("chan", "win", None))
    return jax.shard_map(
        per_device, mesh=mesh, in_specs=in_specs, out_specs=out_specs, check_vma=False
    )
```

profile of v0, /device:TPU:8, one launch (start us, length us, event | category | flops | bytes accessed | tf_op | source)
XLA Modules:
  0.0 492.9 jit_solution(9468264591209402900)
XLA Ops:
  94.8 4.7 fusion.87
  99.6 15.2 %fusion.90 = f32[128,1,128,32]{2,0,3,1:T(8,128)S(1)} fusion(bf16[32,1,128,768]{3,2,1,0:T(8,128)(2,1)S(1)} %bitcast.1378, bf16[8,4,128,768]{3,2,1,0:T(8,128)(2,1)} %bitcast.1383, s32[]{:T(128)} %bitcast.218, s32[]{:T(128)S(6)} %select_n.54, pred[]{:T(512)} %bitcast.217), kind=kOutput, calls=%fused_computation.127 | convolution fusion | flops 805404672 | bytes 8586244 | tf_op jit(solution)/shard_map/wit,lwjt->jil/dot_general | solution.py:36
  145.2 4.5 copy-done.2
  153.5 7.7 %convolution_bitcast_fusion.7 = f32[128,16,128]{2,0,1:T(8,128)S(1)} fusion(bf16[16,4,128,768]{3,2,1,0:T(8,128)(2,1)} %get-tuple-element.26, bf16[8,4,128,768]{3,2,1,0:T(8,128)(2,1)} %bitcast.1386, s32[]{:T(128)S(6)} %select_n.48), kind=kOutput, calls=%fused_computation.266 | convolution fusion | flops 1610612736 | bytes 14417924 | tf_op jit(solution)/shard_map/wit,lwjt->ilj/dot_general | solution.py:36
  180.6 10.9 %convolution_bitcast_fusion.6 = f32[128,16,128]{2,0,1:T(8,128)} fusion(bf16[16,4,128,768]{3,2,1,0:T(8,128)(2,1)} %get-tuple-element.30, bf16[8,4,128,768]{3,2,1,0:T(8,128)(2,1)} %bitcast.1387, s32[]{:T(128)S(6)} %select_n.48), kind=kOutput, calls=%fused_computation.265 | convolution fusion | flops 1610612736 | bytes 14417924 | tf_op jit(solution)/shard_map/wit,lwjt->ilj/dot_general | solution.py:36
  197.5 6.2 %convolution_bitcast_fusion.5 = f32[128,16,128]{2,0,1:T(8,128)} fusion(bf16[16,4,128,768]{3,2,1,0:T(8,128)(2,1)S(1)} %get-tuple-element.33, bf16[8,4,128,768]{3,2,1,0:T(8,128)(2,1)} %bitcast.1388, s32[]{:T(128)S(6)} %select_n.48), kind=kOutput, calls=%fused_computation.264 | convolution fusion | flops 1610612736 | bytes 14417924 | tf_op jit(solution)/shard_map/wit,lwjt->ilj/dot_general | solution.py:36
  251.2 10.1 %convolution_bitcast_fusion.4 = f32[128,16,128]{2,0,1:T(8,128)} fusion(bf16[16,4,128,768]{3,2,1,0:T(8,128)(2,1)} %fusion.120, bf16[8,4,128,768]{3,2,1,0:T(8,128)(2,1)} %bitcast.1389, s32[]{:T(128)S(6)} %select_n.48), kind=kOutput, calls=%fused_computation.263 | convolution fusion | flops 1610612736 | bytes 14417924 | tf_op jit(solution)/shard_map/wit,lwjt->ilj/dot_general | solution.py:36
  265.3 7.2 %convolution_bitcast_fusion.3 = f32[128,16,128]{2,0,1:T(8,128)S(1)} fusion(bf16[16,4,128,768]{3,2,1,0:T(8,128)(2,1)} %get-tuple-element.35, bf16[8,4,128,768]{3,2,1,0:T(8,128)(2,1)} %bitcast.1390, s32[]{:T(128)S(6)} %select_n.48), kind=kOutput, calls=%fused_computation.262 | convolution fusion | flops 1610612736 | bytes 14417924 | tf_op jit(solution)/shard_map/wit,lwjt->ilj/dot_general | solution.py:36
  272.5 7.2 %convolution_bitcast_fusion.2 = f32[128,16,128]{2,0,1:T(8,128)S(1)} fusion(bf16[16,4,128,768]{3,2,1,0:T(8,128)(2,1)} %copy-done.1, bf16[8,4,128,768]{3,2,1,0:T(8,128)(2,1)} %bitcast.1391, s32[]{:T(128)S(6)} %select_n.48), kind=kOutput, calls=%fused_computation.261 | convolution fusion | flops 1610612736 | bytes 14417924 | tf_op jit(solution)/shard_map/wit,lwjt->ilj/dot_general | solution.py:36
  279.8 5.2 %convolution_bitcast_fusion.1 = f32[128,16,128]{2,0,1:T(8,128)S(1)} fusion(bf16[16,4,128,768]{3,2,1,0:T(8,128)(2,1)S(1)} %get-tuple-element.42, bf16[8,4,128,768]{3,2,1,0:T(8,128)(2,1)} %bitcast.1392, s32[]{:T(128)S(6)} %select_n.48), kind=kOutput, calls=%fused_computation.260 | convolution fusion | flops 1610612736 | bytes 14417924 | tf_op jit(solution)/shard_map/wit,lwjt->ilj/dot_general | solution.py:36
  285.0 7.2 %convolution_bitcast_fusion = f32[128,16,128]{2,0,1:T(8,128)S(1)} fusion(bf16[16,4,128,768]{3,2,1,0:T(8,128)(2,1)} %fusion.248, bf16[8,4,128,768]{3,2,1,0:T(8,128)(2,1)} %bitcast.1393, s32[]{:T(128)S(6)} %select_n.48), kind=kOutput, calls=%fused_computation.259 | convolution fusion | flops 1610612736 | bytes 14417924 | tf_op jit(solution)/shard_map/wit,lwjt->ilj/dot_general | solution.py:36
  295.6 4.7 copy.46
  307.9 4.1 fusion.23
  315.9 4.4 fusion.27
  324.3 4.1 fusion.31
  332.3 10.0 %fusion.35 = (bf16[8,128,1,128,128]{3,1,4,2,0:T(8,128)(2,1)}, bf16[8,128,1,128,128]{3,1,4,2,0:T(8,128)(2,1)}, bf16[8,128,1,128,128]{3,1,4,2,0:T(8,128)(2,1)}, bf16[8,128,1,128,128]{3,1,4,2,0:T(8,128)(2,1)}) fusion(bf16[8,128,1,128,128]{3,1,4,2,0:T(8,128)(2,1)} %fusion.33, s32[]{:T(128)S(6)} %add.192, bf16[128,1,128,128]{2,0,3,1:T(8,128)(2,1)S(1)} %select_convert_fusion, ...), kind=kLoop, calls=%fused_computation.71 | loop fusion | bytes 20971536 | tf_op jit(solution)/shard_map/stack | solution.py:92
  342.3 16.0 %fusion.99 = f32[128,8,128]{2,0,1:T(8,128)S(1)} fusion(bf16[8,128,1,128,128]{3,1,4,2,0:T(8,128)(2,1)} %get-tuple-element.15, bf16[128,1,128,128]{2,0,3,1:T(8,128)(2,1)S(1)} %select_convert_fusion), kind=kOutput, calls=%fused_computation.267 | convolution fusion | flops 4294967296 | bytes 38273024 | tf_op jit(solution)/shard_map/iksu,ljksu->ilj/dot_general | solution.py:99
  378.3 4.4 fusion.49
  382.7 7.7 %fusion.51 = (bf16[8,128,1,128,128]{3,1,4,2,0:T(8,128)(2,1)}, bf16[8,128,1,128,128]{3,1,4,2,0:T(8,128)(2,1)}, bf16[8,128,1,128,128]{3,1,4,2,0:T(8,128)(2,1)}) fusion(bf16[8,128,1,128,128]{3,1,4,2,0:T(8,128)(2,1)} %fusion.49, s32[]{:T(128)S(6)} %add.200, bf16[128,1,128,128]{2,0,3,1:T(8,128)(2,1)S(1)} %select_convert_fusion, ...), kind=kLoop, calls=%fused_computation.87 | loop fusion | bytes 16777228 | tf_op jit(solution)/shard_map/stack | solution.py:92
  390.4 15.8 %fusion.104 = f32[128,8,128]{2,0,1:T(8,128)S(1)} fusion(bf16[8,128,1,128,128]{3,1,4,2,0:T(8,128)(2,1)} %get-tuple-element.19, bf16[128,1,128,128]{2,0,3,1:T(8,128)(2,1)S(1)} %select_convert_fusion), kind=kOutput, calls=%fused_computation.268 | convolution fusion | flops 4294967296 | bytes 38273024 | tf_op jit(solution)/shard_map/iksu,ljksu->ilj/dot_general | solution.py:99
  426.2 6.2 %fusion.67 = (bf16[8,128,1,128,128]{3,1,4,2,0:T(8,128)(2,1)}, bf16[8,128,1,128,128]{3,1,4,2,0:T(8,128)(2,1)}) fusion(bf16[8,128,1,128,128]{3,1,4,2,0:T(8,128)(2,1)} %fusion.65, s32[]{:T(128)S(6)} %add.208, bf16[128,1,128,128]{2,0,3,1:T(8,128)(2,1)S(1)} %select_convert_fusion, bf16[8,128,1,128,128]{3,1,4,2,0:T(8,128)(2,1)} %get-tuple-element.21, s32[]{:T(128)S(6)} %add.211), kind=kLoop, calls=%fused_computation.103 | loop fusion | bytes 12582920 | tf_op jit(solution)/shard_map/stack | solution.py:92
  432.4 15.8 %fusion.109 = f32[128,8,128]{2,0,1:T(8,128)S(1)} fusion(bf16[8,128,1,128,128]{3,1,4,2,0:T(8,128)(2,1)} %get-tuple-element.22, bf16[128,1,128,128]{2,0,3,1:T(8,128)(2,1)S(1)} %select_convert_fusion), kind=kOutput, calls=%fused_computation.269 | convolution fusion | flops 4294967296 | bytes 38273024 | tf_op jit(solution)/shard_map/iksu,ljksu->ilj/dot_general | solution.py:99
  452.2 4.1 fusion.77
  468.2 15.8 %fusion.114 = f32[128,8,128]{2,0,1:T(8,128)S(1)} fusion(bf16[8,128,1,128,128]{3,1,4,2,0:T(8,128)(2,1)} %fusion.19, bf16[128,1,128,128]{2,0,3,1:T(8,128)(2,1)S(1)} %select_convert_fusion), kind=kOutput, calls=%fused_computation.270 | convolution fusion | flops 4294967296 | bytes 38273024 | tf_op jit(solution)/shard_map/iksu,ljksu->ilj/dot_general | solution.py:99
  (317 shorter events, 277.5 us)
Async XLA Ops:
  7.2 40.2 %copy-start.7 = (s32[2,8]{1,0:T(2,128)S(1)}, s32[2,8]{1,0:T(2,128)}, u32[]{:S(2)}) copy-start(s32[2,8]{1,0:T(2,128)} %param.6) | copy-start | bytes 196
  7.2 83.8 %all-gather.3.cloned.1.call-start = ((), (), s32[]{:S(2)}) async-start(), calls=%async_computation.1 | async-start | bytes 6488064 | tf_op jit(solution)/shard_map/all_gather | solution.py:52
  10.0 35.8 %copy-start = (bf16[1,128,768]{2,1,0:T(8,128)(2,1)S(1)}, bf16[1,128,768]{2,1,0:T(8,128)(2,1)}, u32[]{:S(2)}) copy-start(bf16[1,128,768]{2,1,0:T(8,128)(2,1)} %fusion.384) | copy-start | bytes 589828
  10.0 290.4 %all-reduce.6.cloned.1.call-start = ((), (), s32[]{:S(2)}) async-start(), calls=%async_computation | async-start | bytes 8388608 | tf_op jit(solution)/shard_map/psum | solution.py:79
  83.3 7.6 %copy-start.8 = (s32[1,128]{1,0:T(1,128)S(1)}, s32[1,128]{1,0:T(1,128)}, u32[]{:S(2)}) copy-start(s32[1,128]{1,0:T(1,128)} %param.9) | copy-start | bytes 1540
  83.3 7.6 %copy-start.9 = (s32[1,128]{1,0:T(1,128)S(1)}, s32[1,128]{1,0:T(1,128)}, u32[]{:S(2)}) copy-start(s32[1,128]{1,0:T(1,128)} %param.8) | copy-start | bytes 1540
  84.8 6.2 %copy-start.4 = (bf16[32,1,128,768]{3,2,1,0:T(8,128)(2,1)}, bf16[32,1,128,768]{3,2,1,0:T(8,128)(2,1)S(1)}, u32[]{:S(2)}) copy-start(bf16[32,1,128,768]{3,2,1,0:T(8,128)(2,1)S(1)} %get-tuple-element.47) | copy-start | bytes 18874372
  88.3 2.6 copy-start.3
  94.7 4.9 slice-start.2
  94.8 4.8 slice-start.3
  99.5 15.2 %slice-start.4 = ((s8[6291456]{0:T(1024)(128)(4,1)}), s8[4194304]{0:T(1024)(128)(4,1)S(1)}, s32[]{:S(2)}) async-start(s8[6291456]{0:T(1024)(128)(4,1)} %bitcast.1379), calls=%async_computation.6 | async-start | bytes 8388608
  99.6 15.2 %slice-start.5 = ((s8[6291456]{0:T(1024)(128)(4,1)}), s8[2097152]{0:T(1024)(128)(4,1)S(1)}, s32[]{:S(2)}) async-start(s8[6291456]{0:T(1024)(128)(4,1)} %bitcast.1379), calls=%async_computation.7 | async-start | bytes 4194304
  114.8 3.0 slice-start
  114.8 3.0 slice-start.1
  145.1 4.5 copy-start.2
  212.7 4.5 copy-start.1
  251.2 10.1 %copy-start.6 = (f32[128,16,128]{2,0,1:T(8,128)S(1)}, f32[128,16,128]{2,0,1:T(8,128)}, u32[]{:S(2)}) copy-start(f32[128,16,128]{2,0,1:T(8,128)} %convolution_bitcast_fusion.6) | copy-start | bytes 3145732
  292.2 2.2 copy-start.5
Sparse Core Ops, SparseCore 0:
  11.5 70.7 all-gather.2
  123.4 105.0 all-reduce.5
where the time goes:
time: 503 us; the launch traced here: 493 us
  local copies, waits for them, and re-layouts  310 us (62%)
  matrix products  151 us (30%)
  between operations  16.1 us (3%)
  other arithmetic  15.7 us (3%)
    unnamed x284, local copies, waits for them, and re-layouts  261 us
    dot_general x12, matrix products, correlate(): jnp.einsum('wit,lwjt->' + form, sources, shifted, preferred_element_type=...  87.4 us
    dot_general x4, matrix products, per_device(): jnp.einsum('iksu,ljksu->ilj', coda, shifted, preferred_element_type=jnp.f...  63.3 us
    another operation x4, local copies, waits for them, and re-layouts, per_device(): jnp.stack([window[:, :, :, offset + lag_value:offset + lag_value + CODA]...  28 us
    another operation x12, local copies, waits for them, and re-layouts, correlate(): jnp.stack([window[:, :, offset + lag_value:offset + lag_value + length] f...  17.2 us
  transfers between devices with their start and end apart: 2, of which 0 were waited for; matrix products, arithmetic and copies ran while one was open for 50% of the time, Pallas kernels for 0%

commit v1 on v0

v1 whole, which is shorter than its diff:
```python
import functools
import math

import jax
import jax.numpy as jnp
from jax import lax
from jax.experimental import pallas as pl
from jax.experimental.pallas import tpu as pltpu
from jax.sharding import PartitionSpec as P

LAGS = 256
CODA = 128
CODA_LO = 128
LAGS3 = 128
EPS = 1e-05
STEP = 16
GROUP = 4
VMEM_LIMIT = 60 << 20

f32 = jnp.float32
bf16 = jnp.bfloat16


def whiten(traces):
    samples = traces.astype(f32)
    energy_mean = jnp.mean(samples * samples, axis=-1, keepdims=True)
    return (samples * lax.rsqrt(energy_mean + EPS)).astype(bf16)


def shift_right(block, count):
    if count == 0:
        return block.astype(bf16)
    moved = pltpu.roll(block, count, 1)
    lane = lax.broadcasted_iota(jnp.int32, block.shape, 1)
    return jnp.where(lane < count, 0.0, moved).astype(bf16)


def coda_kernel(win_ref, aux_ref, own_ref, start_ref, end_ref, out_ref, shifted, own_t, coda, coda_t, acc, rows):
    windows, blk, length = own_ref.shape
    used = length - CODA_LO
    share = out_ref.shape[1]
    steps = share // 2
    pairs = CODA // 2
    scale_two = 1.0 / math.sqrt(windows * length)
    scale_three = 1.0 / math.sqrt(blk * CODA)
    win = win_ref[0]

    for w in range(windows):
        own_t[w, :length, :] = own_ref[w].T
        own_t[w, length:, :] = jnp.zeros((own_t.shape[1] - length, blk), bf16)
        samples = aux_ref[w][:, :used].astype(f32)
        for b in range(STEP):
            shifted[b * blk : (b + 1) * blk, w * used : (w + 1) * used] = shift_right(samples, b)
    coda[CODA * blk :, :] = jnp.zeros((coda.shape[0] - CODA * blk, blk), bf16)
    coda_t[: (steps - 1) * blk, :] = jnp.zeros(((steps - 1) * blk, 2 * blk), bf16)

    half = STEP // 2

    def part(step, _):
        a_pair = step // 2
        b_half = step % 2
        pieces = []
        for w in range(windows):
            halves = [
                own_t[w, pl.ds(pl.multiple_of(CODA_LO + (2 * a_pair + a) * STEP, STEP), used), :]
                for a in range(2)
            ]
            pieces.append(jnp.concatenate(halves, axis=1))
        weights = jnp.concatenate(pieces, axis=0)
        first = pl.multiple_of(b_half * half * blk, blk)
        result = jnp.dot(shifted[pl.ds(first, half * blk), :], weights, preferred_element_type=f32)
        for b in range(half):
            for a in range(2):
                lag = (2 * a_pair + a) * STEP + b_half * half + b
                tile = result[b * blk : (b + 1) * blk, a * blk : (a + 1) * blk] * scale_two
                live = (lag >= start_ref[...]) & (lag < end_ref[...])
                tile = jnp.where(live, tile, 0.0)
                coda[pl.ds(pl.multiple_of(lag * blk, blk), blk), :] = tile.astype(bf16)
                row = pl.multiple_of((lag // 2 + steps - 1) * blk, blk)
                coda_t[pl.ds(row, blk), (b % 2) * blk : (b % 2 + 1) * blk] = tile.T.astype(bf16)
        return 0

    lax.fori_loop(0, CODA // STEP, part, 0)

    acc[...] = jnp.zeros(acc.shape, f32)

    def accumulate(group, blocks):
        lhs, rhs = [], []
        for q in range(GROUP):
            pair = group * GROUP + q
            row = (pair + steps - blocks) * blk
            lhs.append(coda_t[pl.ds(pl.multiple_of(row, blk), blocks * blk), :])
            first = (2 * pair + win * share) * blk
            rhs.append(
                jnp.concatenate(
                    [coda[pl.ds(pl.multiple_of(first + b * blk, blk), 2 * blk), :] for b in range(2)], axis=1
                )
            )
        value = jnp.dot(
            jnp.concatenate(lhs, axis=1), jnp.concatenate(rhs, axis=0), preferred_element_type=f32
        )
        acc[(steps - blocks) * blk :, :] += value

    peeled = steps // GROUP - 1
    for group in range(peeled):
        accumulate(group, (group + 1) * GROUP)
    groups = pairs // GROUP - win * (share // (2 * GROUP))

    def whole(group, _):
        accumulate(group, steps)
        return 0

    lax.fori_loop(peeled, groups, whole, 0)
    for i in range(steps):
        for b in range(2):
            lag = 2 * (steps - 1 - i) + b
            rows[pl.ds(lag, blk, stride=share), :] = (
                acc[i * blk : (i + 1) * blk, b * blk : (b + 1) * blk] * scale_three
            )
    out_ref[...] = rows[...].reshape(blk, share, blk).astype(bf16)


def pair_kernel(win_ref, own_ref, partner_ref, out_ref, shifted, partner_t, rows):
    windows, blk, length = own_ref.shape
    rounds = partner_ref.shape[1]
    share = out_ref.shape[2]
    scale_two = 1.0 / math.sqrt(windows * length)
    win = win_ref[0]
    for w in range(windows):
        for r in range(rounds):
            partner_t[w, :length, r * blk : (r + 1) * blk] = partner_ref[w, r].T
        partner_t[w, length:, :] = jnp.zeros((partner_t.shape[1] - length, rounds * blk), bf16)
        samples = own_ref[w].astype(f32)
        for b in range(STEP):
            shifted[b * blk : (b + 1) * blk, w * length : (w + 1) * length] = shift_right(samples, b)

    half = STEP // 2

    def pair(step, _):
        a = step // 2
        b_half = step % 2
        first = pl.multiple_of(win * share + a * STEP, STEP)
        weights = jnp.concatenate([partner_t[w, pl.ds(first, length), :] for w in range(windows)], axis=0)
        row = pl.multiple_of(b_half * half * blk, blk)
        result = jnp.dot(shifted[pl.ds(row, half * blk), :], weights, preferred_element_type=f32)
        for b in range(half):
            lag = a * STEP + b_half * half + b
            for r in range(rounds):
                rows[r, pl.ds(lag, blk, stride=share), :] = (
                    result[b * blk : (b + 1) * blk, r * blk : (r + 1) * blk] * scale_two
                )
        return 0

    lax.fori_loop(0, 2 * (share // STEP), pair, 0)
    for r in range(rounds):
        out_ref[r] = rows[r].reshape(blk, share, blk).astype(bf16)


SMEM_SPEC = pl.BlockSpec(memory_space=pltpu.SMEM)
VMEM_SPEC = pl.BlockSpec(memory_space=pltpu.VMEM)


def coda_coherence(win, aux, own, start, end, share):
    windows, blk, length = own.shape
    used = length - CODA_LO
    steps = share // 2
    return pl.pallas_call(
        coda_kernel,
        out_shape=jax.ShapeDtypeStruct((blk, share, blk), bf16),
        in_specs=[SMEM_SPEC] + [VMEM_SPEC] * 4,
        out_specs=VMEM_SPEC,
        scratch_shapes=[
            pltpu.VMEM((STEP * blk, windows * used), bf16),
            pltpu.VMEM((windows, length + CODA, blk), bf16),
            pltpu.VMEM(((CODA + 1) * blk, blk), bf16),
            pltpu.VMEM(((CODA // 2 + steps - 1) * blk, 2 * blk), bf16),
            pltpu.VMEM((steps * blk, 2 * blk), f32),
            pltpu.VMEM((share * blk, blk), f32),
        ],
        compiler_params=pltpu.CompilerParams(vmem_limit_bytes=VMEM_LIMIT),
        name="coda_coherence",
    )(win, aux, own, start, end)


def pair_coherence(win, own, partner, share):
    windows, blk, length = own.shape
    rounds = partner.shape[1]
    return pl.pallas_call(
        pair_kernel,
        out_shape=jax.ShapeDtypeStruct((rounds, blk, share, blk), bf16),
        in_specs=[SMEM_SPEC] + [VMEM_SPEC] * 2,
        out_specs=VMEM_SPEC,
        scratch_shapes=[
            pltpu.VMEM((STEP * blk, windows * length), bf16),
            pltpu.VMEM((windows, length + LAGS, rounds * blk), bf16),
            pltpu.VMEM((rounds, blk * share, blk), f32),
        ],
        compiler_params=pltpu.CompilerParams(vmem_limit_bytes=VMEM_LIMIT),
        name="pair_coherence",
    )(win, own, partner)


def per_device(traces, pairing, aux_owners, coda_start, coda_end):
    win_size = lax.axis_size("win")
    chan_size = lax.axis_size("chan")
    win_index = lax.axis_index("win")
    chan_index = lax.axis_index("chan")
    blk = traces.shape[1]
    white = whiten(traces)[0]

    def exchange(block, k):
        return lax.ppermute(block, "win", [(i, i ^ k) for i in range(win_size)])

    own_all = jnp.stack([white] + [exchange(white, k) for k in range(1, win_size)])
    same_core = [list(range(core, chan_size, 2)) for core in range(2)]
    column = lax.all_gather(white, "chan", axis=0, axis_index_groups=same_core)
    other = lax.ppermute(column, "chan", [(i, i ^ 1) for i in range(chan_size)])
    both = jnp.stack([column, other])

    def pick(block):
        return both[(block % 2) ^ (chan_index % 2), block // 2]

    aux = pick(aux_owners[0])
    partners = jnp.stack([pick(pairing[r, chan_index]) for r in range(pairing.shape[0])])
    aux_all = jnp.stack([aux] + [exchange(aux, k) for k in range(1, win_size)])
    partner_all = jnp.stack([partners] + [exchange(partners, k) for k in range(1, win_size)])
    win = win_index.reshape(1).astype(jnp.int32)
    start = jnp.broadcast_to(coda_start[0][:, None], (blk, blk))
    end = jnp.broadcast_to(coda_end[0][:, None], (blk, blk))
    three = coda_coherence(win, aux_all, own_all, start, end, LAGS3 // win_size)
    pair = pair_coherence(win, own_all, partner_all, LAGS // win_size)
    return (pair, three)


def solution(mesh):
    in_specs = (P("win", "chan", None), P(), P(), P(), P())
    out_specs = (P(None, "chan", "win", None), P("chan", "win", None))
    return jax.shard_map(per_device, mesh=mesh, in_specs=in_specs, out_specs=out_specs, check_vma=False)
```

time: 503 us -> 136 us (0.27)
  the two profiles are of different devices: /device:TPU:8 before, /device:TPU:0 now
where the time goes in v1:
time: 136 us
  Pallas kernels  68.9 us (51%)
  blocking collectives  21.3 us (16%)
  waiting for transfers between devices  19.5 us (14%)
  starting transfers between devices  11.6 us (9%)
  between operations  6.6 us (5%)
  other arithmetic  5.86 us (4%)
  local copies, waits for them, and re-layouts  2.06 us (2%)
    pallas_call x1, Pallas kernels, coda_coherence(): pl.pallas_call(coda_kernel, out_shape=jax.ShapeDtypeStruct((blk, share, b...  39.3 us
    pallas_call x1, Pallas kernels, pair_coherence(): pl.pallas_call(pair_kernel, out_shape=jax.ShapeDtypeStruct((rounds, blk,...  29.6 us
    all_gather x1, blocking collectives, per_device(): column = lax.all_gather(white, 'chan', axis=0, axis_index_groups=same_core)  21.3 us
    ppermute x9, waiting for transfers between devices, exchange(): return lax.ppermute(block, 'win', [(i, i ^ k) for i in range(win_size)])  19.5 us
    ppermute x9, starting transfers between devices, exchange(): return lax.ppermute(block, 'win', [(i, i ^ k) for i in range(win_size)])  11.6 us
  transfers between devices with their start and end apart: 10, of which 3 were waited for; matrix products, arithmetic and copies ran while one was open for 3% of the time, Pallas kernels for 29%

profile of v1, /device:TPU:0, one launch (start us, length us, event | category | flops | bytes accessed | tf_op | source)
XLA Modules:
  0.0 135.8 jit_solution(7507702129151296780)
XLA Ops:
  0.7 1.1 fusion
  1.8 1.0 fusion.1
  2.8 21.3 %all_gather.3 = bf16[4,128,768]{2,1,0:T(8,128)(2,1)S(1)} all-gather(bf16[1,128,768]{2,1,0:T(8,128)(2,1)S(1)} %fusion.1), channel_id=1, replica_groups={{0,8,16,24},{4,12,20,28},{1,9,17,25},{5,13,21,29},{2,10,18,26},{6,14,22..., dimensions={0}, use_global_device_ids=true | all-gather | bytes 983040 | tf_op jit(solution)/shard_map/all_gather | solution.py:216
  24.2 2.5 %collective-permute-start.2 = (bf16[128,768]{1,0:T(8,128)(2,1)S(1)}, bf16[128,768]{1,0:T(8,128)(2,1)S(1)}, u32[]{:S(2)}, u32[]{:S(2)}) collective-permute-start(bf16[128,768]{1,0:T(8,128)(2,1)S(1)} %fusion.8), channel_id=1, source_target_pairs={{0,3},{1,2},{2,1},{3,0},{4,7},{5,6},{6,5},{7,4},{8,11},{9,10},{10,... | collective-permute-start | bytes 589832 | tf_op jit(solution)/shard_map/ppermute | solution.py:212
  26.7 0.5 collective-permute-start.1
  27.2 0.5 collective-permute-start
  28.5 0.6 constant_dynamic-slice_fusion
  34.3 0.2 fusion.2
  34.5 2.5 %collective-permute-start.9 = (bf16[128,768]{1,0:T(8,128)(2,1)S(1)}, bf16[128,768]{1,0:T(8,128)(2,1)S(1)}, u32[]{:S(2)}, u32[]{:S(2)}) collective-permute-start(bf16[128,768]{1,0:T(8,128)(2,1)S(1)} %bitcast.32), channel_id=1, source_target_pairs={{0,3},{1,2},{2,1},{3,0},{4,7},{5,6},{6,5},{7,4},{8,11},{9,10},{10,... | collective-permute-start | bytes 589832 | tf_op jit(solution)/shard_map/ppermute | solution.py:212
  37.1 0.5 collective-permute-start.6
  37.7 1.5 %collective-permute-start.5 = (bf16[2,128,768]{2,1,0:T(8,128)(2,1)S(1)}, bf16[2,128,768]{2,1,0:T(8,128)(2,1)S(1)}, u32[]{:S(2)}, u32[]{:S(2)}) collective-permute-start(bf16[2,128,768]{2,1,0:T(8,128)(2,1)S(1)} %get-tuple-element.6), channel_id=1, source_target_pairs={{0,2},{1,3},{2,0},{3,1},{4,6},{5,7},{6,4},{7,5},{8,10},{9,11},{10,... | collective-permute-start | bytes 1179656 | tf_op jit(solution)/shard_map/ppermute | solution.py:212
  39.2 1.5 %collective-permute-start.4 = (bf16[2,128,768]{2,1,0:T(8,128)(2,1)S(1)}, bf16[2,128,768]{2,1,0:T(8,128)(2,1)S(1)}, u32[]{:S(2)}, u32[]{:S(2)}) collective-permute-start(bf16[2,128,768]{2,1,0:T(8,128)(2,1)S(1)} %get-tuple-element.6), channel_id=1, source_target_pairs={{0,1},{1,0},{2,3},{3,2},{4,5},{5,4},{6,7},{7,6},{8,9},{9,8},{10,11... | collective-permute-start | bytes 1179656 | tf_op jit(solution)/shard_map/ppermute | solution.py:212
  40.7 0.5 collective-permute-start.8
  41.2 2.2 %collective-permute-done.9 = bf16[128,768]{1,0:T(8,128)(2,1)S(1)} collective-permute-done((bf16[128,768]{1,0:T(8,128)(2,1)S(1)}, bf16[128,768]{1,0:T(8,128)(2,1)S(1)}, u32[]{:S(2)}, u32[]{:S(2)}) %collective-permute-start.9) | collective-permute-done | bytes 196640 | tf_op jit(solution)/shard_map/ppermute | solution.py:212
  43.4 1.5 %collective-permute-start.7 = (bf16[128,768]{1,0:T(8,128)(2,1)S(1)}, bf16[128,768]{1,0:T(8,128)(2,1)S(1)}, u32[]{:S(2)}, u32[]{:S(2)}) collective-permute-start(bf16[128,768]{1,0:T(8,128)(2,1)S(1)} %bitcast.34), channel_id=1, source_target_pairs={{0,1},{1,0},{2,3},{3,2},{4,5},{5,4},{6,7},{7,6},{8,9},{9,8},{10,11... | collective-permute-start | bytes 589832 | tf_op jit(solution)/shard_map/ppermute | solution.py:212
  44.9 1.0 pad_maximum_fusion.1.own_ref
  45.9 17.2 %collective-permute-done.8 = bf16[128,768]{1,0:T(8,128)(2,1)S(1)} collective-permute-done((bf16[128,768]{1,0:T(8,128)(2,1)S(1)}, bf16[128,768]{1,0:T(8,128)(2,1)S(1)}, u32[]{:S(2)}, u32[]{:S(2)}) %collective-permute-start.8) | collective-permute-done | bytes 196640 | tf_op jit(solution)/shard_map/ppermute | solution.py:212
  63.0 0.1 collective-permute-done.7
  63.1 1.0 pad_maximum_fusion.2.aux_ref
  64.1 0.7 broadcast_in_dim.16.start_ref
  64.8 0.7 broadcast_in_dim.18.end_ref
  65.5 39.3 %coda_coherence.1 = bf16[128,32,128]{2,1,0:T(8,128)(2,1)} custom-call(s32[1]{0:T(128)} %bitcast.win_ref, bf16[4,128,768]{2,1,0:T(8,128)(2,1)} %pad_maximum_fusion.2.aux_ref, bf16[4,128,768]{2,1,0:T(8,128)(2,1)} %pad_maximum_fusion.1.own_ref, s32[128,128]{1,0:T(8,128)} %broadcast_in_dim.16.start_ref, s32[128,128]{1,0:T(8,128)} %broadcast_in_dim.18.end_ref), custom_call_target="tpu_custom_call" | custom-call | tf_op jit(solution)/shard_map/coda_coherence/pallas_call | solution.py:167
  104.9 1.4 %pad_maximum_fusion.partner_ref = bf16[4,2,128,768]{3,2,1,0:T(8,128)(2,1)} fusion(bf16[1,2,128,768]{3,2,1,0:T(8,128)(2,1)S(1)} %bitcast.37, bf16[1,2,128,768]{3,2,1,0:T(8,128)(2,1)S(1)} %bitcast.38, bf16[1,2,128,768]{3,2,1,0:T(8,128)(2,1)S(1)} %bitcast.39, bf16[1,2,128,768]{3,2,1,0:T(8,128)(2,1)S(1)} %get-tuple-element.5), kind=kLoop, calls=%fused_computation.6 | loop fusion | flops 2359296 | bytes 3145728 | tf_op jit(solution)/shard_map/stack | solution.py:226
  106.2 29.6 %pair_coherence.1 = bf16[2,128,64,128]{3,2,1,0:T(8,128)(2,1)} custom-call(s32[1]{0:T(128)} %bitcast.win_ref, bf16[4,128,768]{2,1,0:T(8,128)(2,1)} %pad_maximum_fusion.1.own_ref, bf16[4,2,128,768]{3,2,1,0:T(8,128)(2,1)} %pad_maximum_fusion.partner_ref), custom_call_target="tpu_custom_call" | custom-call | tf_op jit(solution)/shard_map/pair_coherence/pallas_call | solution.py:188
  (19 shorter events, 0.2 us)
Async XLA Ops:
  0.6 23.5 %copy-start = (bf16[1,128,768]{2,1,0:T(8,128)(2,1)S(1)}, bf16[1,128,768]{2,1,0:T(8,128)(2,1)}, u32[]{:S(2)}) copy-start(bf16[1,128,768]{2,1,0:T(8,128)(2,1)} %param.5) | copy-start | bytes 589828
  0.6 27.8 %copy-start.1 = (s32[2,8]{1,0:T(2,128)S(1)}, s32[2,8]{1,0:T(2,128)}, u32[]{:S(2)}) copy-start(s32[2,8]{1,0:T(2,128)} %param.6) | copy-start | bytes 196
  24.1 10.2 %collective-permute-start.3 = (bf16[4,128,768]{2,1,0:T(8,128)(2,1)S(1)}, bf16[4,128,768]{2,1,0:T(8,128)(2,1)S(1)}, u32[]{:S(2)}, u32[]{:S(2)}) collective-permute-start(bf16[4,128,768]{2,1,0:T(8,128)(2,1)S(1)} %all_gather.3), channel_id=1, source_target_pairs={{0,4},{4,0},{8,12},{12,8},{16,20},{20,16},{24,28},{28,24},{1,5},{5... | collective-permute-start | bytes 2359304 | tf_op jit(solution)/shard_map/ppermute | solution.py:217
  24.2 13.5 %collective-permute-start.2 = (bf16[128,768]{1,0:T(8,128)(2,1)S(1)}, bf16[128,768]{1,0:T(8,128)(2,1)S(1)}, u32[]{:S(2)}, u32[]{:S(2)}) collective-permute-start(bf16[128,768]{1,0:T(8,128)(2,1)S(1)} %fusion.8), channel_id=1, source_target_pairs={{0,3},{1,2},{2,1},{3,0},{4,7},{5,6},{6,5},{7,4},{8,11},{9,10},{10,... | collective-permute-start | bytes 589832 | tf_op jit(solution)/shard_map/ppermute | solution.py:212
  26.7 12.5 %collective-permute-start.1 = (bf16[128,768]{1,0:T(8,128)(2,1)S(1)}, bf16[128,768]{1,0:T(8,128)(2,1)S(1)}, u32[]{:S(2)}, u32[]{:S(2)}) collective-permute-start(bf16[128,768]{1,0:T(8,128)(2,1)S(1)} %fusion.8), channel_id=1, source_target_pairs={{0,2},{1,3},{2,0},{3,1},{4,6},{5,7},{6,4},{7,5},{8,10},{9,11},{10,... | collective-permute-start | bytes 589832 | tf_op jit(solution)/shard_map/ppermute | solution.py:212
  27.2 13.5 %collective-permute-start = (bf16[128,768]{1,0:T(8,128)(2,1)S(1)}, bf16[128,768]{1,0:T(8,128)(2,1)S(1)}, u32[]{:S(2)}, u32[]{:S(2)}) collective-permute-start(bf16[128,768]{1,0:T(8,128)(2,1)S(1)} %fusion.8), channel_id=1, source_target_pairs={{0,1},{1,0},{2,3},{3,2},{4,5},{5,4},{6,7},{7,6},{8,9},{9,8},{10,11... | collective-permute-start | bytes 589832 | tf_op jit(solution)/shard_map/ppermute | solution.py:212
  34.5 8.9 %collective-permute-start.9 = (bf16[128,768]{1,0:T(8,128)(2,1)S(1)}, bf16[128,768]{1,0:T(8,128)(2,1)S(1)}, u32[]{:S(2)}, u32[]{:S(2)}) collective-permute-start(bf16[128,768]{1,0:T(8,128)(2,1)S(1)} %bitcast.32), channel_id=1, source_target_pairs={{0,3},{1,2},{2,1},{3,0},{4,7},{5,6},{6,5},{7,4},{8,11},{9,10},{10,... | collective-permute-start | bytes 589832 | tf_op jit(solution)/shard_map/ppermute | solution.py:212
  37.1 67.8 %collective-permute-start.6 = (bf16[2,128,768]{2,1,0:T(8,128)(2,1)S(1)}, bf16[2,128,768]{2,1,0:T(8,128)(2,1)S(1)}, u32[]{:S(2)}, u32[]{:S(2)}) collective-permute-start(bf16[2,128,768]{2,1,0:T(8,128)(2,1)S(1)} %get-tuple-element.6), channel_id=1, source_target_pairs={{0,3},{1,2},{2,1},{3,0},{4,7},{5,6},{6,5},{7,4},{8,11},{9,10},{10,... | collective-permute-start | bytes 1179656 | tf_op jit(solution)/shard_map/ppermute | solution.py:212
  37.7 67.2 %collective-permute-start.5 = (bf16[2,128,768]{2,1,0:T(8,128)(2,1)S(1)}, bf16[2,128,768]{2,1,0:T(8,128)(2,1)S(1)}, u32[]{:S(2)}, u32[]{:S(2)}) collective-permute-start(bf16[2,128,768]{2,1,0:T(8,128)(2,1)S(1)} %get-tuple-element.6), channel_id=1, source_target_pairs={{0,2},{1,3},{2,0},{3,1},{4,6},{5,7},{6,4},{7,5},{8,10},{9,11},{10,... | collective-permute-start | bytes 1179656 | tf_op jit(solution)/shard_map/ppermute | solution.py:212
  39.2 65.7 %collective-permute-start.4 = (bf16[2,128,768]{2,1,0:T(8,128)(2,1)S(1)}, bf16[2,128,768]{2,1,0:T(8,128)(2,1)S(1)}, u32[]{:S(2)}, u32[]{:S(2)}) collective-permute-start(bf16[2,128,768]{2,1,0:T(8,128)(2,1)S(1)} %get-tuple-element.6), channel_id=1, source_target_pairs={{0,1},{1,0},{2,3},{3,2},{4,5},{5,4},{6,7},{7,6},{8,9},{9,8},{10,11... | collective-permute-start | bytes 1179656 | tf_op jit(solution)/shard_map/ppermute | solution.py:212
  40.7 22.4 %collective-permute-start.8 = (bf16[128,768]{1,0:T(8,128)(2,1)S(1)}, bf16[128,768]{1,0:T(8,128)(2,1)S(1)}, u32[]{:S(2)}, u32[]{:S(2)}) collective-permute-start(bf16[128,768]{1,0:T(8,128)(2,1)S(1)} %bitcast.33), channel_id=1, source_target_pairs={{0,2},{1,3},{2,0},{3,1},{4,6},{5,7},{6,4},{7,5},{8,10},{9,11},{10,... | collective-permute-start | bytes 589832 | tf_op jit(solution)/shard_map/ppermute | solution.py:212
  43.4 19.7 %collective-permute-start.7 = (bf16[128,768]{1,0:T(8,128)(2,1)S(1)}, bf16[128,768]{1,0:T(8,128)(2,1)S(1)}, u32[]{:S(2)}, u32[]{:S(2)}) collective-permute-start(bf16[128,768]{1,0:T(8,128)(2,1)S(1)} %bitcast.34), channel_id=1, source_target_pairs={{0,1},{1,0},{2,3},{3,2},{4,5},{5,4},{6,7},{7,6},{8,9},{9,8},{10,11... | collective-permute-start | bytes 589832 | tf_op jit(solution)/shard_map/ppermute | solution.py:212
  44.9 19.2 %copy-start.2 = (s32[1,128]{1,0:T(1,128)S(1)}, s32[1,128]{1,0:T(1,128)}, u32[]{:S(2)}) copy-start(s32[1,128]{1,0:T(1,128)} %param.8) | copy-start | bytes 1540
  44.9 19.9 %copy-start.3 = (s32[1,128]{1,0:T(1,128)S(1)}, s32[1,128]{1,0:T(1,128)}, u32[]{:S(2)}) copy-start(s32[1,128]{1,0:T(1,128)} %param.9) | copy-start | bytes 1540

commit v2 on v1

--- a/solution.py
+++ b/solution.py
@@ -17,14 +17,28 @@
 GROUP = 4
 VMEM_LIMIT = 60 << 20
 
+SMEM_SPEC = pl.BlockSpec(memory_space=pltpu.SMEM)
+VMEM_SPEC = pl.BlockSpec(memory_space=pltpu.VMEM)
+ROW_PAD = 8
+
 f32 = jnp.float32
 bf16 = jnp.bfloat16
 
 
+def whiten_kernel(traces_ref, out_ref):
+    samples = traces_ref[0].astype(f32)
+    energy_mean = jnp.mean(samples * samples, axis=-1, keepdims=True)
+    out_ref[...] = (samples * lax.rsqrt(energy_mean + EPS)).astype(bf16)
+
+
 def whiten(traces):
-    samples = traces.astype(f32)
-    energy_mean = jnp.mean(samples * samples, axis=-1, keepdims=True)
-    return (samples * lax.rsqrt(energy_mean + EPS)).astype(bf16)
+    return pl.pallas_call(
+        whiten_kernel,
+        out_shape=jax.ShapeDtypeStruct(traces.shape[1:], bf16),
+        in_specs=[VMEM_SPEC],
+        out_specs=VMEM_SPEC,
+        name="whiten",
+    )(traces)
 
 
 def shift_right(block, count):
@@ -35,8 +49,10 @@
     return jnp.where(lane < count, 0.0, moved).astype(bf16)
 
 
-def coda_kernel(win_ref, aux_ref, own_ref, start_ref, end_ref, out_ref, shifted, own_t, coda, coda_t, acc, rows):
-    windows, blk, length = own_ref.shape
+def coda_kernel(windows, win_ref, start_ref, end_ref, *refs):
+    aux_ref, own_ref = refs[:windows], refs[windows : 2 * windows]
+    out_ref, shifted, own_t, coda, coda_t, acc, rows = refs[2 * windows :]
+    blk, length = own_ref[0].shape
     used = length - CODA_LO
     share = out_ref.shape[1]
     steps = share // 2
@@ -46,7 +62,7 @@
     win = win_ref[0]
 
     for w in range(windows):
-        own_t[w, :length, :] = own_ref[w].T
+        own_t[w, :length, :] = own_ref[w][...].T
         own_t[w, length:, :] = jnp.zeros((own_t.shape[1] - length, blk), bf16)
         samples = aux_ref[w][:, :used].astype(f32)
         for b in range(STEP):
@@ -114,23 +130,24 @@
     for i in range(steps):
         for b in range(2):
             lag = 2 * (steps - 1 - i) + b
-            rows[pl.ds(lag, blk, stride=share), :] = (
+            rows[pl.ds(lag, blk, stride=share + ROW_PAD), :] = (
                 acc[i * blk : (i + 1) * blk, b * blk : (b + 1) * blk] * scale_three
             )
-    out_ref[...] = rows[...].reshape(blk, share, blk).astype(bf16)
-
-
-def pair_kernel(win_ref, own_ref, partner_ref, out_ref, shifted, partner_t, rows):
-    windows, blk, length = own_ref.shape
-    rounds = partner_ref.shape[1]
+    out_ref[...] = rows[...].reshape(blk, share + ROW_PAD, blk)[:, :share].astype(bf16)
+
+
+def pair_kernel(windows, win_ref, *refs):
+    own_ref, partner_ref = refs[:windows], refs[windows : 2 * windows]
+    out_ref, shifted, partner_t, rows = refs[2 * windows :]
+    rounds, blk, length = partner_ref[0].shape
     share = out_ref.shape[2]
     scale_two = 1.0 / math.sqrt(windows * length)
     win = win_ref[0]
     for w in range(windows):
         for r in range(rounds):
-            partner_t[w, :length, r * blk : (r + 1) * blk] = partner_ref[w, r].T
+            partner_t[w, :length, r * blk : (r + 1) * blk] = partner_ref[w][r].T
         partner_t[w, length:, :] = jnp.zeros((partner_t.shape[1] - length, rounds * blk), bf16)
-        samples = own_ref[w].astype(f32)
+        samples = own_ref[w][...].astype(f32)
         for b in range(STEP):
             shifted[b * blk : (b + 1) * blk, w * length : (w + 1) * length] = shift_right(samples, b)
 
@@ -146,28 +163,25 @@
         for b in range(half):
             lag = a * STEP + b_half * half + b
             for r in range(rounds):
-                rows[r, pl.ds(lag, blk, stride=share), :] = (
+                rows[r, pl.ds(lag, blk, stride=share + ROW_PAD), :] = (
                     result[b * blk : (b + 1) * blk, r * blk : (r + 1) * blk] * scale_two
                 )
         return 0
 
     lax.fori_loop(0, 2 * (share // STEP), pair, 0)
     for r in range(rounds):
-        out_ref[r] = rows[r].reshape(blk, share, blk).astype(bf16)
-
-
-SMEM_SPEC = pl.BlockSpec(memory_space=pltpu.SMEM)
-VMEM_SPEC = pl.BlockSpec(memory_space=pltpu.VMEM)
+        out_ref[r] = rows[r].reshape(blk, share + ROW_PAD, blk)[:, :share].astype(bf16)
 
 
 def coda_coherence(win, aux, own, start, end, share):
-    windows, blk, length = own.shape
+    windows = len(own)
+    blk, length = own[0].shape
     used = length - CODA_LO
     steps = share // 2
     return pl.pallas_call(
-        coda_kernel,
+        functools.partial(coda_kernel, windows),
         out_shape=jax.ShapeDtypeStruct((blk, share, blk), bf16),
-        in_specs=[SMEM_SPEC] + [VMEM_SPEC] * 4,
+        in_specs=[SMEM_SPEC] + [VMEM_SPEC] * (2 + 2 * windows),
         out_specs=VMEM_SPEC,
         scratch_shapes=[
             pltpu.VMEM((STEP * blk, windows * used), bf16),
@@ -175,29 +189,29 @@
             pltpu.VMEM(((CODA + 1) * blk, blk), bf16),
             pltpu.VMEM(((CODA // 2 + steps - 1) * blk, 2 * blk), bf16),
             pltpu.VMEM((steps * blk, 2 * blk), f32),
-            pltpu.VMEM((share * blk, blk), f32),
+            pltpu.VMEM(((share + ROW_PAD) * blk, blk), f32),
         ],
         compiler_params=pltpu.CompilerParams(vmem_limit_bytes=VMEM_LIMIT),
         name="coda_coherence",
-    )(win, aux, own, start, end)
+    )(win, start, end, *aux, *own)
 
 
 def pair_coherence(win, own, partner, share):
-    windows, blk, length = own.shape
-    rounds = partner.shape[1]
+    windows = len(own)
+    rounds, blk, length = partner[0].shape
     return pl.pallas_call(
-        pair_kernel,
+        functools.partial(pair_kernel, windows),
         out_shape=jax.ShapeDtypeStruct((rounds, blk, share, blk), bf16),
-        in_specs=[SMEM_SPEC] + [VMEM_SPEC] * 2,
+        in_specs=[SMEM_SPEC] + [VMEM_SPEC] * (2 * windows),
         out_specs=VMEM_SPEC,
         scratch_shapes=[
             pltpu.VMEM((STEP * blk, windows * length), bf16),
             pltpu.VMEM((windows, length + LAGS, rounds * blk), bf16),
-            pltpu.VMEM((rounds, blk * share, blk), f32),
+            pltpu.VMEM((rounds, blk * (share + ROW_PAD), blk), f32),
         ],
         compiler_params=pltpu.CompilerParams(vmem_limit_bytes=VMEM_LIMIT),
         name="pair_coherence",
-    )(win, own, partner)
+    )(win, *own, *partner)
 
 
 def per_device(traces, pairing, aux_owners, coda_start, coda_end):
@@ -206,24 +220,41 @@
     win_index = lax.axis_index("win")
     chan_index = lax.axis_index("chan")
     blk = traces.shape[1]
-    white = whiten(traces)[0]
+    rounds = pairing.shape[0]
+    white = whiten(traces)
 
     def exchange(block, k):
         return lax.ppermute(block, "win", [(i, i ^ k) for i in range(win_size)])
 
-    own_all = jnp.stack([white] + [exchange(white, k) for k in range(1, win_size)])
-    same_core = [list(range(core, chan_size, 2)) for core in range(2)]
-    column = lax.all_gather(white, "chan", axis=0, axis_index_groups=same_core)
-    other = lax.ppermute(column, "chan", [(i, i ^ 1) for i in range(chan_size)])
-    both = jnp.stack([column, other])
-
-    def pick(block):
-        return both[(block % 2) ^ (chan_index % 2), block // 2]
-
-    aux = pick(aux_owners[0])
-    partners = jnp.stack([pick(pairing[r, chan_index]) for r in range(pairing.shape[0])])
-    aux_all = jnp.stack([aux] + [exchange(aux, k) for k in range(1, win_size)])
-    partner_all = jnp.stack([partners] + [exchange(partners, k) for k in range(1, win_size)])
+    own_all = [white] + [exchange(white, k) for k in range(1, win_size)]
+    column = [white] + [
+        lax.ppermute(white, "chan", [(i, (i + 2 * k) % chan_size) for i in range(chan_size)])
+        for k in range(1, chan_size // 2)
+    ]
+
+    own_all, column = lax.optimization_barrier((own_all, column))
+
+    def look_up(block):
+        steps = jnp.mod(chan_index - block, chan_size) // 2
+        found = column[0]
+        for k in range(1, chan_size // 2):
+            found = jnp.where(steps == k, column[k], found)
+        return found
+
+    def wanted(chan):
+        return [aux_owners[0]] + [pairing[r, chan] for r in range(rounds)]
+
+    asked = jnp.stack([look_up(block) for block in wanted(chan_index ^ 1)])
+    answered = lax.ppermute(asked, "chan", [(i, i ^ 1) for i in range(chan_size)])
+    blocks = [
+        jnp.where((block - chan_index) % 2 == 0, look_up(block), answered[n])
+        for n, block in enumerate(wanted(chan_index))
+    ]
+    aux = blocks[0]
+    partners = jnp.stack(blocks[1:])
+    aux_all = [aux] + [exchange(aux, k) for k in range(1, win_size)]
+    partners, *aux_all = lax.optimization_barrier((partners, *aux_all))
+    partner_all = [partners] + [exchange(partners, k) for k in range(1, win_size)]
     win = win_index.reshape(1).astype(jnp.int32)
     start = jnp.broadcast_to(coda_start[0][:, None], (blk, blk))
     end = jnp.broadcast_to(coda_end[0][:, None], (blk, blk))

time: 136 us -> 111 us (0.82)
  the two profiles are of different devices: /device:TPU:0 before, /device:TPU:8 now
where the time goes in v2:
time: 111 us
  Pallas kernels  62.4 us (56%)
  waiting for transfers between devices  22.5 us (20%)
  starting transfers between devices  13.4 us (12%)
  between operations  5.62 us (5%)
  local copies, waits for them, and re-layouts  4.56 us (4%)
  other arithmetic  2.12 us (2%)
    pallas_call x1, Pallas kernels, coda_coherence(): pl.pallas_call(functools.partial(coda_kernel, windows), out_shape=jax.Sha...  37.8 us
    pallas_call x1, Pallas kernels, pair_coherence(): pl.pallas_call(functools.partial(pair_kernel, windows), out_shape=jax.Sha...  22.8 us
    ppermute x9, waiting for transfers between devices, exchange(): return lax.ppermute(block, 'win', [(i, i ^ k) for i in range(win_size)])  11.7 us
    ppermute x3, waiting for transfers between devices, per_device(): lax.ppermute(white, 'chan', [(i, (i + 2 * k) % chan_size) for i in range(...  10.7 us
    ppermute x9, starting transfers between devices, exchange(): return lax.ppermute(block, 'win', [(i, i ^ k) for i in range(win_size)])  10.6 us
    ppermute x3, starting transfers between devices, per_device(): lax.ppermute(white, 'chan', [(i, (i + 2 * k) % chan_size) for i in range(...  2.7 us
  transfers between devices with their start and end apart: 13, of which 7 were waited for; matrix products, arithmetic and copies ran while one was open for 3% of the time, Pallas kernels for 34%

profile of v2, /device:TPU:8, one launch (start us, length us, event | category | flops | bytes accessed | tf_op | source)
XLA Modules:
  0.0 110.5 jit_solution(8463591465795533758)
XLA Ops:
  0.6 1.8 %whiten.1.refs_0_.refs_4_ = bf16[128,768]{1,0:T(8,128)(2,1)} custom-call(bf16[1,128,768]{2,1,0:T(8,128)(2,1)} %traces_ref.1), custom_call_target="tpu_custom_call" | custom-call | tf_op jit(solution)/shard_map/whiten/pallas_call | solution.py:35
  2.4 1.5 %collective-permute-start = (bf16[128,768]{1,0:T(8,128)(2,1)}, bf16[128,768]{1,0:T(8,128)(2,1)S(1)}, u32[]{:S(2)}, u32[]{:S(2)}) collective-permute-start(bf16[128,768]{1,0:T(8,128)(2,1)} %whiten.1.refs_0_.refs_4_), channel_id=1, source_target_pairs={{0,1},{1,0},{2,3},{3,2},{4,5},{5,4},{6,7},{7,6},{8,9},{9,8},{10,11... | collective-permute-start | bytes 589832 | tf_op jit(solution)/shard_map/ppermute | solution.py:227
  3.9 1.5 %collective-permute-start.1 = (bf16[128,768]{1,0:T(8,128)(2,1)}, bf16[128,768]{1,0:T(8,128)(2,1)S(1)}, u32[]{:S(2)}, u32[]{:S(2)}) collective-permute-start(bf16[128,768]{1,0:T(8,128)(2,1)} %whiten.1.refs_0_.refs_4_), channel_id=1, source_target_pairs={{0,2},{1,3},{2,0},{3,1},{4,6},{5,7},{6,4},{7,5},{8,10},{9,11},{10,... | collective-permute-start | bytes 589832 | tf_op jit(solution)/shard_map/ppermute | solution.py:227
  5.9 1.6 %collective-permute-start.3 = (bf16[128,768]{1,0:T(8,128)(2,1)}, bf16[128,768]{1,0:T(8,128)(2,1)S(1)}, u32[]{:S(2)}, u32[]{:S(2)}) collective-permute-start(bf16[128,768]{1,0:T(8,128)(2,1)} %whiten.1.refs_0_.refs_4_), channel_id=1, source_target_pairs={{0,8},{4,12},{8,16},{12,20},{16,24},{20,28},{24,0},{28,4},{1,9},{5... | collective-permute-start | bytes 589832 | tf_op jit(solution)/shard_map/ppermute | solution.py:231
  7.5 1.0 collective-permute-start.4
  8.5 1.9 %collective-permute-done.refs_1_.refs_5_ = bf16[128,768]{1,0:T(8,128)(2,1)S(1)} collective-permute-done((bf16[128,768]{1,0:T(8,128)(2,1)}, bf16[128,768]{1,0:T(8,128)(2,1)S(1)}, u32[]{:S(2)}, u32[]{:S(2)}) %collective-permute-start) | collective-permute-done | bytes 196640 | tf_op jit(solution)/shard_map/ppermute | solution.py:227
  11.2 1.5 %constant_dynamic-slice_fusion.3 = (s32[1,1]{1,0:T(1,128)}, s32[1,1]{1,0:T(1,128)}, s32[1,1]{1,0:T(1,128)}, s32[1,1]{1,0:T(1,128)}) fusion(s32[2,8]{1,0:T(2,128)} %param.6, s32[]{:T(128)S(6)} %select_n.178, s32[]{:T(128)S(6)} %select_n.197), kind=kLoop, calls=%fused_computation.16 | loop fusion | bytes 40 | tf_op jit(solution)/shard_map/dynamic_slice | solution.py:245
  14.7 6.9 %collective-permute-done.3 = bf16[128,768]{1,0:T(8,128)(2,1)S(1)} collective-permute-done((bf16[128,768]{1,0:T(8,128)(2,1)}, bf16[128,768]{1,0:T(8,128)(2,1)S(1)}, u32[]{:S(2)}, u32[]{:S(2)}) %collective-permute-start.3) | collective-permute-done | bytes 196640 | tf_op jit(solution)/shard_map/ppermute | solution.py:231
  21.6 2.2 %collective-permute-done.4 = bf16[128,768]{1,0:T(8,128)(2,1)S(1)} collective-permute-done((bf16[128,768]{1,0:T(8,128)(2,1)}, bf16[128,768]{1,0:T(8,128)(2,1)S(1)}, u32[]{:S(2)}, u32[]{:S(2)}) %collective-permute-start.4) | collective-permute-done | bytes 196640 | tf_op jit(solution)/shard_map/ppermute | solution.py:231
  23.8 1.7 %collective-permute-done.5 = bf16[128,768]{1,0:T(8,128)(2,1)S(1)} collective-permute-done((bf16[128,768]{1,0:T(8,128)(2,1)}, bf16[128,768]{1,0:T(8,128)(2,1)S(1)}, u32[]{:S(2)}, u32[]{:S(2)}) %collective-permute-start.5) | collective-permute-done | bytes 196640 | tf_op jit(solution)/shard_map/ppermute | solution.py:231
  25.4 1.0 select_select_fusion
  29.4 1.0 fusion.4
  30.4 1.6 %collective-permute-start.7 = (bf16[128,768]{1,0:T(8,128)(2,1)S(1)}, bf16[128,768]{1,0:T(8,128)(2,1)S(1)}, u32[]{:S(2)}, u32[]{:S(2)}) collective-permute-start(bf16[128,768]{1,0:T(8,128)(2,1)S(1)} %get-tuple-element.24.refs_0_), channel_id=1, source_target_pairs={{0,1},{1,0},{2,3},{3,2},{4,5},{5,4},{6,7},{7,6},{8,9},{9,8},{10,11... | collective-permute-start | bytes 589832 | tf_op jit(solution)/shard_map/ppermute | solution.py:227
  32.0 1.5 %collective-permute-start.8 = (bf16[128,768]{1,0:T(8,128)(2,1)S(1)}, bf16[128,768]{1,0:T(8,128)(2,1)S(1)}, u32[]{:S(2)}, u32[]{:S(2)}) collective-permute-start(bf16[128,768]{1,0:T(8,128)(2,1)S(1)} %get-tuple-element.24.refs_0_), channel_id=1, source_target_pairs={{0,2},{1,3},{2,0},{3,1},{4,6},{5,7},{6,4},{7,5},{8,10},{9,11},{10,... | collective-permute-start | bytes 589832 | tf_op jit(solution)/shard_map/ppermute | solution.py:227
  34.0 4.2 %collective-permute-done.7.refs_1_ = bf16[128,768]{1,0:T(8,128)(2,1)S(1)} collective-permute-done((bf16[128,768]{1,0:T(8,128)(2,1)S(1)}, bf16[128,768]{1,0:T(8,128)(2,1)S(1)}, u32[]{:S(2)}, u32[]{:S(2)}) %collective-permute-start.7) | collective-permute-done | bytes 196640 | tf_op jit(solution)/shard_map/ppermute | solution.py:227
  38.2 5.0 %collective-permute-done.8.refs_2_ = bf16[128,768]{1,0:T(8,128)(2,1)S(1)} collective-permute-done((bf16[128,768]{1,0:T(8,128)(2,1)S(1)}, bf16[128,768]{1,0:T(8,128)(2,1)S(1)}, u32[]{:S(2)}, u32[]{:S(2)}) %collective-permute-start.8) | collective-permute-done | bytes 196640 | tf_op jit(solution)/shard_map/ppermute | solution.py:227
  43.2 1.2 %collective-permute-start.10 = (bf16[2,128,768]{2,1,0:T(8,128)(2,1)S(1)}, bf16[2,128,768]{2,1,0:T(8,128)(2,1)S(1)}, u32[]{:S(2)}, u32[]{:S(2)}) collective-permute-start(bf16[2,128,768]{2,1,0:T(8,128)(2,1)S(1)} %pad_maximum_fusion.1.refs_4_), channel_id=1, source_target_pairs={{0,1},{1,0},{2,3},{3,2},{4,5},{5,4},{6,7},{7,6},{8,9},{9,8},{10,11... | collective-permute-start | bytes 1179656 | tf_op jit(solution)/shard_map/ppermute | solution.py:227
  44.5 0.9 collective-permute-start.11
  45.3 1.4 %collective-permute-start.12 = (bf16[2,128,768]{2,1,0:T(8,128)(2,1)S(1)}, bf16[2,128,768]{2,1,0:T(8,128)(2,1)S(1)}, u32[]{:S(2)}, u32[]{:S(2)}) collective-permute-start(bf16[2,128,768]{2,1,0:T(8,128)(2,1)S(1)} %pad_maximum_fusion.1.refs_4_), channel_id=1, source_target_pairs={{0,3},{1,2},{2,1},{3,0},{4,7},{5,6},{6,5},{7,4},{8,11},{9,10},{10,... | collective-permute-start | bytes 1179656 | tf_op jit(solution)/shard_map/ppermute | solution.py:227
  47.5 0.7 broadcast_in_dim.17.end_ref
  48.2 37.8 %coda_coherence.1 = bf16[128,32,128]{2,1,0:T(8,128)(2,1)} custom-call(s32[1]{0:T(128)} %bitcast.win_ref, s32[128,128]{1,0:T(8,128)} %broadcast_in_dim.15.start_ref, s32[128,128]{1,0:T(8,128)} %broadcast_in_dim.17.end_ref, bf16[128,768]{1,0:T(8,128)(2,1)} %copy-done.1, bf16[128,768]{1,0:T(8,128)(2,1)} %copy-done.8, bf16[128,768]{1,0:T(8,128)(2,1)} %copy-done.9, ...), custom_call_target="tpu_custom_call" | custom-call | tf_op jit(solution)/shard_map/coda_coherence/pallas_call | solution.py:181
  86.1 0.7 copy-done.5
  87.0 0.7 copy-done.7
  87.7 22.8 %pair_coherence.1 = bf16[2,128,64,128]{3,2,1,0:T(8,128)(2,1)} custom-call(s32[1]{0:T(128)} %bitcast.win_ref, bf16[128,768]{1,0:T(8,128)(2,1)} %whiten.1.refs_0_.refs_4_, bf16[128,768]{1,0:T(8,128)(2,1)} %copy-done.2, bf16[128,768]{1,0:T(8,128)(2,1)} %copy-done.3, bf16[128,768]{1,0:T(8,128)(2,1)} %copy-done.4, bf16[2,128,768]{2,1,0:T(8,128)(2,1)} %copy-done, ...), custom_call_target="tpu_custom_call" | custom-call | tf_op jit(solution)/shard_map/pair_coherence/pallas_call | solution.py:202
  (38 shorter events, 2.8 us)
Async XLA Ops:
  0.6 46.2 %copy-start.11 = (s32[1,128]{1,0:T(1,128)S(1)}, s32[1,128]{1,0:T(1,128)}, u32[]{:S(2)}) copy-start(s32[1,128]{1,0:T(1,128)} %param.8) | copy-start | bytes 1540
  0.6 46.9 %copy-start.12 = (s32[1,128]{1,0:T(1,128)S(1)}, s32[1,128]{1,0:T(1,128)}, u32[]{:S(2)}) copy-start(s32[1,128]{1,0:T(1,128)} %param.9) | copy-start | bytes 1540
  2.4 8.0 %collective-permute-start = (bf16[128,768]{1,0:T(8,128)(2,1)}, bf16[128,768]{1,0:T(8,128)(2,1)S(1)}, u32[]{:S(2)}, u32[]{:S(2)}) collective-permute-start(bf16[128,768]{1,0:T(8,128)(2,1)} %whiten.1.refs_0_.refs_4_), channel_id=1, source_target_pairs={{0,1},{1,0},{2,3},{3,2},{4,5},{5,4},{6,7},{7,6},{8,9},{9,8},{10,11... | collective-permute-start | bytes 589832 | tf_op jit(solution)/shard_map/ppermute | solution.py:227
  3.9 10.8 %collective-permute-start.1 = (bf16[128,768]{1,0:T(8,128)(2,1)}, bf16[128,768]{1,0:T(8,128)(2,1)S(1)}, u32[]{:S(2)}, u32[]{:S(2)}) collective-permute-start(bf16[128,768]{1,0:T(8,128)(2,1)} %whiten.1.refs_0_.refs_4_), channel_id=1, source_target_pairs={{0,2},{1,3},{2,0},{3,1},{4,6},{5,7},{6,4},{7,5},{8,10},{9,11},{10,... | collective-permute-start | bytes 589832 | tf_op jit(solution)/shard_map/ppermute | solution.py:227
  5.4 9.3 %collective-permute-start.2 = (bf16[128,768]{1,0:T(8,128)(2,1)}, bf16[128,768]{1,0:T(8,128)(2,1)S(1)}, u32[]{:S(2)}, u32[]{:S(2)}) collective-permute-start(bf16[128,768]{1,0:T(8,128)(2,1)} %whiten.1.refs_0_.refs_4_), channel_id=1, source_target_pairs={{0,3},{1,2},{2,1},{3,0},{4,7},{5,6},{6,5},{7,4},{8,11},{9,10},{10,... | collective-permute-start | bytes 589832 | tf_op jit(solution)/shard_map/ppermute | solution.py:227
  5.9 15.7 %collective-permute-start.3 = (bf16[128,768]{1,0:T(8,128)(2,1)}, bf16[128,768]{1,0:T(8,128)(2,1)S(1)}, u32[]{:S(2)}, u32[]{:S(2)}) collective-permute-start(bf16[128,768]{1,0:T(8,128)(2,1)} %whiten.1.refs_0_.refs_4_), channel_id=1, source_target_pairs={{0,8},{4,12},{8,16},{12,20},{16,24},{20,28},{24,0},{28,4},{1,9},{5... | collective-permute-start | bytes 589832 | tf_op jit(solution)/shard_map/ppermute | solution.py:231
  7.5 16.3 %collective-permute-start.4 = (bf16[128,768]{1,0:T(8,128)(2,1)}, bf16[128,768]{1,0:T(8,128)(2,1)S(1)}, u32[]{:S(2)}, u32[]{:S(2)}) collective-permute-start(bf16[128,768]{1,0:T(8,128)(2,1)} %whiten.1.refs_0_.refs_4_), channel_id=1, source_target_pairs={{0,16},{4,20},{8,24},{12,28},{16,0},{20,4},{24,8},{28,12},{1,17},{... | collective-permute-start | bytes 589832 | tf_op jit(solution)/shard_map/ppermute | solution.py:231
  10.4 37.8 %copy-start.2 = (bf16[128,768]{1,0:T(8,128)(2,1)}, bf16[128,768]{1,0:T(8,128)(2,1)S(1)}, u32[]{:S(2)}) copy-start(bf16[128,768]{1,0:T(8,128)(2,1)S(1)} %collective-permute-done.refs_1_.refs_5_) | copy-start | bytes 589828
  10.4 15.0 %collective-permute-start.5 = (bf16[128,768]{1,0:T(8,128)(2,1)}, bf16[128,768]{1,0:T(8,128)(2,1)S(1)}, u32[]{:S(2)}, u32[]{:S(2)}) collective-permute-start(bf16[128,768]{1,0:T(8,128)(2,1)} %whiten.1.refs_0_.refs_4_), channel_id=1, source_target_pairs={{0,24},{4,28},{8,0},{12,4},{16,8},{20,12},{24,16},{28,20},{1,25},{... | collective-permute-start | bytes 589832 | tf_op jit(solution)/shard_map/ppermute | solution.py:231
  14.7 33.5 %copy-start.3 = (bf16[128,768]{1,0:T(8,128)(2,1)}, bf16[128,768]{1,0:T(8,128)(2,1)S(1)}, u32[]{:S(2)}) copy-start(bf16[128,768]{1,0:T(8,128)(2,1)S(1)} %collective-permute-done.1.refs_2_.refs_6_) | copy-start | bytes 589828
  14.7 33.5 %copy-start.4 = (bf16[128,768]{1,0:T(8,128)(2,1)}, bf16[128,768]{1,0:T(8,128)(2,1)S(1)}, u32[]{:S(2)}) copy-start(bf16[128,768]{1,0:T(8,128)(2,1)S(1)} %collective-permute-done.2.refs_3_.refs_7_) | copy-start | bytes 589828
  26.5 2.9 %collective-permute-start.6 = (bf16[3,128,768]{2,1,0:T(8,128)(2,1)S(1)}, bf16[3,128,768]{2,1,0:T(8,128)(2,1)S(1)}, u32[]{:S(2)}, u32[]{:S(2)}) collective-permute-start(bf16[3,128,768]{2,1,0:T(8,128)(2,1)S(1)} %pad_maximum_fusion), channel_id=1, source_target_pairs={{0,4},{4,0},{8,12},{12,8},{16,20},{20,16},{24,28},{28,24},{1,5},{5... | collective-permute-start | bytes 1769480 | tf_op jit(solution)/shard_map/ppermute | solution.py:248
  30.4 17.8 %copy-start.1 = (bf16[128,768]{1,0:T(8,128)(2,1)}, bf16[128,768]{1,0:T(8,128)(2,1)S(1)}, u32[]{:S(2)}) copy-start(bf16[128,768]{1,0:T(8,128)(2,1)S(1)} %get-tuple-element.24.refs_0_) | copy-start | bytes 589828
  30.4 7.8 %collective-permute-start.7 = (bf16[128,768]{1,0:T(8,128)(2,1)S(1)}, bf16[128,768]{1,0:T(8,128)(2,1)S(1)}, u32[]{:S(2)}, u32[]{:S(2)}) collective-permute-start(bf16[128,768]{1,0:T(8,128)(2,1)S(1)} %get-tuple-element.24.refs_0_), channel_id=1, source_target_pairs={{0,1},{1,0},{2,3},{3,2},{4,5},{5,4},{6,7},{7,6},{8,9},{9,8},{10,11... | collective-permute-start | bytes 589832 | tf_op jit(solution)/shard_map/ppermute | solution.py:227
  32.0 11.2 %collective-permute-start.8 = (bf16[128,768]{1,0:T(8,128)(2,1)S(1)}, bf16[128,768]{1,0:T(8,128)(2,1)S(1)}, u32[]{:S(2)}, u32[]{:S(2)}) collective-permute-start(bf16[128,768]{1,0:T(8,128)(2,1)S(1)} %get-tuple-element.24.refs_0_), channel_id=1, source_target_pairs={{0,2},{1,3},{2,0},{3,1},{4,6},{5,7},{6,4},{7,5},{8,10},{9,11},{10,... | collective-permute-start | bytes 589832 | tf_op jit(solution)/shard_map/ppermute | solution.py:227
  33.5 9.7 %collective-permute-start.9 = (bf16[128,768]{1,0:T(8,128)(2,1)S(1)}, bf16[128,768]{1,0:T(8,128)(2,1)S(1)}, u32[]{:S(2)}, u32[]{:S(2)}) collective-permute-start(bf16[128,768]{1,0:T(8,128)(2,1)S(1)} %get-tuple-element.24.refs_0_), channel_id=1, source_target_pairs={{0,3},{1,2},{2,1},{3,0},{4,7},{5,6},{6,5},{7,4},{8,11},{9,10},{10,... | collective-permute-start | bytes 589832 | tf_op jit(solution)/shard_map/ppermute | solution.py:227
  34.0 52.1 %copy-start = (bf16[2,128,768]{2,1,0:T(8,128)(2,1)}, bf16[2,128,768]{2,1,0:T(8,128)(2,1)S(1)}, u32[]{:S(2)}) copy-start(bf16[2,128,768]{2,1,0:T(8,128)(2,1)S(1)} %pad_maximum_fusion.1.refs_4_) | copy-start | bytes 1179652
  38.2 10.0 %copy-start.8 = (bf16[128,768]{1,0:T(8,128)(2,1)}, bf16[128,768]{1,0:T(8,128)(2,1)S(1)}, u32[]{:S(2)}) copy-start(bf16[128,768]{1,0:T(8,128)(2,1)S(1)} %collective-permute-done.7.refs_1_) | copy-start | bytes 589828
  43.2 5.0 %copy-start.9 = (bf16[128,768]{1,0:T(8,128)(2,1)}, bf16[128,768]{1,0:T(8,128)(2,1)S(1)}, u32[]{:S(2)}) copy-start(bf16[128,768]{1,0:T(8,128)(2,1)S(1)} %collective-permute-done.8.refs_2_) | copy-start | bytes 589828
  43.2 5.0 %copy-start.10 = (bf16[128,768]{1,0:T(8,128)(2,1)}, bf16[128,768]{1,0:T(8,128)(2,1)S(1)}, u32[]{:S(2)}) copy-start(bf16[128,768]{1,0:T(8,128)(2,1)S(1)} %collective-permute-done.9.refs_3_) | copy-start | bytes 589828
  43.2 42.9 %collective-permute-start.10 = (bf16[2,128,768]{2,1,0:T(8,128)(2,1)S(1)}, bf16[2,128,768]{2,1,0:T(8,128)(2,1)S(1)}, u32[]{:S(2)}, u32[]{:S(2)}) collective-permute-start(bf16[2,128,768]{2,1,0:T(8,128)(2,1)S(1)} %pad_maximum_fusion.1.refs_4_), channel_id=1, source_target_pairs={{0,1},{1,0},{2,3},{3,2},{4,5},{5,4},{6,7},{7,6},{8,9},{9,8},{10,11... | collective-permute-start | bytes 1179656 | tf_op jit(solution)/shard_map/ppermute | solution.py:227
  44.5 41.6 %collective-permute-start.11 = (bf16[2,128,768]{2,1,0:T(8,128)(2,1)S(1)}, bf16[2,128,768]{2,1,0:T(8,128)(2,1)S(1)}, u32[]{:S(2)}, u32[]{:S(2)}) collective-permute-start(bf16[2,128,768]{2,1,0:T(8,128)(2,1)S(1)} %pad_maximum_fusion.1.refs_4_), channel_id=1, source_target_pairs={{0,2},{1,3},{2,0},{3,1},{4,6},{5,7},{6,4},{7,5},{8,10},{9,11},{10,... | collective-permute-start | bytes 1179656 | tf_op jit(solution)/shard_map/ppermute | solution.py:227
  45.3 40.8 %collective-permute-start.12 = (bf16[2,128,768]{2,1,0:T(8,128)(2,1)S(1)}, bf16[2,128,768]{2,1,0:T(8,128)(2,1)S(1)}, u32[]{:S(2)}, u32[]{:S(2)}) collective-permute-start(bf16[2,128,768]{2,1,0:T(8,128)(2,1)S(1)} %pad_maximum_fusion.1.refs_4_), channel_id=1, source_target_pairs={{0,3},{1,2},{2,1},{3,0},{4,7},{5,6},{6,5},{7,4},{8,11},{9,10},{10,... | collective-permute-start | bytes 1179656 | tf_op jit(solution)/shard_map/ppermute | solution.py:227
  86.1 0.9 copy-start.6
  (2 other events, 1.5 us)

commit v3 on v2

v3 whole, which is shorter than its diff:
```python
import functools
import math

import jax
import jax.numpy as jnp
from jax import lax
from jax.experimental import pallas as pl
from jax.experimental.pallas import tpu as pltpu
from jax.sharding import PartitionSpec as P

LAGS = 256
CODA = 128
CODA_LO = 128
LAGS3 = 128
EPS = 1e-05
STEP = 16
GROUP = 4

SMEM_SPEC = pl.BlockSpec(memory_space=pltpu.SMEM)
VMEM_SPEC = pl.BlockSpec(memory_space=pltpu.VMEM)
ROW_PAD = 8

f32 = jnp.float32
bf16 = jnp.bfloat16


def whiten_kernel(traces_ref, out_ref):
    samples = traces_ref[0].astype(f32)
    energy_mean = jnp.mean(samples * samples, axis=-1, keepdims=True)
    out_ref[...] = (samples * lax.rsqrt(energy_mean + EPS)).astype(bf16)


def whiten(traces):
    return pl.pallas_call(
        whiten_kernel,
        out_shape=jax.ShapeDtypeStruct(traces.shape[1:], bf16),
        in_specs=[VMEM_SPEC],
        out_specs=VMEM_SPEC,
        name="whiten",
    )(traces)


def shift_right(block, count):
    if count == 0:
        return block.astype(bf16)
    moved = pltpu.roll(block, count, 1)
    lane = lax.broadcasted_iota(jnp.int32, block.shape, 1)
    return jnp.where(lane < count, 0.0, moved).astype(bf16)


def pick_kernel(count, which_ref, *refs):
    column, out_refs = refs[:count], refs[count:]
    slots = [out_refs[0], out_refs[1]]
    for out_ref in out_refs[2:]:
        slots += [out_ref.at[r] for r in range(out_ref.shape[0])]
    for n, slot in enumerate(slots):
        for k in range(count):

            @pl.when(which_ref[n] == k)
            def _():
                slot[...] = column[k][...]


def pick(which, column, rounds):
    block = column[0].shape
    shapes = [block, block, (rounds,) + block, (rounds,) + block]
    return pl.pallas_call(
        functools.partial(pick_kernel, len(column)),
        out_shape=[jax.ShapeDtypeStruct(shape, bf16) for shape in shapes],
        in_specs=[SMEM_SPEC] + [VMEM_SPEC] * len(column),
        out_specs=[VMEM_SPEC] * 4,
        compiler_params=pltpu.CompilerParams(vmem_limit_bytes=2 << 20),
        name="pick",
    )(which, *column)


def merge_kernel(crossed_ref, held_ref, got_ref, out_ref):
    for r in range(held_ref.shape[0]):

        @pl.when(crossed_ref[r] == 0)
        def _():
            out_ref[r] = held_ref[r]

        @pl.when(crossed_ref[r] != 0)
        def _():
            out_ref[r] = got_ref[r]


def merge(crossed, held, got):
    return pl.pallas_call(
        merge_kernel,
        out_shape=jax.ShapeDtypeStruct(held.shape, bf16),
        in_specs=[SMEM_SPEC, VMEM_SPEC, VMEM_SPEC],
        out_specs=VMEM_SPEC,
        compiler_params=pltpu.CompilerParams(vmem_limit_bytes=2 << 20),
        name="merge",
    )(crossed, held, got)


def shift_kernel(block_ref, out_ref):
    blk, length = block_ref.shape
    lane = lax.broadcasted_iota(jnp.int32, (STEP, length), 1)
    row = lax.broadcasted_iota(jnp.int32, (STEP, length), 0)
    for i in range(blk):
        samples = jnp.broadcast_to(block_ref[i : i + 1, :].astype(f32), (STEP, length))
        moved = pltpu.roll(samples, 0, 1, stride=1, stride_axis=0)
        out_ref[i * STEP : (i + 1) * STEP, :] = jnp.where(lane < row, 0.0, moved).astype(bf16)


def shifted_copies(block):
    blk, length = block.shape
    return pl.pallas_call(
        shift_kernel,
        out_shape=jax.ShapeDtypeStruct((blk * STEP, length), bf16),
        in_specs=[VMEM_SPEC],
        out_specs=VMEM_SPEC,
        compiler_params=pltpu.CompilerParams(vmem_limit_bytes=4 << 20),
        name="shifted_copies",
    )(block)


def part_first_kernel(aux_ref, own_ref, out_ref, shifted, own_t):
    blk, length = own_ref.shape
    used = length - CODA_LO
    step = pl.program_id(0)

    @pl.when(step == 0)
    def _():
        own_t[:length, :] = own_ref[...].T
        own_t[length:, :] = jnp.zeros((own_t.shape[0] - length, blk), bf16)
        samples = aux_ref[...][:, :used].astype(f32)
        for b in range(STEP):
            shifted[b * blk : (b + 1) * blk, :] = shift_right(samples, b)

    halves = [
        own_t[pl.ds(pl.multiple_of(CODA_LO + (2 * step + a) * STEP, STEP), used), :] for a in range(2)
    ]
    out_ref[0] = jnp.dot(shifted[...], jnp.concatenate(halves, axis=1), preferred_element_type=f32)


def part_first(aux, own):
    blk, length = own.shape
    used = length - CODA_LO
    steps = CODA // (2 * STEP)
    return pl.pallas_call(
        part_first_kernel,
        out_shape=jax.ShapeDtypeStruct((steps, STEP * blk, 2 * blk), f32),
        grid=(steps,),
        in_specs=[VMEM_SPEC] * 2,
        out_specs=pl.BlockSpec((1, STEP * blk, 2 * blk), lambda step: (step, 0, 0)),
        scratch_shapes=[pltpu.VMEM((STEP * blk, used), bf16), pltpu.VMEM((length + CODA, blk), bf16)],
        compiler_params=pltpu.CompilerParams(vmem_limit_bytes=16 << 20),
        cost_estimate=pl.CostEstimate(
            flops=2 * CODA * blk * blk * used, transcendentals=0, bytes_accessed=4 * CODA * blk * blk
        ),
        name="part_first",
    )(aux, own)


def coda_kernel(windows, win_ref, start_ref, end_ref, first, *refs):
    aux_ref, own_ref = refs[:windows], refs[windows : 2 * windows]
    out_ref, shifted, own_t, limits, coda, coda_t, acc, rows = refs[2 * windows :]
    blk, length = own_ref[0].shape
    used = length - CODA_LO
    share = out_ref.shape[1]
    steps = share // 2
    pairs = CODA // 2
    scale_two = 1.0 / math.sqrt((windows + 1) * length)
    scale_three = 1.0 / math.sqrt(blk * CODA)
    win = win_ref[0]

    limits[0] = jnp.broadcast_to(start_ref[...], (blk, blk)).T
    limits[1] = jnp.broadcast_to(end_ref[...], (blk, blk)).T
    for w in range(windows):
        own_t[w, :length, :] = own_ref[w][...].T
        own_t[w, length:, :] = jnp.zeros((own_t.shape[1] - length, blk), bf16)
        samples = aux_ref[w][:, :used].astype(f32)
        for b in range(STEP):
            shifted[b * blk : (b + 1) * blk, w * used : (w + 1) * used] = shift_right(samples, b)
    coda[CODA * blk :, :] = jnp.zeros((coda.shape[0] - CODA * blk, blk), bf16)
    coda_t[: (steps - 1) * blk, :] = jnp.zeros(((steps - 1) * blk, 2 * blk), bf16)
    acc[...] = jnp.zeros(acc.shape, f32)

    half = STEP // 2

    def part(step, _):
        a_pair = step // 2
        b_half = step % 2
        pieces = []
        for w in range(windows):
            halves = [
                own_t[w, pl.ds(pl.multiple_of(CODA_LO + (2 * a_pair + a) * STEP, STEP), used), :]
                for a in range(2)
            ]
            pieces.append(jnp.concatenate(halves, axis=1))
        weights = jnp.concatenate(pieces, axis=0)
        row = pl.multiple_of(b_half * half * blk, blk)
        result = jnp.dot(shifted[pl.ds(row, half * blk), :], weights, preferred_element_type=f32)
        for b in range(half):
            for a in range(2):
                lag = (2 * a_pair + a) * STEP + b_half * half + b
                earlier = first[a_pair, pl.ds(row + b * blk, blk), a * blk : (a + 1) * blk]
                tile = (result[b * blk : (b + 1) * blk, a * blk : (a + 1) * blk] + earlier) * scale_two
                live = (lag >= limits[0]) & (lag < limits[1])
                tile = jnp.where(live, tile, 0.0)
                coda[pl.ds(pl.multiple_of(lag * blk, blk), blk), :] = tile.astype(bf16)
                place = pl.multiple_of((lag // 2 + steps - 1) * blk, blk)
                coda_t[pl.ds(place, blk), (b % 2) * blk : (b % 2 + 1) * blk] = tile.T.astype(bf16)
        return 0

    lax.fori_loop(0, CODA // STEP, part, 0)

    def accumulate(group, blocks):
        lhs, rhs = [], []
        for q in range(GROUP):
            pair = group * GROUP + q
            row = (pair + steps - blocks) * blk
            lhs.append(coda_t[pl.ds(pl.multiple_of(row, blk), blocks * blk), :])
            top = (2 * pair + win * share) * blk
            rhs.append(
                jnp.concatenate(
                    [coda[pl.ds(pl.multiple_of(top + b * blk, blk), 2 * blk), :] for b in range(2)], axis=1
                )
            )
        value = jnp.dot(
            jnp.concatenate(lhs, axis=1), jnp.concatenate(rhs, axis=0), preferred_element_type=f32
        )
        acc[(steps - blocks) * blk :, :] += value

    peeled = steps // GROUP - 1
    for group in range(peeled):
        accumulate(group, (group + 1) * GROUP)
    groups = pairs // GROUP - win * (share // (2 * GROUP))

    def whole(group, _):
        accumulate(group, steps)
        return 0

    lax.fori_loop(peeled, groups, whole, 0)
    for i in range(steps):
        for b in range(2):
            lag = 2 * (steps - 1 - i) + b
            rows[pl.ds(lag, blk, stride=share + ROW_PAD), :] = (
                acc[i * blk : (i + 1) * blk, b * blk : (b + 1) * blk] * scale_three
            )
    out_ref[...] = rows[...].reshape(blk, share + ROW_PAD, blk)[:, :share].astype(bf16)


def coda_limit(windows, blk, used):
    return (21 << 20) + 2 * STEP * blk * windows * used


def coda_coherence(win, start, end, first, aux, own, share):
    windows = len(own)
    blk, length = own[0].shape
    used = length - CODA_LO
    steps = share // 2
    return pl.pallas_call(
        functools.partial(coda_kernel, windows),
        out_shape=jax.ShapeDtypeStruct((blk, share, blk), bf16),
        in_specs=[SMEM_SPEC] + [VMEM_SPEC] * (3 + 2 * windows),
        out_specs=VMEM_SPEC,
        scratch_shapes=[
            pltpu.VMEM((STEP * blk, windows * used), bf16),
            pltpu.VMEM((windows, length + CODA, blk), bf16),
            pltpu.VMEM((2, blk, blk), jnp.int32),
            pltpu.VMEM(((CODA + 1) * blk, blk), bf16),
            pltpu.VMEM(((CODA // 2 + steps - 1) * blk, 2 * blk), bf16),
            pltpu.VMEM((steps * blk, 2 * blk), f32),
            pltpu.VMEM(((share + ROW_PAD) * blk, blk), f32),
        ],
        compiler_params=pltpu.CompilerParams(vmem_limit_bytes=coda_limit(windows, blk, used)),
        name="coda_coherence",
    )(win, start, end, first, *aux, *own)


def transpose_partners(partner_ref, partner_t):
    rounds, blk, length = partner_ref.shape
    for r in range(rounds):
        partner_t[:length, r * blk : (r + 1) * blk] = partner_ref[r].T
    partner_t[length:, :] = jnp.zeros((partner_t.shape[0] - length, rounds * blk), bf16)


def pair_first_kernel(win_ref, shifted_ref, partner_ref, out_ref, partner_t):
    length = partner_ref.shape[2]
    steps = pl.num_programs(0)
    step = pl.program_id(0)

    @pl.when(step == 0)
    def _():
        transpose_partners(partner_ref, partner_t)

    top = pl.multiple_of((win_ref[0] * steps + step) * STEP, STEP)
    out_ref[0] = jnp.dot(shifted_ref[...], partner_t[pl.ds(top, length), :], preferred_element_type=f32)


def pair_first(win, shifted, partner, share):
    rounds, blk, length = partner.shape
    steps = share // STEP
    return pl.pallas_call(
        pair_first_kernel,
        out_shape=jax.ShapeDtypeStruct((steps, blk * STEP, rounds * blk), f32),
        grid=(steps,),
        in_specs=[SMEM_SPEC, VMEM_SPEC, VMEM_SPEC],
        out_specs=pl.BlockSpec((1, blk * STEP, rounds * blk), lambda step: (step, 0, 0)),
        scratch_shapes=[pltpu.VMEM((length + LAGS, rounds * blk), bf16)],
        compiler_params=pltpu.CompilerParams(vmem_limit_bytes=12 << 20),
        cost_estimate=pl.CostEstimate(
            flops=2 * share * rounds * blk * blk * length,
            transcendentals=0,
            bytes_accessed=4 * share * rounds * blk * blk,
        ),
        name="pair_first",
    )(win, shifted, partner)


def pair_kernel(windows, win_ref, first_ref, *refs):
    shifted, partner_ref = refs[:windows], refs[windows : 2 * windows]
    out_ref, partner_t = refs[2 * windows :]
    rounds, blk, length = partner_ref[0].shape
    scale_two = 1.0 / math.sqrt((windows + 1) * length)
    steps = pl.num_programs(0)
    step = pl.program_id(0)

    @pl.when(step == 0)
    def _():
        for w in range(windows):
            transpose_partners(partner_ref[w], partner_t.at[w])

    top = pl.multiple_of((win_ref[0] * steps + step) * STEP, STEP)
    weights = jnp.concatenate([partner_t[w, pl.ds(top, length), :] for w in range(windows)], axis=0)
    half = blk // 2
    for part in range(2):
        rows = slice(part * half * STEP, (part + 1) * half * STEP)
        samples = jnp.concatenate([shifted[w][rows, :] for w in range(windows)], axis=1)
        result = jnp.dot(samples, weights, preferred_element_type=f32)
        result = ((result + first_ref[0, rows, :]) * scale_two).astype(bf16)
        for r in range(rounds):
            out_ref[r, part * half : (part + 1) * half] = result[:, r * blk : (r + 1) * blk].reshape(
                half, STEP, blk
            )


def pair_coherence(win, first, shifted, partner, share):
    windows = len(shifted)
    rounds, blk, length = partner[0].shape
    steps = share // STEP
    return pl.pallas_call(
        functools.partial(pair_kernel, windows),
        out_shape=jax.ShapeDtypeStruct((rounds, blk, share, blk), bf16),
        grid=(steps,),
        in_specs=[SMEM_SPEC, pl.BlockSpec((1,) + first.shape[1:], lambda step: (step, 0, 0))]
        + [VMEM_SPEC] * (2 * windows),
        out_specs=pl.BlockSpec((rounds, blk, STEP, blk), lambda step: (0, 0, step, 0)),
        scratch_shapes=[pltpu.VMEM((windows, length + LAGS, rounds * blk), bf16)],
        compiler_params=pltpu.CompilerParams(vmem_limit_bytes=20 << 20),
        name="pair_coherence",
    )(win, first, *shifted, *partner)


def per_device(traces, pairing, aux_owners, coda_start, coda_end):
    win_size = lax.axis_size("win")
    chan_size = lax.axis_size("chan")
    win_index = lax.axis_index("win")
    chan_index = lax.axis_index("chan")
    blk = traces.shape[1]
    rounds = pairing.shape[0]
    wanted = jnp.concatenate(
        [
            aux_owners,
            aux_owners,
            lax.dynamic_index_in_dim(pairing, chan_index ^ 1, 1, keepdims=False),
            lax.dynamic_index_in_dim(pairing, chan_index, 1, keepdims=False),
        ]
    )
    which = jnp.mod(chan_index - wanted, chan_size) // 2
    crossed = jnp.mod(chan_index - wanted, 2)
    aux_crossed, crossed = crossed[:1], crossed[2 + rounds :]
    win = win_index.reshape(1).astype(jnp.int32)
    traces, which, aux_crossed, crossed, win = lax.optimization_barrier(
        (traces, which, aux_crossed, crossed, win)
    )
    white = whiten(traces)

    def exchange(block, k):
        return lax.ppermute(block, "win", [(i, i ^ k) for i in range(win_size)])

    def cross(block):
        return lax.ppermute(block, "chan", [(i, i ^ 1) for i in range(chan_size)])

    column = [white] + [
        lax.ppermute(white, "chan", [(i, (i + 2 * k) % chan_size) for i in range(chan_size)])
        for k in range(1, chan_size // 2)
    ]
    own_all = [white] + [exchange(white, k) for k in range(1, win_size)]
    copies = [shifted_copies(block) for block in own_all]
    own_all, first_copies, column = lax.optimization_barrier((own_all, copies[0], column))
    aux_sent, aux_held, sent, held = pick(which, column, rounds)
    aux = merge(aux_crossed, aux_held[None], cross(aux_sent)[None])[0]
    partners = merge(crossed, held, cross(sent))
    aux_rest = [exchange(aux, k) for k in range(1, win_size)]
    pair_begun = pair_first(win, first_copies, partners, LAGS // win_size)
    part_begun = part_first(aux, own_all[0])
    partners, aux_rest, pair_begun, part_begun, copies = lax.optimization_barrier(
        (partners, aux_rest, pair_begun, part_begun, copies[1:])
    )
    partner_rest = [exchange(partners, k) for k in range(1, win_size)]
    three = coda_coherence(
        win, coda_start, coda_end, part_begun, aux_rest, own_all[1:], LAGS3 // win_size
    )
    pair = pair_coherence(win, pair_begun, copies, partner_rest, LAGS // win_size)
    return (pair, three)


def solution(mesh):
    in_specs = (P("win", "chan", None), P(), P(), P(), P())
    out_specs = (P(None, "chan", "win", None), P("chan", "win", None))
    return jax.shard_map(per_device, mesh=mesh, in_specs=in_specs, out_specs=out_specs, check_vma=False)
```

time: 111 us -> 94 us (0.85)
  waiting for transfers between devices: 22.5 us -> 15 us
  between operations: 5.62 us -> 1.45 us
  local copies, waits for them, and re-layouts: 4.56 us -> 2.03 us
  other arithmetic: 2.12 us -> 0.11 us
    pallas_call x0 -> x9, Pallas kernels: none -> 14.1 us  [the longest x1 4.82 us: part_first(): pl.pallas_call(part_first_kernel, out_shape=jax.ShapeDtypeStruct((steps,...]
    pallas_call x1, Pallas kernels: 22.8 us -> 11.8 us  [pair_coherence(): pl.pallas_call(functools.partial(pair_kernel, windows), out_shape=jax.Sha...]
    ppermute x9, waiting for transfers between devices: 11.7 us -> 4.26 us  [exchange(): return lax.ppermute(block, 'win', [(i, i ^ k) for i in range(win_size)])]
    pallas_call x1, Pallas kernels: 37.8 us -> 33.7 us  [coda_coherence(): pl.pallas_call(functools.partial(coda_kernel, windows), out_shape=jax.Sha...]
    broadcast_in_dim x2 -> x0, local copies, waits for them, and re-layouts: 1.41 us -> none  [the longest x1 0.71 us: per_device(): end = jnp.broadcast_to(coda_end[0][:, None], (blk, blk))]
    another operation x3 -> x0, other arithmetic: 1.12 us -> none  [the longest x2 1.05 us: per_device(): partners = jnp.stack(blocks[1:])]
  transfers between devices with their start and end apart: 13 -> 14, of which waited for: 7 -> 5; matrix products, arithmetic and copies ran while one was open for 3% -> 0% of each run, Pallas kernels for 34% -> 50%
where the time goes in v3:
time: 94 us; the launch traced here: 93.8 us
  Pallas kernels  61.4 us (65%)
  waiting for transfers between devices  15 us (16%)
  starting transfers between devices  13.9 us (15%)
  local copies, waits for them, and re-layouts  2.03 us (2%)
  between operations  1.45 us (2%)
    pallas_call x1, Pallas kernels, coda_coherence(): pl.pallas_call(functools.partial(coda_kernel, windows), out_shape=jax.Sha...  33.7 us
    pallas_call x1, Pallas kernels, pair_coherence(): pl.pallas_call(functools.partial(pair_kernel, windows), out_shape=jax.Sha...  11.8 us
    ppermute x3, waiting for transfers between devices, per_device(): lax.ppermute(white, 'chan', [(i, (i + 2 * k) % chan_size) for i in range(...  10.7 us
    ppermute x9, starting transfers between devices, exchange(): return lax.ppermute(block, 'win', [(i, i ^ k) for i in range(win_size)])  10.6 us
    pallas_call x1, Pallas kernels, part_first(): pl.pallas_call(part_first_kernel, out_shape=jax.ShapeDtypeStruct((steps,...  4.82 us
    ppermute x9, waiting for transfers between devices, exchange(): return lax.ppermute(block, 'win', [(i, i ^ k) for i in range(win_size)])  4.26 us
    pallas_call x1, Pallas kernels, pair_first(): pl.pallas_call(pair_first_kernel, out_shape=jax.ShapeDtypeStruct((steps,...  4.18 us
    pallas_call x4, Pallas kernels, shifted_copies(): pl.pallas_call(shift_kernel, out_shape=jax.ShapeDtypeStruct((blk * STEP,...  3.51 us
  transfers between devices with their start and end apart: 14, of which 5 were waited for; matrix products, arithmetic and copies ran while one was open for 0% of the time, Pallas kernels for 50%

profile of v3, /device:TPU:8, one launch (start us, length us, event | category | flops | bytes accessed | tf_op | source)
XLA Modules:
  0.0 93.8 jit_solution(3944224882589709625)
XLA Ops:
  1.3 1.0 %dynamic-slice_reduce_fusion.1 = (s32[2]{0:T(128)S(1)}, s32[2]{0:T(128)S(1)}) fusion(s32[2,8]{1,0:T(2,128)} %param.6, s32[]{:T(128)S(6)} %select_n.23, s32[]{:T(128)S(6)} %select_n.24), kind=kLoop, calls=%fused_computation.10 | loop fusion | bytes 40 | tf_op jit(solution)/shard_map/jit(dynamic_index_in_dim)/dynamic_slice | solution.py:372
  2.5 1.7 %whiten.1.block_ref.refs_0_.own_ref = bf16[128,768]{1,0:T(8,128)(2,1)} custom-call(bf16[1,128,768]{2,1,0:T(8,128)(2,1)} %traces_ref), custom_call_target="tpu_custom_call" | custom-call | tf_op jit(solution)/shard_map/whiten/pallas_call | solution.py:34
  4.2 1.5 %collective-permute-start = (bf16[128,768]{1,0:T(8,128)(2,1)}, bf16[128,768]{1,0:T(8,128)(2,1)S(1)}, u32[]{:S(2)}, u32[]{:S(2)}) collective-permute-start(bf16[128,768]{1,0:T(8,128)(2,1)} %whiten.1.block_ref.refs_0_.own_ref), channel_id=1, source_target_pairs={{0,1},{1,0},{2,3},{3,2},{4,5},{5,4},{6,7},{7,6},{8,9},{9,8},{10,11... | collective-permute-start | bytes 589832 | tf_op jit(solution)/shard_map/ppermute | solution.py:386
  5.7 1.5 %collective-permute-start.1 = (bf16[128,768]{1,0:T(8,128)(2,1)}, bf16[128,768]{1,0:T(8,128)(2,1)S(1)}, u32[]{:S(2)}, u32[]{:S(2)}) collective-permute-start(bf16[128,768]{1,0:T(8,128)(2,1)} %whiten.1.block_ref.refs_0_.own_ref), channel_id=1, source_target_pairs={{0,2},{1,3},{2,0},{3,1},{4,6},{5,7},{6,4},{7,5},{8,10},{9,11},{10,... | collective-permute-start | bytes 589832 | tf_op jit(solution)/shard_map/ppermute | solution.py:386
  7.7 1.6 %collective-permute-start.3 = (bf16[128,768]{1,0:T(8,128)(2,1)}, bf16[128,768]{1,0:T(8,128)(2,1)S(1)}, u32[]{:S(2)}, u32[]{:S(2)}) collective-permute-start(bf16[128,768]{1,0:T(8,128)(2,1)} %whiten.1.block_ref.refs_0_.own_ref), channel_id=1, source_target_pairs={{0,8},{4,12},{8,16},{12,20},{16,24},{20,28},{24,0},{28,4},{1,9},{5... | collective-permute-start | bytes 589832 | tf_op jit(solution)/shard_map/ppermute | solution.py:392
  9.3 1.0 %collective-permute-start.4 = (bf16[128,768]{1,0:T(8,128)(2,1)}, bf16[128,768]{1,0:T(8,128)(2,1)S(1)}, u32[]{:S(2)}, u32[]{:S(2)}) collective-permute-start(bf16[128,768]{1,0:T(8,128)(2,1)} %whiten.1.block_ref.refs_0_.own_ref), channel_id=1, source_target_pairs={{0,16},{4,20},{8,24},{12,28},{16,0},{20,4},{24,8},{28,12},{1,17},{... | collective-permute-start | bytes 589832 | tf_op jit(solution)/shard_map/ppermute | solution.py:392
  10.3 1.9 %collective-permute-done.block_ref.refs_3_ = bf16[128,768]{1,0:T(8,128)(2,1)S(1)} collective-permute-done((bf16[128,768]{1,0:T(8,128)(2,1)}, bf16[128,768]{1,0:T(8,128)(2,1)S(1)}, u32[]{:S(2)}, u32[]{:S(2)}) %collective-permute-start) | collective-permute-done | bytes 196640 | tf_op jit(solution)/shard_map/ppermute | solution.py:386
  12.3 1.0 %copy-done = bf16[128,768]{1,0:T(8,128)(2,1)S(1)} copy-done((bf16[128,768]{1,0:T(8,128)(2,1)S(1)}, bf16[128,768]{1,0:T(8,128)(2,1)}, u32[]{:S(2)}) %copy-start) | copy-done | bytes 196632
  13.3 0.9 shifted_copies.4.shifted_ref
  14.1 2.3 %collective-permute-done.1.block_ref.refs_4_ = bf16[128,768]{1,0:T(8,128)(2,1)S(1)} collective-permute-done((bf16[128,768]{1,0:T(8,128)(2,1)}, bf16[128,768]{1,0:T(8,128)(2,1)S(1)}, u32[]{:S(2)}, u32[]{:S(2)}) %collective-permute-start.1) | collective-permute-done | bytes 196640 | tf_op jit(solution)/shard_map/ppermute | solution.py:386
  16.5 6.9 %collective-permute-done.3.refs_1_ = bf16[128,768]{1,0:T(8,128)(2,1)S(1)} collective-permute-done((bf16[128,768]{1,0:T(8,128)(2,1)}, bf16[128,768]{1,0:T(8,128)(2,1)S(1)}, u32[]{:S(2)}, u32[]{:S(2)}) %collective-permute-start.3) | collective-permute-done | bytes 196640 | tf_op jit(solution)/shard_map/ppermute | solution.py:392
  23.4 2.2 %collective-permute-done.4.refs_2_ = bf16[128,768]{1,0:T(8,128)(2,1)S(1)} collective-permute-done((bf16[128,768]{1,0:T(8,128)(2,1)}, bf16[128,768]{1,0:T(8,128)(2,1)S(1)}, u32[]{:S(2)}, u32[]{:S(2)}) %collective-permute-start.4) | collective-permute-done | bytes 196640 | tf_op jit(solution)/shard_map/ppermute | solution.py:392
  25.5 1.7 %collective-permute-done.5.refs_3_ = bf16[128,768]{1,0:T(8,128)(2,1)S(1)} collective-permute-done((bf16[128,768]{1,0:T(8,128)(2,1)}, bf16[128,768]{1,0:T(8,128)(2,1)S(1)}, u32[]{:S(2)}, u32[]{:S(2)}) %collective-permute-start.5) | collective-permute-done | bytes 196640 | tf_op jit(solution)/shard_map/ppermute | solution.py:392
  27.2 0.8 pick.1
  28.6 0.9 shifted_copies.5.refs_0_
  29.5 0.9 shifted_copies.6.refs_1_
  30.4 0.9 shifted_copies.7.refs_2_
  31.3 2.5 %collective-permute-start.10 = (bf16[128,768]{1,0:T(8,128)(2,1)S(1)}, bf16[128,768]{1,0:T(8,128)(2,1)S(1)}, u32[]{:S(2)}, u32[]{:S(2)}) collective-permute-start(bf16[128,768]{1,0:T(8,128)(2,1)S(1)} %bitcast.5), channel_id=1, source_target_pairs={{0,3},{1,2},{2,1},{3,0},{4,7},{5,6},{6,5},{7,4},{8,11},{9,10},{10,... | collective-permute-start | bytes 589832 | tf_op jit(solution)/shard_map/ppermute | solution.py:386
  34.9 4.8 %part_first.1.first = f32[4,2048,256]{2,1,0:T(8,128)S(1)} custom-call(bf16[128,768]{1,0:T(8,128)(2,1)S(1)} %bitcast.8, bf16[128,768]{1,0:T(8,128)(2,1)S(1)} %copy-done.1), custom_call_target="tpu_custom_call" | custom-call | flops 2684354560 | bytes 8388608 | tf_op jit(solution)/shard_map/part_first/pallas_call | solution.py:145
  40.5 4.2 %pair_first.1.first_ref = f32[4,2048,256]{2,1,0:T(8,128)S(1)} custom-call(s32[1]{0:T(128)} %bitcast.win_ref, bf16[2048,768]{1,0:T(8,128)(2,1)S(1)} %shifted_copies.4.shifted_ref, bf16[2,128,768]{2,1,0:T(8,128)(2,1)S(1)} %merge.2.partner_ref), custom_call_target="tpu_custom_call" | custom-call | flops 3221225472 | bytes 8388608 | tf_op jit(solution)/shard_map/pair_first/pallas_call | solution.py:300
  44.7 1.6 %collective-permute-start.11 = (bf16[2,128,768]{2,1,0:T(8,128)(2,1)S(1)}, bf16[2,128,768]{2,1,0:T(8,128)(2,1)S(1)}, u32[]{:S(2)}, u32[]{:S(2)}) collective-permute-start(bf16[2,128,768]{2,1,0:T(8,128)(2,1)S(1)} %merge.2.partner_ref), channel_id=1, source_target_pairs={{0,1},{1,0},{2,3},{3,2},{4,5},{5,4},{6,7},{7,6},{8,9},{9,8},{10,11... | collective-permute-start | bytes 1179656 | tf_op jit(solution)/shard_map/ppermute | solution.py:386
  46.3 1.5 %collective-permute-start.12 = (bf16[2,128,768]{2,1,0:T(8,128)(2,1)S(1)}, bf16[2,128,768]{2,1,0:T(8,128)(2,1)S(1)}, u32[]{:S(2)}, u32[]{:S(2)}) collective-permute-start(bf16[2,128,768]{2,1,0:T(8,128)(2,1)S(1)} %merge.2.partner_ref), channel_id=1, source_target_pairs={{0,2},{1,3},{2,0},{3,1},{4,6},{5,7},{6,4},{7,5},{8,10},{9,11},{10,... | collective-permute-start | bytes 1179656 | tf_op jit(solution)/shard_map/ppermute | solution.py:386
  48.3 33.7 %coda_coherence.1 = bf16[128,32,128]{2,1,0:T(8,128)(2,1)} custom-call(s32[1]{0:T(128)} %bitcast.win_ref, s32[1,128]{1,0:T(1,128)S(1)} %copy-done.2, s32[1,128]{1,0:T(1,128)S(1)} %copy-done.3, f32[4,2048,256]{2,1,0:T(8,128)S(1)} %part_first.1.first, bf16[128,768]{1,0:T(8,128)(2,1)S(1)} %collective-permute-done.8.refs_0_, ...), custom_call_target="tpu_custom_call" | custom-call | tf_op jit(solution)/shard_map/coda_coherence/pallas_call | solution.py:258
  82.0 11.8 %pair_coherence.1 = bf16[2,128,64,128]{3,2,1,0:T(8,128)(2,1)} custom-call(s32[1]{0:T(128)} %bitcast.win_ref, f32[4,2048,256]{2,1,0:T(8,128)S(1)} %pair_first.1.first_ref, bf16[2048,768]{1,0:T(8,128)(2,1)S(1)} %shifted_copies.5.refs_0_, bf16[2048,768]{1,0:T(8,128)(2,1)S(1)} %shifted_copies.6.refs_1_, bf16[2048,768]{1,0:T(8,128)(2,1)S(1)} %shifted_copies.7.refs_2_, ...), custom_call_target="tpu_custom_call" | custom-call | tf_op jit(solution)/shard_map/pair_coherence/pallas_call | solution.py:348
  (28 shorter events, 3.7 us)
Async XLA Ops:
  4.2 8.0 %collective-permute-start = (bf16[128,768]{1,0:T(8,128)(2,1)}, bf16[128,768]{1,0:T(8,128)(2,1)S(1)}, u32[]{:S(2)}, u32[]{:S(2)}) collective-permute-start(bf16[128,768]{1,0:T(8,128)(2,1)} %whiten.1.block_ref.refs_0_.own_ref), channel_id=1, source_target_pairs={{0,1},{1,0},{2,3},{3,2},{4,5},{5,4},{6,7},{7,6},{8,9},{9,8},{10,11... | collective-permute-start | bytes 589832 | tf_op jit(solution)/shard_map/ppermute | solution.py:386
  5.7 10.8 %collective-permute-start.1 = (bf16[128,768]{1,0:T(8,128)(2,1)}, bf16[128,768]{1,0:T(8,128)(2,1)S(1)}, u32[]{:S(2)}, u32[]{:S(2)}) collective-permute-start(bf16[128,768]{1,0:T(8,128)(2,1)} %whiten.1.block_ref.refs_0_.own_ref), channel_id=1, source_target_pairs={{0,2},{1,3},{2,0},{3,1},{4,6},{5,7},{6,4},{7,5},{8,10},{9,11},{10,... | collective-permute-start | bytes 589832 | tf_op jit(solution)/shard_map/ppermute | solution.py:386
  7.2 9.3 %collective-permute-start.2 = (bf16[128,768]{1,0:T(8,128)(2,1)}, bf16[128,768]{1,0:T(8,128)(2,1)S(1)}, u32[]{:S(2)}, u32[]{:S(2)}) collective-permute-start(bf16[128,768]{1,0:T(8,128)(2,1)} %whiten.1.block_ref.refs_0_.own_ref), channel_id=1, source_target_pairs={{0,3},{1,2},{2,1},{3,0},{4,7},{5,6},{6,5},{7,4},{8,11},{9,10},{10,... | collective-permute-start | bytes 589832 | tf_op jit(solution)/shard_map/ppermute | solution.py:386
  7.7 15.7 %collective-permute-start.3 = (bf16[128,768]{1,0:T(8,128)(2,1)}, bf16[128,768]{1,0:T(8,128)(2,1)S(1)}, u32[]{:S(2)}, u32[]{:S(2)}) collective-permute-start(bf16[128,768]{1,0:T(8,128)(2,1)} %whiten.1.block_ref.refs_0_.own_ref), channel_id=1, source_target_pairs={{0,8},{4,12},{8,16},{12,20},{16,24},{20,28},{24,0},{28,4},{1,9},{5... | collective-permute-start | bytes 589832 | tf_op jit(solution)/shard_map/ppermute | solution.py:392
  9.3 16.3 %collective-permute-start.4 = (bf16[128,768]{1,0:T(8,128)(2,1)}, bf16[128,768]{1,0:T(8,128)(2,1)S(1)}, u32[]{:S(2)}, u32[]{:S(2)}) collective-permute-start(bf16[128,768]{1,0:T(8,128)(2,1)} %whiten.1.block_ref.refs_0_.own_ref), channel_id=1, source_target_pairs={{0,16},{4,20},{8,24},{12,28},{16,0},{20,4},{24,8},{28,12},{1,17},{... | collective-permute-start | bytes 589832 | tf_op jit(solution)/shard_map/ppermute | solution.py:392
  12.2 15.0 %collective-permute-start.5 = (bf16[128,768]{1,0:T(8,128)(2,1)}, bf16[128,768]{1,0:T(8,128)(2,1)S(1)}, u32[]{:S(2)}, u32[]{:S(2)}) collective-permute-start(bf16[128,768]{1,0:T(8,128)(2,1)} %whiten.1.block_ref.refs_0_.own_ref), channel_id=1, source_target_pairs={{0,24},{4,28},{8,0},{12,4},{16,8},{20,12},{24,16},{28,20},{1,25},{... | collective-permute-start | bytes 589832 | tf_op jit(solution)/shard_map/ppermute | solution.py:392
  12.3 1.0 %copy-start = (bf16[128,768]{1,0:T(8,128)(2,1)S(1)}, bf16[128,768]{1,0:T(8,128)(2,1)}, u32[]{:S(2)}) copy-start(bf16[128,768]{1,0:T(8,128)(2,1)} %whiten.1.block_ref.refs_0_.own_ref) | copy-start | bytes 589828
  28.0 3.2 %collective-permute-start.7 = (bf16[128,768]{1,0:T(8,128)(2,1)S(1)}, bf16[128,768]{1,0:T(8,128)(2,1)S(1)}, u32[]{:S(2)}, u32[]{:S(2)}) collective-permute-start(bf16[128,768]{1,0:T(8,128)(2,1)S(1)} %get-tuple-element.41), channel_id=1, source_target_pairs={{0,4},{4,0},{8,12},{12,8},{16,20},{20,16},{24,28},{28,24},{1,5},{5... | collective-permute-start | bytes 589832 | tf_op jit(solution)/shard_map/ppermute | solution.py:389
  28.1 11.6 %collective-permute-start.6 = (bf16[2,128,768]{2,1,0:T(8,128)(2,1)S(1)}, bf16[2,128,768]{2,1,0:T(8,128)(2,1)S(1)}, u32[]{:S(2)}, u32[]{:S(2)}) collective-permute-start(bf16[2,128,768]{2,1,0:T(8,128)(2,1)S(1)} %get-tuple-element.38), channel_id=1, source_target_pairs={{0,4},{4,0},{8,12},{12,8},{16,20},{20,16},{24,28},{28,24},{1,5},{5... | collective-permute-start | bytes 1179656 | tf_op jit(solution)/shard_map/ppermute | solution.py:389
  29.5 5.4 %copy-start.1 = (bf16[128,768]{1,0:T(8,128)(2,1)S(1)}, bf16[128,768]{1,0:T(8,128)(2,1)}, u32[]{:S(2)}) copy-start(bf16[128,768]{1,0:T(8,128)(2,1)} %whiten.1.block_ref.refs_0_.own_ref) | copy-start | bytes 589828
  31.3 13.4 %collective-permute-start.10 = (bf16[128,768]{1,0:T(8,128)(2,1)S(1)}, bf16[128,768]{1,0:T(8,128)(2,1)S(1)}, u32[]{:S(2)}, u32[]{:S(2)}) collective-permute-start(bf16[128,768]{1,0:T(8,128)(2,1)S(1)} %bitcast.5), channel_id=1, source_target_pairs={{0,3},{1,2},{2,1},{3,0},{4,7},{5,6},{6,5},{7,4},{8,11},{9,10},{10,... | collective-permute-start | bytes 589832 | tf_op jit(solution)/shard_map/ppermute | solution.py:386
  33.8 10.9 %collective-permute-start.8 = (bf16[128,768]{1,0:T(8,128)(2,1)S(1)}, bf16[128,768]{1,0:T(8,128)(2,1)S(1)}, u32[]{:S(2)}, u32[]{:S(2)}) collective-permute-start(bf16[128,768]{1,0:T(8,128)(2,1)S(1)} %bitcast.6), channel_id=1, source_target_pairs={{0,1},{1,0},{2,3},{3,2},{4,5},{5,4},{6,7},{7,6},{8,9},{9,8},{10,11... | collective-permute-start | bytes 589832 | tf_op jit(solution)/shard_map/ppermute | solution.py:386
  34.4 10.4 %collective-permute-start.9 = (bf16[128,768]{1,0:T(8,128)(2,1)S(1)}, bf16[128,768]{1,0:T(8,128)(2,1)S(1)}, u32[]{:S(2)}, u32[]{:S(2)}) collective-permute-start(bf16[128,768]{1,0:T(8,128)(2,1)S(1)} %bitcast.7), channel_id=1, source_target_pairs={{0,2},{1,3},{2,0},{3,1},{4,6},{5,7},{6,4},{7,5},{8,10},{9,11},{10,... | collective-permute-start | bytes 589832 | tf_op jit(solution)/shard_map/ppermute | solution.py:386
  40.5 7.8 %copy-start.2 = (s32[1,128]{1,0:T(1,128)S(1)}, s32[1,128]{1,0:T(1,128)}, u32[]{:S(2)}) copy-start(s32[1,128]{1,0:T(1,128)} %start_ref.1) | copy-start | bytes 1540
  40.5 7.8 %copy-start.3 = (s32[1,128]{1,0:T(1,128)S(1)}, s32[1,128]{1,0:T(1,128)}, u32[]{:S(2)}) copy-start(s32[1,128]{1,0:T(1,128)} %end_ref.1) | copy-start | bytes 1540
  44.7 37.3 %collective-permute-start.11 = (bf16[2,128,768]{2,1,0:T(8,128)(2,1)S(1)}, bf16[2,128,768]{2,1,0:T(8,128)(2,1)S(1)}, u32[]{:S(2)}, u32[]{:S(2)}) collective-permute-start(bf16[2,128,768]{2,1,0:T(8,128)(2,1)S(1)} %merge.2.partner_ref), channel_id=1, source_target_pairs={{0,1},{1,0},{2,3},{3,2},{4,5},{5,4},{6,7},{7,6},{8,9},{9,8},{10,11... | collective-permute-start | bytes 1179656 | tf_op jit(solution)/shard_map/ppermute | solution.py:386
  46.3 35.7 %collective-permute-start.12 = (bf16[2,128,768]{2,1,0:T(8,128)(2,1)S(1)}, bf16[2,128,768]{2,1,0:T(8,128)(2,1)S(1)}, u32[]{:S(2)}, u32[]{:S(2)}) collective-permute-start(bf16[2,128,768]{2,1,0:T(8,128)(2,1)S(1)} %merge.2.partner_ref), channel_id=1, source_target_pairs={{0,2},{1,3},{2,0},{3,1},{4,6},{5,7},{6,4},{7,5},{8,10},{9,11},{10,... | collective-permute-start | bytes 1179656 | tf_op jit(solution)/shard_map/ppermute | solution.py:386
  47.8 34.2 %collective-permute-start.13 = (bf16[2,128,768]{2,1,0:T(8,128)(2,1)S(1)}, bf16[2,128,768]{2,1,0:T(8,128)(2,1)S(1)}, u32[]{:S(2)}, u32[]{:S(2)}) collective-permute-start(bf16[2,128,768]{2,1,0:T(8,128)(2,1)S(1)} %merge.2.partner_ref), channel_id=1, source_target_pairs={{0,3},{1,2},{2,1},{3,0},{4,7},{5,6},{6,5},{7,4},{8,11},{9,10},{10,... | collective-permute-start | bytes 1179656 | tf_op jit(solution)/shard_map/ppermute | solution.py:386

commit v4 on v3

v4 whole, which is shorter than its diff:
```python
import functools
import math

import jax
import jax.numpy as jnp
from jax import lax
from jax.experimental import pallas as pl
from jax.experimental.pallas import tpu as pltpu
from jax.sharding import PartitionSpec as P

LAGS = 256
CODA = 128
CODA_LO = 128
LAGS3 = 128
EPS = 1e-05
STEP = 16
GROUP = 4

SMEM_SPEC = pl.BlockSpec(memory_space=pltpu.SMEM)
VMEM_SPEC = pl.BlockSpec(memory_space=pltpu.VMEM)
ROW_PAD = 8

f32 = jnp.float32
bf16 = jnp.bfloat16


def white_block(traces):
    samples = traces.astype(f32)
    energy_mean = jnp.mean(samples * samples, axis=-1, keepdims=True)
    return (samples * lax.rsqrt(energy_mean + EPS)).astype(bf16)


def shift_right(block, count):
    if count == 0:
        return block.astype(bf16)
    moved = pltpu.roll(block, count, 1)
    lane = lax.broadcasted_iota(jnp.int32, block.shape, 1)
    return jnp.where(lane < count, 0.0, moved).astype(bf16)


def pick_kernel(rounds, owners_ref, pairing_ref, *refs):
    column, out_refs = refs[:-4], refs[-4:]
    count = len(column)
    chan = lax.axis_index("chan")
    other = chan + 1 - 2 * (chan % 2)
    aux = owners_ref[0]
    slots = [(out_refs[0], aux), (out_refs[1], aux)]
    slots += [(out_refs[2].at[r], pairing_ref[r, other]) for r in range(rounds)]
    slots += [(out_refs[3].at[r], pairing_ref[r, chan]) for r in range(rounds)]
    for slot, block in slots:
        distance = (chan - block + 2 * count) % (2 * count) // 2
        for k in range(count):

            @pl.when(distance == k)
            def _():
                slot[...] = column[k][...]


def pick(owners, pairing, column):
    block = column[0].shape
    rounds = pairing.shape[0]
    shapes = [block, block, (rounds,) + block, (rounds,) + block]
    return pl.pallas_call(
        functools.partial(pick_kernel, rounds),
        out_shape=[jax.ShapeDtypeStruct(shape, bf16) for shape in shapes],
        in_specs=[SMEM_SPEC] * 2 + [VMEM_SPEC] * len(column),
        out_specs=[VMEM_SPEC] * 4,
        compiler_params=pltpu.CompilerParams(vmem_limit_bytes=2 << 20),
        name="pick",
    )(owners, pairing, *column)


def merge(blocks_of, scalars, held, got):
    def kernel(scalars_ref, held_ref, got_ref, out_ref):
        chan = lax.axis_index("chan")
        for r, block in enumerate(blocks_of(scalars_ref, chan)):
            same = (chan + block) % 2 == 0
            here, sent, out = (ref if len(ref.shape) == 2 else ref.at[r] for ref in (held_ref, got_ref, out_ref))

            @pl.when(same)
            def _():
                out[...] = white_block(here[...])

            @pl.when(jnp.logical_not(same))
            def _():
                out[...] = white_block(sent[...])

    return pl.pallas_call(
        kernel,
        out_shape=jax.ShapeDtypeStruct(held.shape, bf16),
        in_specs=[SMEM_SPEC, VMEM_SPEC, VMEM_SPEC],
        out_specs=VMEM_SPEC,
        compiler_params=pltpu.CompilerParams(vmem_limit_bytes=4 << 20),
        name="merge",
    )(scalars, held, got)


def shift_kernel(block_ref, out_ref, white_ref, *raw_ref):
    for ref in raw_ref:
        ref[...] = block_ref[...]
    white_ref[...] = white_block(block_ref[...])
    blk, length = block_ref.shape
    lane = lax.broadcasted_iota(jnp.int32, (STEP, length), 1)
    row = lax.broadcasted_iota(jnp.int32, (STEP, length), 0)
    for i in range(blk):
        samples = jnp.broadcast_to(white_ref[i : i + 1, :].astype(f32), (STEP, length))
        moved = pltpu.roll(samples, 0, 1, stride=1, stride_axis=0)
        out_ref[i * STEP : (i + 1) * STEP, :] = jnp.where(lane < row, 0.0, moved).astype(bf16)


def shifted_copies(block, raw=False):
    blk, length = block.shape
    return pl.pallas_call(
        shift_kernel,
        out_shape=[
            jax.ShapeDtypeStruct((blk * STEP, length), bf16),
            jax.ShapeDtypeStruct((blk, length), bf16),
        ]
        + [jax.ShapeDtypeStruct((blk, length), bf16)] * raw,
        in_specs=[VMEM_SPEC],
        out_specs=[VMEM_SPEC] * (2 + raw),
        compiler_params=pltpu.CompilerParams(vmem_limit_bytes=4 << 20),
        name="shifted_copies",
    )(block)


def part_first_kernel(aux_ref, own_ref, out_ref, shifted, own_t):
    blk, length = own_ref.shape
    used = length - CODA_LO
    step = pl.program_id(0)

    @pl.when(step == 0)
    def _():
        own_t[:length, :] = own_ref[...].T
        own_t[length:, :] = jnp.zeros((own_t.shape[0] - length, blk), bf16)
        samples = aux_ref[...][:, :used].astype(f32)
        for b in range(STEP):
            shifted[b * blk : (b + 1) * blk, :] = shift_right(samples, b)

    halves = [
        own_t[pl.ds(pl.multiple_of(CODA_LO + (2 * step + a) * STEP, STEP), used), :] for a in range(2)
    ]
    out_ref[0] = jnp.dot(shifted[...], jnp.concatenate(halves, axis=1), preferred_element_type=f32)


def part_first(aux, own):
    blk, length = own.shape
    used = length - CODA_LO
    steps = CODA // (2 * STEP)
    return pl.pallas_call(
        part_first_kernel,
        out_shape=jax.ShapeDtypeStruct((steps, STEP * blk, 2 * blk), f32),
        grid=(steps,),
        in_specs=[VMEM_SPEC] * 2,
        out_specs=pl.BlockSpec((1, STEP * blk, 2 * blk), lambda step: (step, 0, 0)),
        scratch_shapes=[pltpu.VMEM((STEP * blk, used), bf16), pltpu.VMEM((length + CODA, blk), bf16)],
        compiler_params=pltpu.CompilerParams(vmem_limit_bytes=16 << 20),
        cost_estimate=pl.CostEstimate(
            flops=2 * CODA * blk * blk * used, transcendentals=0, bytes_accessed=4 * CODA * blk * blk
        ),
        name="part_first",
    )(aux, own)


def coda_kernel(windows, start_ref, end_ref, first, *refs):
    aux_ref, own_ref = refs[:windows], refs[windows : 2 * windows]
    out_ref, shifted, own_t, limits, coda, coda_t, acc, rows = refs[2 * windows :]
    blk, length = own_ref[0].shape
    used = length - CODA_LO
    share = out_ref.shape[1]
    steps = share // 2
    pairs = CODA // 2
    scale_two = 1.0 / math.sqrt((windows + 1) * length)
    scale_three = 1.0 / math.sqrt(blk * CODA)
    win = lax.axis_index("win")

    limits[0] = jnp.broadcast_to(start_ref[...], (blk, blk)).T
    limits[1] = jnp.broadcast_to(end_ref[...], (blk, blk)).T
    for w in range(windows):
        own_t[w, :length, :] = own_ref[w][...].T
        own_t[w, length:, :] = jnp.zeros((own_t.shape[1] - length, blk), bf16)
        samples = aux_ref[w][:, :used].astype(f32)
        for b in range(STEP):
            shifted[b * blk : (b + 1) * blk, w * used : (w + 1) * used] = shift_right(samples, b)
    coda[CODA * blk :, :] = jnp.zeros((coda.shape[0] - CODA * blk, blk), bf16)
    coda_t[: (steps - 1) * blk, :] = jnp.zeros(((steps - 1) * blk, 2 * blk), bf16)
    acc[...] = jnp.zeros(acc.shape, f32)

    chunk = STEP // 2

    def part(a_pair, limit):
        pieces = []
        for w in range(windows):
            halves = [
                own_t[w, pl.ds(pl.multiple_of(CODA_LO + (2 * a_pair + a) * STEP, STEP), used), :]
                for a in range(2)
            ]
            pieces.append(jnp.concatenate(halves, axis=1))
        weights = jnp.concatenate(pieces, axis=0)
        for b_first in range(0, STEP, chunk):
            rows_here = slice(b_first * blk, (b_first + chunk) * blk)
            result = jnp.dot(shifted[rows_here, :], weights, preferred_element_type=f32)
            result = (result + first[a_pair, rows_here, :]) * scale_two
            for b in range(chunk):
                for a in range(2):
                    lag = (2 * a_pair + a) * STEP + b_first + b
                    tile = result[b * blk : (b + 1) * blk, a * blk : (a + 1) * blk]
                    if limit == 0:
                        tile = jnp.where(lag >= limits[0], tile, 0.0)
                    if limit == 1:
                        tile = jnp.where(lag < limits[1], tile, 0.0)
                    tile = tile.astype(bf16)
                    coda[pl.ds(pl.multiple_of(lag * blk, blk), blk), :] = tile
                    place = pl.multiple_of((lag // 2 + steps - 1) * blk, blk)
                    coda_t[pl.ds(place, blk), (b % 2) * blk : (b % 2 + 1) * blk] = tile.T

    def run(first_step, last_step, limit):
        def body(step, _):
            part(step, limit)
            return 0

        lax.fori_loop(first_step, last_step, body, 0)

    count = CODA // (2 * STEP)
    run(0, count // 4, 0)
    run(count // 4, 3 * count // 4, None)
    run(3 * count // 4, count, 1)

    def accumulate(group, blocks):
        lhs, rhs = [], []
        for q in range(GROUP):
            pair = group * GROUP + q
            row = (pair + steps - blocks) * blk
            lhs.append(coda_t[pl.ds(pl.multiple_of(row, blk), blocks * blk), :])
            top = (2 * pair + win * share) * blk
            rhs.append(
                jnp.concatenate(
                    [coda[pl.ds(pl.multiple_of(top + b * blk, blk), 2 * blk), :] for b in range(2)], axis=1
                )
            )
        value = jnp.dot(
            jnp.concatenate(lhs, axis=1), jnp.concatenate(rhs, axis=0), preferred_element_type=f32
        )
        acc[(steps - blocks) * blk :, :] += value

    peeled = steps // GROUP - 1
    for group in range(peeled):
        accumulate(group, (group + 1) * GROUP)
    groups = pairs // GROUP - win * (share // (2 * GROUP))

    def whole(group, _):
        accumulate(group, steps)
        return 0

    lax.fori_loop(peeled, groups, whole, 0)
    for i in range(steps):
        for b in range(2):
            lag = 2 * (steps - 1 - i) + b
            rows[pl.ds(lag, blk, stride=share + ROW_PAD), :] = (
                acc[i * blk : (i + 1) * blk, b * blk : (b + 1) * blk] * scale_three
            )
    out_ref[...] = rows[...].reshape(blk, share + ROW_PAD, blk)[:, :share].astype(bf16)


def coda_limit(windows, blk, used):
    return (21 << 20) + 2 * STEP * blk * windows * used


def coda_coherence(start, end, first, aux, own, share):
    windows = len(own)
    blk, length = own[0].shape
    used = length - CODA_LO
    steps = share // 2
    return pl.pallas_call(
        functools.partial(coda_kernel, windows),
        out_shape=jax.ShapeDtypeStruct((blk, share, blk), bf16),
        in_specs=[VMEM_SPEC] * (3 + 2 * windows),
        out_specs=VMEM_SPEC,
        scratch_shapes=[
            pltpu.VMEM((STEP * blk, windows * used), bf16),
            pltpu.VMEM((windows, length + CODA, blk), bf16),
            pltpu.VMEM((2, blk, blk), jnp.int32),
            pltpu.VMEM(((CODA + 1) * blk, blk), bf16),
            pltpu.VMEM(((CODA // 2 + steps - 1) * blk, 2 * blk), bf16),
            pltpu.VMEM((steps * blk, 2 * blk), f32),
            pltpu.VMEM(((share + ROW_PAD) * blk, blk), f32),
        ],
        compiler_params=pltpu.CompilerParams(vmem_limit_bytes=coda_limit(windows, blk, used)),
        name="coda_coherence",
    )(start, end, first, *aux, *own)


def transpose_partners(partner_ref, partner_t):
    rounds, blk, length = partner_ref.shape
    for r in range(rounds):
        partner_t[:length, r * blk : (r + 1) * blk] = partner_ref[r].T
    partner_t[length:, :] = jnp.zeros((partner_t.shape[0] - length, rounds * blk), bf16)


def pair_first_kernel(shifted_ref, partner_ref, out_ref, partner_t):
    length = partner_ref.shape[2]
    steps = pl.num_programs(0)
    step = pl.program_id(0)

    @pl.when(step == 0)
    def _():
        transpose_partners(partner_ref, partner_t)

    top = pl.multiple_of((lax.axis_index("win") * steps + step) * STEP, STEP)
    out_ref[0] = jnp.dot(shifted_ref[...], partner_t[pl.ds(top, length), :], preferred_element_type=f32)


def pair_first(shifted, partner, share):
    rounds, blk, length = partner.shape
    steps = share // STEP
    return pl.pallas_call(
        pair_first_kernel,
        out_shape=jax.ShapeDtypeStruct((steps, blk * STEP, rounds * blk), f32),
        grid=(steps,),
        in_specs=[VMEM_SPEC, VMEM_SPEC],
        out_specs=pl.BlockSpec((1, blk * STEP, rounds * blk), lambda step: (step, 0, 0)),
        scratch_shapes=[pltpu.VMEM((length + LAGS, rounds * blk), bf16)],
        compiler_params=pltpu.CompilerParams(vmem_limit_bytes=12 << 20),
        cost_estimate=pl.CostEstimate(
            flops=2 * share * rounds * blk * blk * length,
            transcendentals=0,
            bytes_accessed=4 * share * rounds * blk * blk,
        ),
        name="pair_first",
    )(shifted, partner)


def pair_kernel(windows, first_ref, *refs):
    shifted, partner_ref = refs[:windows], refs[windows : 2 * windows]
    out_ref, partner_t = refs[2 * windows :]
    rounds, blk, length = partner_ref[0].shape
    scale_two = 1.0 / math.sqrt((windows + 1) * length)
    steps = pl.num_programs(0)
    step = pl.program_id(0)

    @pl.when(step == 0)
    def _():
        for w in range(windows):
            transpose_partners(partner_ref[w], partner_t.at[w])

    top = pl.multiple_of((lax.axis_index("win") * steps + step) * STEP, STEP)
    weights = jnp.concatenate([partner_t[w, pl.ds(top, length), :] for w in range(windows)], axis=0)
    half = blk // 2
    for part in range(2):
        rows = slice(part * half * STEP, (part + 1) * half * STEP)
        samples = jnp.concatenate([shifted[w][rows, :] for w in range(windows)], axis=1)
        result = jnp.dot(samples, weights, preferred_element_type=f32)
        result = ((result + first_ref[0, rows, :]) * scale_two).astype(bf16)
        for r in range(rounds):
            out_ref[r, part * half : (part + 1) * half] = result[:, r * blk : (r + 1) * blk].reshape(
                half, STEP, blk
            )


def pair_coherence(first, shifted, partner, share):
    windows = len(shifted)
    rounds, blk, length = partner[0].shape
    steps = share // STEP
    return pl.pallas_call(
        functools.partial(pair_kernel, windows),
        out_shape=jax.ShapeDtypeStruct((rounds, blk, share, blk), bf16),
        grid=(steps,),
        in_specs=[pl.BlockSpec((1,) + first.shape[1:], lambda step: (step, 0, 0))]
        + [VMEM_SPEC] * (2 * windows),
        out_specs=pl.BlockSpec((rounds, blk, STEP, blk), lambda step: (0, 0, step, 0)),
        scratch_shapes=[pltpu.VMEM((windows, length + LAGS, rounds * blk), bf16)],
        compiler_params=pltpu.CompilerParams(vmem_limit_bytes=20 << 20),
        name="pair_coherence",
    )(first, *shifted, *partner)


def per_device(traces, pairing, aux_owners, coda_start, coda_end):
    win_size = lax.axis_size("win")
    chan_size = lax.axis_size("chan")
    rounds = pairing.shape[0]
    raw = traces[0]

    def exchange(block, k):
        return lax.ppermute(block, "win", [(i, i ^ k) for i in range(win_size)])

    def cross(block):
        return lax.ppermute(block, "chan", [(i, i ^ 1) for i in range(chan_size)])

    column = [raw] + [
        lax.ppermute(raw, "chan", [(i, (i + 2 * k) % chan_size) for i in range(chan_size)])
        for k in range(1, chan_size // 2)
    ]
    own_all = [raw] + [exchange(raw, k) for k in range(1, win_size)]
    shifted = [shifted_copies(block, n == 0) for n, block in enumerate(own_all)]
    column[0] = shifted[0][2]
    copies, own_white = [pair[0] for pair in shifted], [pair[1] for pair in shifted]
    copies, own_white, column = lax.optimization_barrier((copies, own_white, column))
    aux_sent, aux_held, sent, held = pick(aux_owners, pairing, column)
    aux = merge(lambda ref, chan: [ref[0]], aux_owners, aux_held, cross(aux_sent))
    partners = merge(
        lambda ref, chan: [ref[r, chan] for r in range(rounds)], pairing, held, cross(sent)
    )
    aux_rest = [exchange(aux, k) for k in range(1, win_size)]
    pair_begun = pair_first(copies[0], partners, LAGS // win_size)
    part_begun = part_first(aux, own_white[0])
    partners, aux_rest, pair_begun, part_begun = lax.optimization_barrier(
        (partners, aux_rest, pair_begun, part_begun)
    )
    partner_rest = [exchange(partners, k) for k in range(1, win_size)]
    three = coda_coherence(coda_start, coda_end, part_begun, aux_rest, own_white[1:], LAGS3 // win_size)
    pair = pair_coherence(pair_begun, copies[1:], partner_rest, LAGS // win_size)
    return (pair, three)


def solution(mesh):
    in_specs = (P("win", "chan", None), P(), P(), P(), P())
    out_specs = (P(None, "chan", "win", None), P("chan", "win", None))
    return jax.shard_map(per_device, mesh=mesh, in_specs=in_specs, out_specs=out_specs, check_vma=False)
```

time: 94 us -> 87 us (0.926)
  Pallas kernels: 61.4 us -> 57.6 us
  waiting for transfers between devices: 15 us -> 12.2 us
    pallas_call x1, Pallas kernels: 33.7 us -> 30.9 us  [coda_coherence(): pl.pallas_call(functools.partial(coda_kernel, windows), out_shape=jax.Sha...]
    ppermute x3, waiting for transfers between devices: 10.7 us -> 8.76 us  [per_device(): lax.ppermute(raw, 'chan', [(i, (i + 2 * k) % chan_size) for i in range(ch...]
    ppermute x9, waiting for transfers between devices: 4.26 us -> 2.52 us  [exchange(): return lax.ppermute(block, 'win', [(i, i ^ k) for i in range(win_size)])]
    pallas_call x8 -> x7, Pallas kernels: 6.85 us -> 5.84 us  [the longest x4 3.91 us: shifted_copies(): pl.pallas_call(shift_kernel, out_shape=[jax.ShapeDtypeStruct((blk * STEP,...]
    dynamic_slice x1 -> x0, local copies, waits for them, and re-layouts: 0.97 us -> none  [per_device(): lax.dynamic_index_in_dim(pairing, chan_index ^ 1, 1, keepdims=False)]
  transfers between devices with their start and end apart: 14 -> 14, of which waited for: 5 -> 6; matrix products, arithmetic and copies ran while one was open for 0% -> 0% of each run, Pallas kernels for 50% -> 52%
where the time goes in v4:
time: 87 us; the launch traced here: 86.9 us
  Pallas kernels  57.6 us (66%)
  starting transfers between devices  13.9 us (16%)
  waiting for transfers between devices  12.2 us (14%)
  local copies, waits for them, and re-layouts  1.66 us (2%)
  between operations  1.44 us (2%)
    pallas_call x1, Pallas kernels, coda_coherence(): pl.pallas_call(functools.partial(coda_kernel, windows), out_shape=jax.Sha...  30.9 us
    pallas_call x1, Pallas kernels, pair_coherence(): pl.pallas_call(functools.partial(pair_kernel, windows), out_shape=jax.Sha...  11.8 us
    ppermute x9, starting transfers between devices, exchange(): return lax.ppermute(block, 'win', [(i, i ^ k) for i in range(win_size)])  10.7 us
    ppermute x3, waiting for transfers between devices, per_device(): lax.ppermute(raw, 'chan', [(i, (i + 2 * k) % chan_size) for i in range(ch...  8.76 us
    pallas_call x1, Pallas kernels, part_first(): pl.pallas_call(part_first_kernel, out_shape=jax.ShapeDtypeStruct((steps,...  4.82 us
    pallas_call x1, Pallas kernels, pair_first(): pl.pallas_call(pair_first_kernel, out_shape=jax.ShapeDtypeStruct((steps,...  4.19 us
    pallas_call x4, Pallas kernels, shifted_copies(): pl.pallas_call(shift_kernel, out_shape=[jax.ShapeDtypeStruct((blk * STEP,...  3.91 us
    ppermute x3, starting transfers between devices, per_device(): lax.ppermute(raw, 'chan', [(i, (i + 2 * k) % chan_size) for i in range(ch...  2.7 us
  transfers between devices with their start and end apart: 14, of which 6 were waited for; matrix products, arithmetic and copies ran while one was open for 0% of the time, Pallas kernels for 52%

profile of v4, /device:TPU:8, one launch (start us, length us, event | category | flops | bytes accessed | tf_op | source)
XLA Modules:
  0.0 86.9 jit_solution(7822132087569526715)
XLA Ops:
  0.6 1.6 %collective-permute-start = (bf16[128,768]{1,0:T(8,128)(2,1)}, bf16[128,768]{1,0:T(8,128)(2,1)S(1)}, u32[]{:S(2)}, u32[]{:S(2)}) collective-permute-start(bf16[128,768]{1,0:T(8,128)(2,1)} %bitcast.1), channel_id=1, source_target_pairs={{0,1},{1,0},{2,3},{3,2},{4,5},{5,4},{6,7},{7,6},{8,9},{9,8},{10,11... | collective-permute-start | bytes 589832 | tf_op jit(solution)/shard_map/ppermute | solution.py:384
  2.2 1.5 %collective-permute-start.1 = (bf16[128,768]{1,0:T(8,128)(2,1)}, bf16[128,768]{1,0:T(8,128)(2,1)S(1)}, u32[]{:S(2)}, u32[]{:S(2)}) collective-permute-start(bf16[128,768]{1,0:T(8,128)(2,1)} %bitcast.2), channel_id=1, source_target_pairs={{0,2},{1,3},{2,0},{3,1},{4,6},{5,7},{6,4},{7,5},{8,10},{9,11},{10,... | collective-permute-start | bytes 589832 | tf_op jit(solution)/shard_map/ppermute | solution.py:384
  4.2 1.6 %collective-permute-start.3 = (bf16[128,768]{1,0:T(8,128)(2,1)}, bf16[128,768]{1,0:T(8,128)(2,1)S(1)}, u32[]{:S(2)}, u32[]{:S(2)}) collective-permute-start(bf16[128,768]{1,0:T(8,128)(2,1)} %bitcast.4), channel_id=1, source_target_pairs={{0,8},{4,12},{8,16},{12,20},{16,24},{20,28},{24,0},{28,4},{1,9},{5... | collective-permute-start | bytes 589832 | tf_op jit(solution)/shard_map/ppermute | solution.py:390
  5.8 1.0 %collective-permute-start.4 = (bf16[128,768]{1,0:T(8,128)(2,1)}, bf16[128,768]{1,0:T(8,128)(2,1)S(1)}, u32[]{:S(2)}, u32[]{:S(2)}) collective-permute-start(bf16[128,768]{1,0:T(8,128)(2,1)} %bitcast.5), channel_id=1, source_target_pairs={{0,16},{4,20},{8,24},{12,28},{16,0},{20,4},{24,8},{28,12},{1,17},{... | collective-permute-start | bytes 589832 | tf_op jit(solution)/shard_map/ppermute | solution.py:390
  6.8 1.9 %collective-permute-done.block_ref = bf16[128,768]{1,0:T(8,128)(2,1)S(1)} collective-permute-done((bf16[128,768]{1,0:T(8,128)(2,1)}, bf16[128,768]{1,0:T(8,128)(2,1)S(1)}, u32[]{:S(2)}, u32[]{:S(2)}) %collective-permute-start) | collective-permute-done | bytes 196640 | tf_op jit(solution)/shard_map/ppermute | solution.py:384
  8.8 1.0 %copy-done = bf16[1,128,768]{2,1,0:T(8,128)(2,1)S(1)} copy-done((bf16[1,128,768]{2,1,0:T(8,128)(2,1)S(1)}, bf16[1,128,768]{2,1,0:T(8,128)(2,1)}, u32[]{:S(2)}) %copy-start) | copy-done | bytes 196632
  9.8 1.0 %shifted_copies.4 = (bf16[2048,768]{1,0:T(8,128)(2,1)S(1)}, bf16[128,768]{1,0:T(8,128)(2,1)S(1)}, bf16[128,768]{1,0:T(8,128)(2,1)S(1)}) custom-call(bf16[128,768]{1,0:T(8,128)(2,1)S(1)} %bitcast.7), custom_call_target="tpu_custom_call" | custom-call | tf_op jit(solution)/shard_map/shifted_copies/pallas_call | solution.py:113
  11.4 1.0 %shifted_copies.5 = (bf16[2048,768]{1,0:T(8,128)(2,1)S(1)}, bf16[128,768]{1,0:T(8,128)(2,1)S(1)}) custom-call(bf16[128,768]{1,0:T(8,128)(2,1)S(1)} %collective-permute-done.block_ref), custom_call_target="tpu_custom_call" | custom-call | tf_op jit(solution)/shard_map/shifted_copies/pallas_call | solution.py:113
  13.0 1.0 %shifted_copies.6 = (bf16[2048,768]{1,0:T(8,128)(2,1)S(1)}, bf16[128,768]{1,0:T(8,128)(2,1)S(1)}) custom-call(bf16[128,768]{1,0:T(8,128)(2,1)S(1)} %collective-permute-done.1.block_ref), custom_call_target="tpu_custom_call" | custom-call | tf_op jit(solution)/shard_map/shifted_copies/pallas_call | solution.py:113
  14.0 1.0 %shifted_copies.7 = (bf16[2048,768]{1,0:T(8,128)(2,1)S(1)}, bf16[128,768]{1,0:T(8,128)(2,1)S(1)}) custom-call(bf16[128,768]{1,0:T(8,128)(2,1)S(1)} %collective-permute-done.2.block_ref), custom_call_target="tpu_custom_call" | custom-call | tf_op jit(solution)/shard_map/shifted_copies/pallas_call | solution.py:113
  15.0 4.9 %collective-permute-done.3.refs_1_ = bf16[128,768]{1,0:T(8,128)(2,1)S(1)} collective-permute-done((bf16[128,768]{1,0:T(8,128)(2,1)}, bf16[128,768]{1,0:T(8,128)(2,1)S(1)}, u32[]{:S(2)}, u32[]{:S(2)}) %collective-permute-start.3) | collective-permute-done | bytes 196640 | tf_op jit(solution)/shard_map/ppermute | solution.py:390
  19.9 2.2 %collective-permute-done.4.refs_2_ = bf16[128,768]{1,0:T(8,128)(2,1)S(1)} collective-permute-done((bf16[128,768]{1,0:T(8,128)(2,1)}, bf16[128,768]{1,0:T(8,128)(2,1)S(1)}, u32[]{:S(2)}, u32[]{:S(2)}) %collective-permute-start.4) | collective-permute-done | bytes 196640 | tf_op jit(solution)/shard_map/ppermute | solution.py:390
  22.0 1.7 %collective-permute-done.5.refs_3_ = bf16[128,768]{1,0:T(8,128)(2,1)S(1)} collective-permute-done((bf16[128,768]{1,0:T(8,128)(2,1)}, bf16[128,768]{1,0:T(8,128)(2,1)S(1)}, u32[]{:S(2)}, u32[]{:S(2)}) %collective-permute-start.5) | collective-permute-done | bytes 196640 | tf_op jit(solution)/shard_map/ppermute | solution.py:390
  23.7 0.7 copy-done.1
  24.4 0.8 pick.1
  25.8 0.9 %collective-permute-done.7.got_ref = bf16[128,768]{1,0:T(8,128)(2,1)S(1)} collective-permute-done((bf16[128,768]{1,0:T(8,128)(2,1)S(1)}, bf16[128,768]{1,0:T(8,128)(2,1)S(1)}, u32[]{:S(2)}, u32[]{:S(2)}) %collective-permute-start.7) | collective-permute-done | bytes 196640 | tf_op jit(solution)/shard_map/ppermute | solution.py:387
  26.8 2.5 %collective-permute-start.10 = (bf16[128,768]{1,0:T(8,128)(2,1)S(1)}, bf16[128,768]{1,0:T(8,128)(2,1)S(1)}, u32[]{:S(2)}, u32[]{:S(2)}) collective-permute-start(bf16[128,768]{1,0:T(8,128)(2,1)S(1)} %merge.3.aux_ref), channel_id=1, source_target_pairs={{0,3},{1,2},{2,1},{3,0},{4,7},{5,6},{6,5},{7,4},{8,11},{9,10},{10,... | collective-permute-start | bytes 589832 | tf_op jit(solution)/shard_map/ppermute | solution.py:384
  30.4 4.8 %part_first.1.first = f32[4,2048,256]{2,1,0:T(8,128)S(1)} custom-call(bf16[128,768]{1,0:T(8,128)(2,1)S(1)} %merge.3.aux_ref, bf16[128,768]{1,0:T(8,128)(2,1)S(1)} %get-tuple-element.51.own_ref), custom_call_target="tpu_custom_call" | custom-call | flops 2684354560 | bytes 8388608 | tf_op jit(solution)/shard_map/part_first/pallas_call | solution.py:150
  35.2 1.0 %merge.2.partner_ref = bf16[2,128,768]{2,1,0:T(8,128)(2,1)S(1)} custom-call(s32[2,8]{1,0:T(2,128)S(1)} %copy-done.2, bf16[2,128,768]{2,1,0:T(8,128)(2,1)S(1)} %get-tuple-element.46.held_ref, bf16[2,128,768]{2,1,0:T(8,128)(2,1)S(1)} %collective-permute-done.6.got_ref), custom_call_target="tpu_custom_call" | custom-call | tf_op jit(solution)/shard_map/merge/pallas_call | solution.py:88
  36.3 4.2 %pair_first.1.first_ref = f32[4,2048,256]{2,1,0:T(8,128)S(1)} custom-call(bf16[2048,768]{1,0:T(8,128)(2,1)S(1)} %get-tuple-element.50.shifted_ref, bf16[2,128,768]{2,1,0:T(8,128)(2,1)S(1)} %merge.2.partner_ref), custom_call_target="tpu_custom_call" | custom-call | flops 3221225472 | bytes 8388608 | tf_op jit(solution)/shard_map/pair_first/pallas_call | solution.py:316
  40.5 1.6 %collective-permute-start.11 = (bf16[2,128,768]{2,1,0:T(8,128)(2,1)S(1)}, bf16[2,128,768]{2,1,0:T(8,128)(2,1)S(1)}, u32[]{:S(2)}, u32[]{:S(2)}) collective-permute-start(bf16[2,128,768]{2,1,0:T(8,128)(2,1)S(1)} %merge.2.partner_ref), channel_id=1, source_target_pairs={{0,1},{1,0},{2,3},{3,2},{4,5},{5,4},{6,7},{7,6},{8,9},{9,8},{10,11... | collective-permute-start | bytes 1179656 | tf_op jit(solution)/shard_map/ppermute | solution.py:384
  42.1 1.5 %collective-permute-start.12 = (bf16[2,128,768]{2,1,0:T(8,128)(2,1)S(1)}, bf16[2,128,768]{2,1,0:T(8,128)(2,1)S(1)}, u32[]{:S(2)}, u32[]{:S(2)}) collective-permute-start(bf16[2,128,768]{2,1,0:T(8,128)(2,1)S(1)} %merge.2.partner_ref), channel_id=1, source_target_pairs={{0,2},{1,3},{2,0},{3,1},{4,6},{5,7},{6,4},{7,5},{8,10},{9,11},{10,... | collective-permute-start | bytes 1179656 | tf_op jit(solution)/shard_map/ppermute | solution.py:384
  44.1 30.9 %coda_coherence.1 = bf16[128,32,128]{2,1,0:T(8,128)(2,1)} custom-call(s32[1,128]{1,0:T(1,128)S(1)} %copy-done.3, s32[1,128]{1,0:T(1,128)S(1)} %copy-done.4, f32[4,2048,256]{2,1,0:T(8,128)S(1)} %part_first.1.first, bf16[128,768]{1,0:T(8,128)(2,1)S(1)} %collective-permute-done.8.refs_0_, bf16[128,768]{1,0:T(8,128)(2,1)S(1)} %collective-permute-done.9.refs_1_, ...), custom_call_target="tpu_custom_call" | custom-call | tf_op jit(solution)/shard_map/coda_coherence/pallas_call | solution.py:274
  75.0 11.8 %pair_coherence.1 = bf16[2,128,64,128]{3,2,1,0:T(8,128)(2,1)} custom-call(f32[4,2048,256]{2,1,0:T(8,128)S(1)} %pair_first.1.first_ref, bf16[2048,768]{1,0:T(8,128)(2,1)S(1)} %get-tuple-element.53.refs_0_, bf16[2048,768]{1,0:T(8,128)(2,1)S(1)} %get-tuple-element.54.refs_1_, bf16[2048,768]{1,0:T(8,128)(2,1)S(1)} %get-tuple-element.55.refs_2_, ...), custom_call_target="tpu_custom_call" | custom-call | tf_op jit(solution)/shard_map/pair_coherence/pallas_call | solution.py:364
  (25 shorter events, 3.4 us)
Async XLA Ops:
  0.6 8.1 %collective-permute-start = (bf16[128,768]{1,0:T(8,128)(2,1)}, bf16[128,768]{1,0:T(8,128)(2,1)S(1)}, u32[]{:S(2)}, u32[]{:S(2)}) collective-permute-start(bf16[128,768]{1,0:T(8,128)(2,1)} %bitcast.1), channel_id=1, source_target_pairs={{0,1},{1,0},{2,3},{3,2},{4,5},{5,4},{6,7},{7,6},{8,9},{9,8},{10,11... | collective-permute-start | bytes 589832 | tf_op jit(solution)/shard_map/ppermute | solution.py:384
  2.2 10.8 %collective-permute-start.1 = (bf16[128,768]{1,0:T(8,128)(2,1)}, bf16[128,768]{1,0:T(8,128)(2,1)S(1)}, u32[]{:S(2)}, u32[]{:S(2)}) collective-permute-start(bf16[128,768]{1,0:T(8,128)(2,1)} %bitcast.2), channel_id=1, source_target_pairs={{0,2},{1,3},{2,0},{3,1},{4,6},{5,7},{6,4},{7,5},{8,10},{9,11},{10,... | collective-permute-start | bytes 589832 | tf_op jit(solution)/shard_map/ppermute | solution.py:384
  3.7 10.3 %collective-permute-start.2 = (bf16[128,768]{1,0:T(8,128)(2,1)}, bf16[128,768]{1,0:T(8,128)(2,1)S(1)}, u32[]{:S(2)}, u32[]{:S(2)}) collective-permute-start(bf16[128,768]{1,0:T(8,128)(2,1)} %bitcast.3), channel_id=1, source_target_pairs={{0,3},{1,2},{2,1},{3,0},{4,7},{5,6},{6,5},{7,4},{8,11},{9,10},{10,... | collective-permute-start | bytes 589832 | tf_op jit(solution)/shard_map/ppermute | solution.py:384
  4.2 15.7 %collective-permute-start.3 = (bf16[128,768]{1,0:T(8,128)(2,1)}, bf16[128,768]{1,0:T(8,128)(2,1)S(1)}, u32[]{:S(2)}, u32[]{:S(2)}) collective-permute-start(bf16[128,768]{1,0:T(8,128)(2,1)} %bitcast.4), channel_id=1, source_target_pairs={{0,8},{4,12},{8,16},{12,20},{16,24},{20,28},{24,0},{28,4},{1,9},{5... | collective-permute-start | bytes 589832 | tf_op jit(solution)/shard_map/ppermute | solution.py:390
  5.8 16.3 %collective-permute-start.4 = (bf16[128,768]{1,0:T(8,128)(2,1)}, bf16[128,768]{1,0:T(8,128)(2,1)S(1)}, u32[]{:S(2)}, u32[]{:S(2)}) collective-permute-start(bf16[128,768]{1,0:T(8,128)(2,1)} %bitcast.5), channel_id=1, source_target_pairs={{0,16},{4,20},{8,24},{12,28},{16,0},{20,4},{24,8},{28,12},{1,17},{... | collective-permute-start | bytes 589832 | tf_op jit(solution)/shard_map/ppermute | solution.py:390
  8.7 15.0 %collective-permute-start.5 = (bf16[128,768]{1,0:T(8,128)(2,1)}, bf16[128,768]{1,0:T(8,128)(2,1)S(1)}, u32[]{:S(2)}, u32[]{:S(2)}) collective-permute-start(bf16[128,768]{1,0:T(8,128)(2,1)} %bitcast.6), channel_id=1, source_target_pairs={{0,24},{4,28},{8,0},{12,4},{16,8},{20,12},{24,16},{28,20},{1,25},{... | collective-permute-start | bytes 589832 | tf_op jit(solution)/shard_map/ppermute | solution.py:390
  8.8 1.0 %copy-start = (bf16[1,128,768]{2,1,0:T(8,128)(2,1)S(1)}, bf16[1,128,768]{2,1,0:T(8,128)(2,1)}, u32[]{:S(2)}) copy-start(bf16[1,128,768]{2,1,0:T(8,128)(2,1)} %param.5) | copy-start | bytes 589828
  23.7 0.7 copy-start.1
  25.2 1.5 %collective-permute-start.7 = (bf16[128,768]{1,0:T(8,128)(2,1)S(1)}, bf16[128,768]{1,0:T(8,128)(2,1)S(1)}, u32[]{:S(2)}, u32[]{:S(2)}) collective-permute-start(bf16[128,768]{1,0:T(8,128)(2,1)S(1)} %get-tuple-element.49), channel_id=1, source_target_pairs={{0,4},{4,0},{8,12},{12,8},{16,20},{20,16},{24,28},{28,24},{1,5},{5... | collective-permute-start | bytes 589832 | tf_op jit(solution)/shard_map/ppermute | solution.py:387
  25.3 10.0 %collective-permute-start.6 = (bf16[2,128,768]{2,1,0:T(8,128)(2,1)S(1)}, bf16[2,128,768]{2,1,0:T(8,128)(2,1)S(1)}, u32[]{:S(2)}, u32[]{:S(2)}) collective-permute-start(bf16[2,128,768]{2,1,0:T(8,128)(2,1)S(1)} %get-tuple-element.47), channel_id=1, source_target_pairs={{0,4},{4,0},{8,12},{12,8},{16,20},{20,16},{24,28},{28,24},{1,5},{5... | collective-permute-start | bytes 1179656 | tf_op jit(solution)/shard_map/ppermute | solution.py:387
  26.8 8.4 %copy-start.2 = (s32[2,8]{1,0:T(2,128)S(1)}, s32[2,8]{1,0:T(2,128)}, u32[]{:S(2)}) copy-start(s32[2,8]{1,0:T(2,128)} %scalars_ref.2) | copy-start | bytes 196
  26.8 13.6 %collective-permute-start.10 = (bf16[128,768]{1,0:T(8,128)(2,1)S(1)}, bf16[128,768]{1,0:T(8,128)(2,1)S(1)}, u32[]{:S(2)}, u32[]{:S(2)}) collective-permute-start(bf16[128,768]{1,0:T(8,128)(2,1)S(1)} %merge.3.aux_ref), channel_id=1, source_target_pairs={{0,3},{1,2},{2,1},{3,0},{4,7},{5,6},{6,5},{7,4},{8,11},{9,10},{10,... | collective-permute-start | bytes 589832 | tf_op jit(solution)/shard_map/ppermute | solution.py:384
  29.4 11.1 %collective-permute-start.8 = (bf16[128,768]{1,0:T(8,128)(2,1)S(1)}, bf16[128,768]{1,0:T(8,128)(2,1)S(1)}, u32[]{:S(2)}, u32[]{:S(2)}) collective-permute-start(bf16[128,768]{1,0:T(8,128)(2,1)S(1)} %merge.3.aux_ref), channel_id=1, source_target_pairs={{0,1},{1,0},{2,3},{3,2},{4,5},{5,4},{6,7},{7,6},{8,9},{9,8},{10,11... | collective-permute-start | bytes 589832 | tf_op jit(solution)/shard_map/ppermute | solution.py:384
  29.9 10.6 %collective-permute-start.9 = (bf16[128,768]{1,0:T(8,128)(2,1)S(1)}, bf16[128,768]{1,0:T(8,128)(2,1)S(1)}, u32[]{:S(2)}, u32[]{:S(2)}) collective-permute-start(bf16[128,768]{1,0:T(8,128)(2,1)S(1)} %merge.3.aux_ref), channel_id=1, source_target_pairs={{0,2},{1,3},{2,0},{3,1},{4,6},{5,7},{6,4},{7,5},{8,10},{9,11},{10,... | collective-permute-start | bytes 589832 | tf_op jit(solution)/shard_map/ppermute | solution.py:384
  36.3 7.8 %copy-start.3 = (s32[1,128]{1,0:T(1,128)S(1)}, s32[1,128]{1,0:T(1,128)}, u32[]{:S(2)}) copy-start(s32[1,128]{1,0:T(1,128)} %start_ref.1) | copy-start | bytes 1540
  36.3 7.8 %copy-start.4 = (s32[1,128]{1,0:T(1,128)S(1)}, s32[1,128]{1,0:T(1,128)}, u32[]{:S(2)}) copy-start(s32[1,128]{1,0:T(1,128)} %end_ref.1) | copy-start | bytes 1540
  40.5 34.5 %collective-permute-start.11 = (bf16[2,128,768]{2,1,0:T(8,128)(2,1)S(1)}, bf16[2,128,768]{2,1,0:T(8,128)(2,1)S(1)}, u32[]{:S(2)}, u32[]{:S(2)}) collective-permute-start(bf16[2,128,768]{2,1,0:T(8,128)(2,1)S(1)} %merge.2.partner_ref), channel_id=1, source_target_pairs={{0,1},{1,0},{2,3},{3,2},{4,5},{5,4},{6,7},{7,6},{8,9},{9,8},{10,11... | collective-permute-start | bytes 1179656 | tf_op jit(solution)/shard_map/ppermute | solution.py:384
  42.1 32.9 %collective-permute-start.12 = (bf16[2,128,768]{2,1,0:T(8,128)(2,1)S(1)}, bf16[2,128,768]{2,1,0:T(8,128)(2,1)S(1)}, u32[]{:S(2)}, u32[]{:S(2)}) collective-permute-start(bf16[2,128,768]{2,1,0:T(8,128)(2,1)S(1)} %merge.2.partner_ref), channel_id=1, source_target_pairs={{0,2},{1,3},{2,0},{3,1},{4,6},{5,7},{6,4},{7,5},{8,10},{9,11},{10,... | collective-permute-start | bytes 1179656 | tf_op jit(solution)/shard_map/ppermute | solution.py:384
  43.6 31.4 %collective-permute-start.13 = (bf16[2,128,768]{2,1,0:T(8,128)(2,1)S(1)}, bf16[2,128,768]{2,1,0:T(8,128)(2,1)S(1)}, u32[]{:S(2)}, u32[]{:S(2)}) collective-permute-start(bf16[2,128,768]{2,1,0:T(8,128)(2,1)S(1)} %merge.2.partner_ref), channel_id=1, source_target_pairs={{0,3},{1,2},{2,1},{3,0},{4,7},{5,6},{6,5},{7,4},{8,11},{9,10},{10,... | collective-permute-start | bytes 1179656 | tf_op jit(solution)/shard_map/ppermute | solution.py:384

commit v5 on v4

--- a/solution.py
+++ b/solution.py
@@ -18,7 +18,9 @@
 
 SMEM_SPEC = pl.BlockSpec(memory_space=pltpu.SMEM)
 VMEM_SPEC = pl.BlockSpec(memory_space=pltpu.VMEM)
+ANY_SPEC = pl.BlockSpec(memory_space=pl.ANY)
 ROW_PAD = 8
+MOVED = 8
 
 f32 = jnp.float32
 bf16 = jnp.bfloat16
@@ -164,7 +166,7 @@
 
 def coda_kernel(windows, start_ref, end_ref, first, *refs):
     aux_ref, own_ref = refs[:windows], refs[windows : 2 * windows]
-    out_ref, shifted, own_t, limits, coda, coda_t, acc, rows = refs[2 * windows :]
+    out_ref, moved_ref, shifted, own_t, limits, coda, coda_t, acc, rows = refs[2 * windows :]
     blk, length = own_ref[0].shape
     used = length - CODA_LO
     share = out_ref.shape[1]
@@ -184,7 +186,6 @@
             shifted[b * blk : (b + 1) * blk, w * used : (w + 1) * used] = shift_right(samples, b)
     coda[CODA * blk :, :] = jnp.zeros((coda.shape[0] - CODA * blk, blk), bf16)
     coda_t[: (steps - 1) * blk, :] = jnp.zeros(((steps - 1) * blk, 2 * blk), bf16)
-    acc[...] = jnp.zeros(acc.shape, f32)
 
     chunk = STEP // 2
 
@@ -226,13 +227,13 @@
     run(count // 4, 3 * count // 4, None)
     run(3 * count // 4, count, 1)
 
-    def accumulate(group, blocks):
+    def accumulate(group, size, blocks, lag_first, total):
         lhs, rhs = [], []
-        for q in range(GROUP):
-            pair = group * GROUP + q
+        for q in range(size):
+            pair = group * size + q
             row = (pair + steps - blocks) * blk
             lhs.append(coda_t[pl.ds(pl.multiple_of(row, blk), blocks * blk), :])
-            top = (2 * pair + win * share) * blk
+            top = (2 * pair + lag_first) * blk
             rhs.append(
                 jnp.concatenate(
                     [coda[pl.ds(pl.multiple_of(top + b * blk, blk), 2 * blk), :] for b in range(2)], axis=1
@@ -241,25 +242,75 @@
         value = jnp.dot(
             jnp.concatenate(lhs, axis=1), jnp.concatenate(rhs, axis=0), preferred_element_type=f32
         )
-        acc[(steps - blocks) * blk :, :] += value
-
-    peeled = steps // GROUP - 1
-    for group in range(peeled):
-        accumulate(group, (group + 1) * GROUP)
-    groups = pairs // GROUP - win * (share // (2 * GROUP))
-
-    def whole(group, _):
-        accumulate(group, steps)
-        return 0
-
-    lax.fori_loop(peeled, groups, whole, 0)
-    for i in range(steps):
-        for b in range(2):
-            lag = 2 * (steps - 1 - i) + b
-            rows[pl.ds(lag, blk, stride=share + ROW_PAD), :] = (
-                acc[i * blk : (i + 1) * blk, b * blk : (b + 1) * blk] * scale_three
-            )
-    out_ref[...] = rows[...].reshape(blk, share + ROW_PAD, blk)[:, :share].astype(bf16)
+        acc[(total - blocks) * blk : total * blk, :] += value
+
+    def correlate(lag_first, total, target_ref, size=GROUP):
+        acc[: total * blk, :] = jnp.zeros((total * blk, acc.shape[1]), f32)
+        peeled = total // size - 1
+        for group in range(peeled):
+            accumulate(group, size, (group + 1) * size, lag_first, total)
+
+        def whole(group, _):
+            accumulate(group, size, total, lag_first, total)
+            return 0
+
+        lax.fori_loop(max(peeled, 0), (pairs - lag_first // 2 + size - 1) // size, whole, 0)
+        stride = 2 * total + ROW_PAD
+        for i in range(total):
+            for b in range(2):
+                lag = 2 * (total - 1 - i) + b
+                rows[pl.ds(lag, blk, stride=stride), :] = (
+                    acc[i * blk : (i + 1) * blk, b * blk : (b + 1) * blk] * scale_three
+                )
+        target_ref[:, : 2 * total, :] = (
+            rows[: blk * stride].reshape(blk, stride, blk)[:, : 2 * total].astype(bf16)
+        )
+
+    last = lax.axis_size("win") - 1
+
+    @pl.when(win > 0)
+    def _():
+        correlate(win * share, steps, out_ref)
+
+    kept = share // 2
+
+    @pl.when(win == 0)
+    def _():
+        correlate(0, kept // 2, out_ref)
+
+    @pl.when(win > last - kept // MOVED)
+    def _():
+        correlate(kept + MOVED * (last - win), MOVED // 2, moved_ref, 2 * GROUP)
+
+
+def finish_kernel(count, *refs):
+    moved_refs, (_, out_ref, sems) = refs[:count], refs[count:]
+    kept = out_ref.shape[1] - MOVED * count
+
+    @pl.when(lax.axis_index("win") == 0)
+    def _():
+        copies = [
+            pltpu.make_async_copy(moved, out_ref.at[:, kept + MOVED * n : kept + MOVED * (n + 1), :], sems.at[n])
+            for n, moved in enumerate(moved_refs)
+        ]
+        for copy in copies:
+            copy.start()
+        for copy in copies:
+            copy.wait()
+
+
+def finish(moved, three):
+    count = len(moved)
+    return pl.pallas_call(
+        functools.partial(finish_kernel, count),
+        out_shape=jax.ShapeDtypeStruct(three.shape, bf16),
+        in_specs=[ANY_SPEC] * (count + 1),
+        out_specs=ANY_SPEC,
+        scratch_shapes=[pltpu.SemaphoreType.DMA((count,))],
+        input_output_aliases={count: 0},
+        compiler_params=pltpu.CompilerParams(vmem_limit_bytes=1 << 20),
+        name="finish",
+    )(*moved, three)
 
 
 def coda_limit(windows, blk, used):
@@ -273,19 +324,25 @@
     steps = share // 2
     return pl.pallas_call(
         functools.partial(coda_kernel, windows),
-        out_shape=jax.ShapeDtypeStruct((blk, share, blk), bf16),
+        out_shape=[
+            jax.ShapeDtypeStruct((blk, share, blk), bf16),
+            jax.ShapeDtypeStruct((blk, MOVED, blk), bf16),
+        ],
         in_specs=[VMEM_SPEC] * (3 + 2 * windows),
-        out_specs=VMEM_SPEC,
+        out_specs=[VMEM_SPEC] * 2,
         scratch_shapes=[
             pltpu.VMEM((STEP * blk, windows * used), bf16),
             pltpu.VMEM((windows, length + CODA, blk), bf16),
             pltpu.VMEM((2, blk, blk), jnp.int32),
-            pltpu.VMEM(((CODA + 1) * blk, blk), bf16),
+            pltpu.VMEM(((CODA + 4 * GROUP) * blk, blk), bf16),
             pltpu.VMEM(((CODA // 2 + steps - 1) * blk, 2 * blk), bf16),
             pltpu.VMEM((steps * blk, 2 * blk), f32),
             pltpu.VMEM(((share + ROW_PAD) * blk, blk), f32),
         ],
         compiler_params=pltpu.CompilerParams(vmem_limit_bytes=coda_limit(windows, blk, used)),
+        cost_estimate=pl.CostEstimate(
+            flops=2 * CODA * blk * blk * (windows * used + blk * share), transcendentals=0, bytes_accessed=16 << 20
+        ),
         name="coda_coherence",
     )(start, end, first, *aux, *own)
 
@@ -370,6 +427,9 @@
         out_specs=pl.BlockSpec((rounds, blk, STEP, blk), lambda step: (0, 0, step, 0)),
         scratch_shapes=[pltpu.VMEM((windows, length + LAGS, rounds * blk), bf16)],
         compiler_params=pltpu.CompilerParams(vmem_limit_bytes=20 << 20),
+        cost_estimate=pl.CostEstimate(
+            flops=2 * rounds * share * blk * blk * windows * length, transcendentals=0, bytes_accessed=16 << 20
+        ),
         name="pair_coherence",
     )(first, *shifted, *partner)
 
@@ -407,9 +467,12 @@
         (partners, aux_rest, pair_begun, part_begun)
     )
     partner_rest = [exchange(partners, k) for k in range(1, win_size)]
-    three = coda_coherence(coda_start, coda_end, part_begun, aux_rest, own_white[1:], LAGS3 // win_size)
+    three, moved = coda_coherence(coda_start, coda_end, part_begun, aux_rest, own_white[1:], LAGS3 // win_size)
     pair = pair_coherence(pair_begun, copies[1:], partner_rest, LAGS // win_size)
-    return (pair, three)
+    helpers = LAGS3 // win_size // 2 // MOVED
+    moved = [lax.ppermute(moved, "win", [(win_size - 1 - n, 0)]) for n in range(helpers)]
+    pair, three, moved = lax.optimization_barrier((pair, three, moved))
+    return (pair, finish(moved, three))
 
 
 def solution(mesh):

time: 87 us -> 84.7 us (0.974)
  Pallas kernels: 57.6 us -> 51.2 us
  starting transfers between devices: 13.9 us -> 16.5 us
    pallas_call x1 -> x2, Pallas kernels: 30.9 us -> 24.5 us  [the longest x1 23.7 us: coda_coherence(): pl.pallas_call(functools.partial(coda_kernel, windows), out_shape=[jax.Sh...]
    ppermute x0 -> x2, starting transfers between devices: none -> 2.57 us  [per_device(): lax.ppermute(moved, 'win', [(win_size - 1 - n, 0)])]
  transfers between devices with their start and end apart: 14 -> 16, of which waited for: 6 -> 7; matrix products, arithmetic and copies ran while one was open for 0% -> 0% of each run, Pallas kernels for 52% -> 59%
where the time goes in v5:
time: 84.7 us; the launch traced here: 83.8 us
  Pallas kernels  51.2 us (60%)
  starting transfers between devices  16.5 us (19%)
  waiting for transfers between devices  12.8 us (15%)
  local copies, waits for them, and re-layouts  1.66 us (2%)
  between operations  1.63 us (2%)
    pallas_call x1, Pallas kernels, coda_coherence(): pl.pallas_call(functools.partial(coda_kernel, windows), out_shape=[jax.Sh...  23.7 us
    pallas_call x1, Pallas kernels, pair_coherence(): pl.pallas_call(functools.partial(pair_kernel, windows), out_shape=jax.Sha...  11.8 us
    ppermute x9, starting transfers between devices, exchange(): return lax.ppermute(block, 'win', [(i, i ^ k) for i in range(win_size)])  10.7 us
    ppermute x3, waiting for transfers between devices, per_device(): lax.ppermute(raw, 'chan', [(i, (i + 2 * k) % chan_size) for i in range(ch...  8.76 us
    pallas_call x1, Pallas kernels, part_first(): pl.pallas_call(part_first_kernel, out_shape=jax.ShapeDtypeStruct((steps,...  4.82 us
    pallas_call x1, Pallas kernels, pair_first(): pl.pallas_call(pair_first_kernel, out_shape=jax.ShapeDtypeStruct((steps,...  4.19 us
    pallas_call x4, Pallas kernels, shifted_copies(): pl.pallas_call(shift_kernel, out_shape=[jax.ShapeDtypeStruct((blk * STEP,...  3.91 us
    ppermute x3, starting transfers between devices, per_device(): lax.ppermute(raw, 'chan', [(i, (i + 2 * k) % chan_size) for i in range(ch...  2.7 us
  transfers between devices with their start and end apart: 16, of which 7 were waited for; matrix products, arithmetic and copies ran while one was open for 0% of the time, Pallas kernels for 59%

profile of v5, /device:TPU:8, one launch (start us, length us, event | category | flops | bytes accessed | tf_op | source)
XLA Modules:
  0.0 83.8 jit_solution(8210801337363830383)
XLA Ops:
  0.6 1.6 %collective-permute-start = (bf16[128,768]{1,0:T(8,128)(2,1)}, bf16[128,768]{1,0:T(8,128)(2,1)S(1)}, u32[]{:S(2)}, u32[]{:S(2)}) collective-permute-start(bf16[128,768]{1,0:T(8,128)(2,1)} %bitcast.1), channel_id=1, source_target_pairs={{0,1},{1,0},{2,3},{3,2},{4,5},{5,4},{6,7},{7,6},{8,9},{9,8},{10,11... | collective-permute-start | bytes 589832 | tf_op jit(solution)/shard_map/ppermute | solution.py:444
  2.2 1.5 %collective-permute-start.1 = (bf16[128,768]{1,0:T(8,128)(2,1)}, bf16[128,768]{1,0:T(8,128)(2,1)S(1)}, u32[]{:S(2)}, u32[]{:S(2)}) collective-permute-start(bf16[128,768]{1,0:T(8,128)(2,1)} %bitcast.2), channel_id=1, source_target_pairs={{0,2},{1,3},{2,0},{3,1},{4,6},{5,7},{6,4},{7,5},{8,10},{9,11},{10,... | collective-permute-start | bytes 589832 | tf_op jit(solution)/shard_map/ppermute | solution.py:444
  4.2 1.6 %collective-permute-start.3 = (bf16[128,768]{1,0:T(8,128)(2,1)}, bf16[128,768]{1,0:T(8,128)(2,1)S(1)}, u32[]{:S(2)}, u32[]{:S(2)}) collective-permute-start(bf16[128,768]{1,0:T(8,128)(2,1)} %bitcast.4), channel_id=1, source_target_pairs={{0,8},{4,12},{8,16},{12,20},{16,24},{20,28},{24,0},{28,4},{1,9},{5... | collective-permute-start | bytes 589832 | tf_op jit(solution)/shard_map/ppermute | solution.py:450
  5.8 1.0 %collective-permute-start.4 = (bf16[128,768]{1,0:T(8,128)(2,1)}, bf16[128,768]{1,0:T(8,128)(2,1)S(1)}, u32[]{:S(2)}, u32[]{:S(2)}) collective-permute-start(bf16[128,768]{1,0:T(8,128)(2,1)} %bitcast.5), channel_id=1, source_target_pairs={{0,16},{4,20},{8,24},{12,28},{16,0},{20,4},{24,8},{28,12},{1,17},{... | collective-permute-start | bytes 589832 | tf_op jit(solution)/shard_map/ppermute | solution.py:450
  6.8 1.9 %collective-permute-done.block_ref = bf16[128,768]{1,0:T(8,128)(2,1)S(1)} collective-permute-done((bf16[128,768]{1,0:T(8,128)(2,1)}, bf16[128,768]{1,0:T(8,128)(2,1)S(1)}, u32[]{:S(2)}, u32[]{:S(2)}) %collective-permute-start) | collective-permute-done | bytes 196640 | tf_op jit(solution)/shard_map/ppermute | solution.py:444
  8.8 1.0 %copy-done = bf16[1,128,768]{2,1,0:T(8,128)(2,1)S(1)} copy-done((bf16[1,128,768]{2,1,0:T(8,128)(2,1)S(1)}, bf16[1,128,768]{2,1,0:T(8,128)(2,1)}, u32[]{:S(2)}) %copy-start) | copy-done | bytes 196632
  9.8 1.0 %shifted_copies.4 = (bf16[2048,768]{1,0:T(8,128)(2,1)S(1)}, bf16[128,768]{1,0:T(8,128)(2,1)S(1)}, bf16[128,768]{1,0:T(8,128)(2,1)S(1)}) custom-call(bf16[128,768]{1,0:T(8,128)(2,1)S(1)} %bitcast.7), custom_call_target="tpu_custom_call" | custom-call | tf_op jit(solution)/shard_map/shifted_copies/pallas_call | solution.py:115
  11.4 1.0 %shifted_copies.5 = (bf16[2048,768]{1,0:T(8,128)(2,1)S(1)}, bf16[128,768]{1,0:T(8,128)(2,1)S(1)}) custom-call(bf16[128,768]{1,0:T(8,128)(2,1)S(1)} %collective-permute-done.block_ref), custom_call_target="tpu_custom_call" | custom-call | tf_op jit(solution)/shard_map/shifted_copies/pallas_call | solution.py:115
  13.0 1.0 %shifted_copies.6 = (bf16[2048,768]{1,0:T(8,128)(2,1)S(1)}, bf16[128,768]{1,0:T(8,128)(2,1)S(1)}) custom-call(bf16[128,768]{1,0:T(8,128)(2,1)S(1)} %collective-permute-done.1.block_ref), custom_call_target="tpu_custom_call" | custom-call | tf_op jit(solution)/shard_map/shifted_copies/pallas_call | solution.py:115
  14.0 1.0 %shifted_copies.7 = (bf16[2048,768]{1,0:T(8,128)(2,1)S(1)}, bf16[128,768]{1,0:T(8,128)(2,1)S(1)}) custom-call(bf16[128,768]{1,0:T(8,128)(2,1)S(1)} %collective-permute-done.2.block_ref), custom_call_target="tpu_custom_call" | custom-call | tf_op jit(solution)/shard_map/shifted_copies/pallas_call | solution.py:115
  15.0 4.9 %collective-permute-done.3.refs_1_ = bf16[128,768]{1,0:T(8,128)(2,1)S(1)} collective-permute-done((bf16[128,768]{1,0:T(8,128)(2,1)}, bf16[128,768]{1,0:T(8,128)(2,1)S(1)}, u32[]{:S(2)}, u32[]{:S(2)}) %collective-permute-start.3) | collective-permute-done | bytes 196640 | tf_op jit(solution)/shard_map/ppermute | solution.py:450
  19.9 2.2 %collective-permute-done.4.refs_2_ = bf16[128,768]{1,0:T(8,128)(2,1)S(1)} collective-permute-done((bf16[128,768]{1,0:T(8,128)(2,1)}, bf16[128,768]{1,0:T(8,128)(2,1)S(1)}, u32[]{:S(2)}, u32[]{:S(2)}) %collective-permute-start.4) | collective-permute-done | bytes 196640 | tf_op jit(solution)/shard_map/ppermute | solution.py:450
  22.0 1.7 %collective-permute-done.5.refs_3_ = bf16[128,768]{1,0:T(8,128)(2,1)S(1)} collective-permute-done((bf16[128,768]{1,0:T(8,128)(2,1)}, bf16[128,768]{1,0:T(8,128)(2,1)S(1)}, u32[]{:S(2)}, u32[]{:S(2)}) %collective-permute-start.5) | collective-permute-done | bytes 196640 | tf_op jit(solution)/shard_map/ppermute | solution.py:450
  25.8 0.9 %collective-permute-done.7.got_ref = bf16[128,768]{1,0:T(8,128)(2,1)S(1)} collective-permute-done((bf16[128,768]{1,0:T(8,128)(2,1)S(1)}, bf16[128,768]{1,0:T(8,128)(2,1)S(1)}, u32[]{:S(2)}, u32[]{:S(2)}) %collective-permute-start.7) | collective-permute-done | bytes 196640 | tf_op jit(solution)/shard_map/ppermute | solution.py:447
  26.8 2.5 %collective-permute-start.10 = (bf16[128,768]{1,0:T(8,128)(2,1)S(1)}, bf16[128,768]{1,0:T(8,128)(2,1)S(1)}, u32[]{:S(2)}, u32[]{:S(2)}) collective-permute-start(bf16[128,768]{1,0:T(8,128)(2,1)S(1)} %merge.3.aux_ref), channel_id=1, source_target_pairs={{0,3},{1,2},{2,1},{3,0},{4,7},{5,6},{6,5},{7,4},{8,11},{9,10},{10,... | collective-permute-start | bytes 589832 | tf_op jit(solution)/shard_map/ppermute | solution.py:444
  30.4 4.8 %part_first.1.first = f32[4,2048,256]{2,1,0:T(8,128)S(1)} custom-call(bf16[128,768]{1,0:T(8,128)(2,1)S(1)} %merge.3.aux_ref, bf16[128,768]{1,0:T(8,128)(2,1)S(1)} %get-tuple-element.57.own_ref), custom_call_target="tpu_custom_call" | custom-call | flops 2684354560 | bytes 8388608 | tf_op jit(solution)/shard_map/part_first/pallas_call | solution.py:152
  35.2 1.0 %merge.2.partner_ref = bf16[2,128,768]{2,1,0:T(8,128)(2,1)S(1)} custom-call(s32[2,8]{1,0:T(2,128)S(1)} %copy-done.2, bf16[2,128,768]{2,1,0:T(8,128)(2,1)S(1)} %get-tuple-element.52.held_ref, bf16[2,128,768]{2,1,0:T(8,128)(2,1)S(1)} %collective-permute-done.6.got_ref), custom_call_target="tpu_custom_call" | custom-call | tf_op jit(solution)/shard_map/merge/pallas_call | solution.py:90
  36.3 4.2 %pair_first.1.first_ref = f32[4,2048,256]{2,1,0:T(8,128)S(1)} custom-call(bf16[2048,768]{1,0:T(8,128)(2,1)S(1)} %get-tuple-element.56.shifted_ref, bf16[2,128,768]{2,1,0:T(8,128)(2,1)S(1)} %merge.2.partner_ref), custom_call_target="tpu_custom_call" | custom-call | flops 3221225472 | bytes 8388608 | tf_op jit(solution)/shard_map/pair_first/pallas_call | solution.py:373
  40.5 1.6 %collective-permute-start.11 = (bf16[2,128,768]{2,1,0:T(8,128)(2,1)S(1)}, bf16[2,128,768]{2,1,0:T(8,128)(2,1)S(1)}, u32[]{:S(2)}, u32[]{:S(2)}) collective-permute-start(bf16[2,128,768]{2,1,0:T(8,128)(2,1)S(1)} %merge.2.partner_ref), channel_id=1, source_target_pairs={{0,1},{1,0},{2,3},{3,2},{4,5},{5,4},{6,7},{7,6},{8,9},{9,8},{10,11... | collective-permute-start | bytes 1179656 | tf_op jit(solution)/shard_map/ppermute | solution.py:444
  42.1 1.5 %collective-permute-start.12 = (bf16[2,128,768]{2,1,0:T(8,128)(2,1)S(1)}, bf16[2,128,768]{2,1,0:T(8,128)(2,1)S(1)}, u32[]{:S(2)}, u32[]{:S(2)}) collective-permute-start(bf16[2,128,768]{2,1,0:T(8,128)(2,1)S(1)} %merge.2.partner_ref), channel_id=1, source_target_pairs={{0,2},{1,3},{2,0},{3,1},{4,6},{5,7},{6,4},{7,5},{8,10},{9,11},{10,... | collective-permute-start | bytes 1179656 | tf_op jit(solution)/shard_map/ppermute | solution.py:444
  44.1 23.7 %coda_coherence.1 = (bf16[128,32,128]{2,1,0:T(8,128)(2,1)}, bf16[128,8,128]{2,1,0:T(8,128)(2,1)S(1)}) custom-call(s32[1,128]{1,0:T(1,128)S(1)} %copy-done.3, s32[1,128]{1,0:T(1,128)S(1)} %copy-done.4, f32[4,2048,256]{2,1,0:T(8,128)S(1)} %part_first.1.first, bf16[128,768]{1,0:T(8,128)(2,1)S(1)} %collective-permute-done.8.refs_0_, ...), custom_call_target="tpu_custom_call" | custom-call | flops 25232932864 | bytes 16777216 | tf_op jit(solution)/shard_map/coda_coherence/pallas_call | solution.py:325
  67.7 1.3 %collective-permute-start.14 = (bf16[128,8,128]{2,1,0:T(8,128)(2,1)S(1)}, bf16[128,8,128]{2,1,0:T(8,128)(2,1)S(1)}, u32[]{:S(2)}, u32[]{:S(2)}) collective-permute-start(bf16[128,8,128]{2,1,0:T(8,128)(2,1)S(1)} %get-tuple-element.71), channel_id=1, source_target_pairs={{3,0},{7,4},{11,8},{15,12},{19,16},{23,20},{27,24},{31,28}} | collective-permute-start | bytes 786440 | tf_op jit(solution)/shard_map/ppermute | solution.py:473
  69.0 1.3 %collective-permute-start.15 = (bf16[128,8,128]{2,1,0:T(8,128)(2,1)S(1)}, bf16[128,8,128]{2,1,0:T(8,128)(2,1)S(1)}, u32[]{:S(2)}, u32[]{:S(2)}) collective-permute-start(bf16[128,8,128]{2,1,0:T(8,128)(2,1)S(1)} %get-tuple-element.71), channel_id=1, source_target_pairs={{2,0},{6,4},{10,8},{14,12},{18,16},{22,20},{26,24},{30,28}} | collective-permute-start | bytes 786440 | tf_op jit(solution)/shard_map/ppermute | solution.py:473
  70.4 11.8 %pair_coherence.1 = bf16[2,128,64,128]{3,2,1,0:T(8,128)(2,1)} custom-call(f32[4,2048,256]{2,1,0:T(8,128)S(1)} %pair_first.1.first_ref, bf16[2048,768]{1,0:T(8,128)(2,1)S(1)} %get-tuple-element.59.refs_0_, bf16[2048,768]{1,0:T(8,128)(2,1)S(1)} %get-tuple-element.60.refs_1_, bf16[2048,768]{1,0:T(8,128)(2,1)S(1)} %get-tuple-element.61.refs_2_, ...), custom_call_target="tpu_custom_call" | custom-call | flops 9663676416 | bytes 16777216 | tf_op jit(solution)/shard_map/pair_coherence/pallas_call | solution.py:421
  (30 shorter events, 6.3 us)
Async XLA Ops:
  0.6 8.1 %collective-permute-start = (bf16[128,768]{1,0:T(8,128)(2,1)}, bf16[128,768]{1,0:T(8,128)(2,1)S(1)}, u32[]{:S(2)}, u32[]{:S(2)}) collective-permute-start(bf16[128,768]{1,0:T(8,128)(2,1)} %bitcast.1), channel_id=1, source_target_pairs={{0,1},{1,0},{2,3},{3,2},{4,5},{5,4},{6,7},{7,6},{8,9},{9,8},{10,11... | collective-permute-start | bytes 589832 | tf_op jit(solution)/shard_map/ppermute | solution.py:444
  2.2 10.8 %collective-permute-start.1 = (bf16[128,768]{1,0:T(8,128)(2,1)}, bf16[128,768]{1,0:T(8,128)(2,1)S(1)}, u32[]{:S(2)}, u32[]{:S(2)}) collective-permute-start(bf16[128,768]{1,0:T(8,128)(2,1)} %bitcast.2), channel_id=1, source_target_pairs={{0,2},{1,3},{2,0},{3,1},{4,6},{5,7},{6,4},{7,5},{8,10},{9,11},{10,... | collective-permute-start | bytes 589832 | tf_op jit(solution)/shard_map/ppermute | solution.py:444
  3.7 10.3 %collective-permute-start.2 = (bf16[128,768]{1,0:T(8,128)(2,1)}, bf16[128,768]{1,0:T(8,128)(2,1)S(1)}, u32[]{:S(2)}, u32[]{:S(2)}) collective-permute-start(bf16[128,768]{1,0:T(8,128)(2,1)} %bitcast.3), channel_id=1, source_target_pairs={{0,3},{1,2},{2,1},{3,0},{4,7},{5,6},{6,5},{7,4},{8,11},{9,10},{10,... | collective-permute-start | bytes 589832 | tf_op jit(solution)/shard_map/ppermute | solution.py:444
  4.2 15.7 %collective-permute-start.3 = (bf16[128,768]{1,0:T(8,128)(2,1)}, bf16[128,768]{1,0:T(8,128)(2,1)S(1)}, u32[]{:S(2)}, u32[]{:S(2)}) collective-permute-start(bf16[128,768]{1,0:T(8,128)(2,1)} %bitcast.4), channel_id=1, source_target_pairs={{0,8},{4,12},{8,16},{12,20},{16,24},{20,28},{24,0},{28,4},{1,9},{5... | collective-permute-start | bytes 589832 | tf_op jit(solution)/shard_map/ppermute | solution.py:450
  5.8 16.3 %collective-permute-start.4 = (bf16[128,768]{1,0:T(8,128)(2,1)}, bf16[128,768]{1,0:T(8,128)(2,1)S(1)}, u32[]{:S(2)}, u32[]{:S(2)}) collective-permute-start(bf16[128,768]{1,0:T(8,128)(2,1)} %bitcast.5), channel_id=1, source_target_pairs={{0,16},{4,20},{8,24},{12,28},{16,0},{20,4},{24,8},{28,12},{1,17},{... | collective-permute-start | bytes 589832 | tf_op jit(solution)/shard_map/ppermute | solution.py:450
  8.7 15.0 %collective-permute-start.5 = (bf16[128,768]{1,0:T(8,128)(2,1)}, bf16[128,768]{1,0:T(8,128)(2,1)S(1)}, u32[]{:S(2)}, u32[]{:S(2)}) collective-permute-start(bf16[128,768]{1,0:T(8,128)(2,1)} %bitcast.6), channel_id=1, source_target_pairs={{0,24},{4,28},{8,0},{12,4},{16,8},{20,12},{24,16},{28,20},{1,25},{... | collective-permute-start | bytes 589832 | tf_op jit(solution)/shard_map/ppermute | solution.py:450
  8.8 1.0 %copy-start = (bf16[1,128,768]{2,1,0:T(8,128)(2,1)S(1)}, bf16[1,128,768]{2,1,0:T(8,128)(2,1)}, u32[]{:S(2)}) copy-start(bf16[1,128,768]{2,1,0:T(8,128)(2,1)} %param.5) | copy-start | bytes 589828
  23.7 0.7 copy-start.1
  25.2 1.5 %collective-permute-start.7 = (bf16[128,768]{1,0:T(8,128)(2,1)S(1)}, bf16[128,768]{1,0:T(8,128)(2,1)S(1)}, u32[]{:S(2)}, u32[]{:S(2)}) collective-permute-start(bf16[128,768]{1,0:T(8,128)(2,1)S(1)} %get-tuple-element.55), channel_id=1, source_target_pairs={{0,4},{4,0},{8,12},{12,8},{16,20},{20,16},{24,28},{28,24},{1,5},{5... | collective-permute-start | bytes 589832 | tf_op jit(solution)/shard_map/ppermute | solution.py:447
  25.3 9.9 %collective-permute-start.6 = (bf16[2,128,768]{2,1,0:T(8,128)(2,1)S(1)}, bf16[2,128,768]{2,1,0:T(8,128)(2,1)S(1)}, u32[]{:S(2)}, u32[]{:S(2)}) collective-permute-start(bf16[2,128,768]{2,1,0:T(8,128)(2,1)S(1)} %get-tuple-element.53), channel_id=1, source_target_pairs={{0,4},{4,0},{8,12},{12,8},{16,20},{20,16},{24,28},{28,24},{1,5},{5... | collective-permute-start | bytes 1179656 | tf_op jit(solution)/shard_map/ppermute | solution.py:447
  26.8 8.4 %copy-start.2 = (s32[2,8]{1,0:T(2,128)S(1)}, s32[2,8]{1,0:T(2,128)}, u32[]{:S(2)}) copy-start(s32[2,8]{1,0:T(2,128)} %scalars_ref.2) | copy-start | bytes 196
  26.8 13.6 %collective-permute-start.10 = (bf16[128,768]{1,0:T(8,128)(2,1)S(1)}, bf16[128,768]{1,0:T(8,128)(2,1)S(1)}, u32[]{:S(2)}, u32[]{:S(2)}) collective-permute-start(bf16[128,768]{1,0:T(8,128)(2,1)S(1)} %merge.3.aux_ref), channel_id=1, source_target_pairs={{0,3},{1,2},{2,1},{3,0},{4,7},{5,6},{6,5},{7,4},{8,11},{9,10},{10,... | collective-permute-start | bytes 589832 | tf_op jit(solution)/shard_map/ppermute | solution.py:444
  29.4 11.1 %collective-permute-start.8 = (bf16[128,768]{1,0:T(8,128)(2,1)S(1)}, bf16[128,768]{1,0:T(8,128)(2,1)S(1)}, u32[]{:S(2)}, u32[]{:S(2)}) collective-permute-start(bf16[128,768]{1,0:T(8,128)(2,1)S(1)} %merge.3.aux_ref), channel_id=1, source_target_pairs={{0,1},{1,0},{2,3},{3,2},{4,5},{5,4},{6,7},{7,6},{8,9},{9,8},{10,11... | collective-permute-start | bytes 589832 | tf_op jit(solution)/shard_map/ppermute | solution.py:444
  29.9 10.6 %collective-permute-start.9 = (bf16[128,768]{1,0:T(8,128)(2,1)S(1)}, bf16[128,768]{1,0:T(8,128)(2,1)S(1)}, u32[]{:S(2)}, u32[]{:S(2)}) collective-permute-start(bf16[128,768]{1,0:T(8,128)(2,1)S(1)} %merge.3.aux_ref), channel_id=1, source_target_pairs={{0,2},{1,3},{2,0},{3,1},{4,6},{5,7},{6,4},{7,5},{8,10},{9,11},{10,... | collective-permute-start | bytes 589832 | tf_op jit(solution)/shard_map/ppermute | solution.py:444
  36.3 7.8 %copy-start.3 = (s32[1,128]{1,0:T(1,128)S(1)}, s32[1,128]{1,0:T(1,128)}, u32[]{:S(2)}) copy-start(s32[1,128]{1,0:T(1,128)} %start_ref.1) | copy-start | bytes 1540
  36.3 7.8 %copy-start.4 = (s32[1,128]{1,0:T(1,128)S(1)}, s32[1,128]{1,0:T(1,128)}, u32[]{:S(2)}) copy-start(s32[1,128]{1,0:T(1,128)} %end_ref.1) | copy-start | bytes 1540
  40.5 29.8 %collective-permute-start.11 = (bf16[2,128,768]{2,1,0:T(8,128)(2,1)S(1)}, bf16[2,128,768]{2,1,0:T(8,128)(2,1)S(1)}, u32[]{:S(2)}, u32[]{:S(2)}) collective-permute-start(bf16[2,128,768]{2,1,0:T(8,128)(2,1)S(1)} %merge.2.partner_ref), channel_id=1, source_target_pairs={{0,1},{1,0},{2,3},{3,2},{4,5},{5,4},{6,7},{7,6},{8,9},{9,8},{10,11... | collective-permute-start | bytes 1179656 | tf_op jit(solution)/shard_map/ppermute | solution.py:444
  42.1 28.3 %collective-permute-start.12 = (bf16[2,128,768]{2,1,0:T(8,128)(2,1)S(1)}, bf16[2,128,768]{2,1,0:T(8,128)(2,1)S(1)}, u32[]{:S(2)}, u32[]{:S(2)}) collective-permute-start(bf16[2,128,768]{2,1,0:T(8,128)(2,1)S(1)} %merge.2.partner_ref), channel_id=1, source_target_pairs={{0,2},{1,3},{2,0},{3,1},{4,6},{5,7},{6,4},{7,5},{8,10},{9,11},{10,... | collective-permute-start | bytes 1179656 | tf_op jit(solution)/shard_map/ppermute | solution.py:444
  43.6 26.8 %collective-permute-start.13 = (bf16[2,128,768]{2,1,0:T(8,128)(2,1)S(1)}, bf16[2,128,768]{2,1,0:T(8,128)(2,1)S(1)}, u32[]{:S(2)}, u32[]{:S(2)}) collective-permute-start(bf16[2,128,768]{2,1,0:T(8,128)(2,1)S(1)} %merge.2.partner_ref), channel_id=1, source_target_pairs={{0,3},{1,2},{2,1},{3,0},{4,7},{5,6},{6,5},{7,4},{8,11},{9,10},{10,... | collective-permute-start | bytes 1179656 | tf_op jit(solution)/shard_map/ppermute | solution.py:444
  67.7 14.5 %collective-permute-start.14 = (bf16[128,8,128]{2,1,0:T(8,128)(2,1)S(1)}, bf16[128,8,128]{2,1,0:T(8,128)(2,1)S(1)}, u32[]{:S(2)}, u32[]{:S(2)}) collective-permute-start(bf16[128,8,128]{2,1,0:T(8,128)(2,1)S(1)} %get-tuple-element.71), channel_id=1, source_target_pairs={{3,0},{7,4},{11,8},{15,12},{19,16},{23,20},{27,24},{31,28}} | collective-permute-start | bytes 786440 | tf_op jit(solution)/shard_map/ppermute | solution.py:473
  69.0 13.8 %collective-permute-start.15 = (bf16[128,8,128]{2,1,0:T(8,128)(2,1)S(1)}, bf16[128,8,128]{2,1,0:T(8,128)(2,1)S(1)}, u32[]{:S(2)}, u32[]{:S(2)}) collective-permute-start(bf16[128,8,128]{2,1,0:T(8,128)(2,1)S(1)} %get-tuple-element.71), channel_id=1, source_target_pairs={{2,0},{6,4},{10,8},{14,12},{18,16},{22,20},{26,24},{30,28}} | collective-permute-start | bytes 786440 | tf_op jit(solution)/shard_map/ppermute | solution.py:473

commit v6 on v5

--- a/solution.py
+++ b/solution.py
@@ -68,6 +68,7 @@
         in_specs=[SMEM_SPEC] * 2 + [VMEM_SPEC] * len(column),
         out_specs=[VMEM_SPEC] * 4,
         compiler_params=pltpu.CompilerParams(vmem_limit_bytes=2 << 20),
+        cost_estimate=pl.CostEstimate(flops=0, transcendentals=0, bytes_accessed=1<<20),
         name="pick",
     )(owners, pairing, *column)
 
@@ -93,6 +94,7 @@
         in_specs=[SMEM_SPEC, VMEM_SPEC, VMEM_SPEC],
         out_specs=VMEM_SPEC,
         compiler_params=pltpu.CompilerParams(vmem_limit_bytes=4 << 20),
+        cost_estimate=pl.CostEstimate(flops=0, transcendentals=0, bytes_accessed=1<<20),
         name="merge",
     )(scalars, held, got)
 
@@ -122,6 +124,7 @@
         in_specs=[VMEM_SPEC],
         out_specs=[VMEM_SPEC] * (2 + raw),
         compiler_params=pltpu.CompilerParams(vmem_limit_bytes=4 << 20),
+        cost_estimate=pl.CostEstimate(flops=0, transcendentals=0, bytes_accessed=3<<20),
         name="shifted_copies",
     )(block)
 
@@ -450,25 +453,27 @@
         lax.ppermute(raw, "chan", [(i, (i + 2 * k) % chan_size) for i in range(chan_size)])
         for k in range(1, chan_size // 2)
     ]
-    own_all = [raw] + [exchange(raw, k) for k in range(1, win_size)]
-    shifted = [shifted_copies(block, n == 0) for n, block in enumerate(own_all)]
-    column[0] = shifted[0][2]
-    copies, own_white = [pair[0] for pair in shifted], [pair[1] for pair in shifted]
-    copies, own_white, column = lax.optimization_barrier((copies, own_white, column))
+    own_rest = [exchange(raw, k) for k in range(1, win_size)]
+    first_copies, own_white, column[0] = shifted_copies(raw, True)
+    early = [shifted_copies(block) for block in own_rest[:2]]
+    first_copies, own_white, early, column = lax.optimization_barrier((first_copies, own_white, early, column))
     aux_sent, aux_held, sent, held = pick(aux_owners, pairing, column)
+    aux_sent, sent, own_rest = lax.optimization_barrier((aux_sent, sent, own_rest[2:]))
+    shifted = early + [shifted_copies(block) for block in own_rest]
+    copies, own_rest = [both[0] for both in shifted], [both[1] for both in shifted]
     aux = merge(lambda ref, chan: [ref[0]], aux_owners, aux_held, cross(aux_sent))
     partners = merge(
         lambda ref, chan: [ref[r, chan] for r in range(rounds)], pairing, held, cross(sent)
     )
     aux_rest = [exchange(aux, k) for k in range(1, win_size)]
-    pair_begun = pair_first(copies[0], partners, LAGS // win_size)
-    part_begun = part_first(aux, own_white[0])
-    partners, aux_rest, pair_begun, part_begun = lax.optimization_barrier(
-        (partners, aux_rest, pair_begun, part_begun)
+    pair_begun = pair_first(first_copies, partners, LAGS // win_size)
+    part_begun = part_first(aux, own_white)
+    partners, aux_rest, pair_begun, part_begun, copies = lax.optimization_barrier(
+        (partners, aux_rest, pair_begun, part_begun, copies)
     )
     partner_rest = [exchange(partners, k) for k in range(1, win_size)]
-    three, moved = coda_coherence(coda_start, coda_end, part_begun, aux_rest, own_white[1:], LAGS3 // win_size)
-    pair = pair_coherence(pair_begun, copies[1:], partner_rest, LAGS // win_size)
+    three, moved = coda_coherence(coda_start, coda_end, part_begun, aux_rest, own_rest, LAGS3 // win_size)
+    pair = pair_coherence(pair_begun, copies, partner_rest, LAGS // win_size)
     helpers = LAGS3 // win_size // 2 // MOVED
     moved = [lax.ppermute(moved, "win", [(win_size - 1 - n, 0)]) for n in range(helpers)]
     pair, three, moved = lax.optimization_barrier((pair, three, moved))

time: 84.7 us -> 84 us (level)
  waiting for transfers between devices: 12.8 us -> 9.53 us
  starting transfers between devices: 16.5 us -> 19.6 us
    ppermute x9, waiting for transfers between devices: 2.52 us -> 0.02 us  [exchange(): return lax.ppermute(block, 'win', [(i, i ^ k) for i in range(win_size)])]
    ppermute x3, starting transfers between devices: 2.7 us -> 4.61 us  [per_device(): lax.ppermute(raw, 'chan', [(i, (i + 2 * k) % chan_size) for i in range(ch...]
    ppermute x9, starting transfers between devices: 10.7 us -> 11.9 us  [exchange(): return lax.ppermute(block, 'win', [(i, i ^ k) for i in range(win_size)])]
    ppermute x2, waiting for transfers between devices: 0.93 us -> 0.01 us  [cross(): return lax.ppermute(block, 'chan', [(i, i ^ 1) for i in range(chan_size)])]
  transfers between devices with their start and end apart: 16 -> 16, of which waited for: 7 -> 4; matrix products, arithmetic and copies ran while one was open for 0% -> 0% of each run, Pallas kernels for 59% -> 60%
where the time goes in v6:
time: 84 us; the launch traced here: 83.6 us
  Pallas kernels  51.2 us (61%)
  starting transfers between devices  19.6 us (23%)
  waiting for transfers between devices  9.53 us (11%)
  local copies, waits for them, and re-layouts  1.66 us (2%)
  between operations  1.65 us (2%)
    pallas_call x1, Pallas kernels, coda_coherence(): pl.pallas_call(functools.partial(coda_kernel, windows), out_shape=[jax.Sh...  23.7 us
    ppermute x9, starting transfers between devices, exchange(): return lax.ppermute(block, 'win', [(i, i ^ k) for i in range(win_size)])  11.9 us
    pallas_call x1, Pallas kernels, pair_coherence(): pl.pallas_call(functools.partial(pair_kernel, windows), out_shape=jax.Sha...  11.8 us
    ppermute x3, waiting for transfers between devices, per_device(): lax.ppermute(raw, 'chan', [(i, (i + 2 * k) % chan_size) for i in range(ch...  8.94 us
    pallas_call x1, Pallas kernels, part_first(): pl.pallas_call(part_first_kernel, out_shape=jax.ShapeDtypeStruct((steps,...  4.82 us
    ppermute x3, starting transfers between devices, per_device(): lax.ppermute(raw, 'chan', [(i, (i + 2 * k) % chan_size) for i in range(ch...  4.61 us
    pallas_call x1, Pallas kernels, pair_first(): pl.pallas_call(pair_first_kernel, out_shape=jax.ShapeDtypeStruct((steps,...  4.19 us
    pallas_call x4, Pallas kernels, shifted_copies(): pl.pallas_call(shift_kernel, out_shape=[jax.ShapeDtypeStruct((blk * STEP,...  3.91 us
  transfers between devices with their start and end apart: 16, of which 4 were waited for; matrix products, arithmetic and copies ran while one was open for 0% of the time, Pallas kernels for 60%

profile of v6, /device:TPU:8, one launch (start us, length us, event | category | flops | bytes accessed | tf_op | source)
XLA Modules:
  0.0 83.6 jit_solution(17377915667881594525)
XLA Ops:
  0.6 1.6 %collective-permute-start = (bf16[128,768]{1,0:T(8,128)(2,1)}, bf16[128,768]{1,0:T(8,128)(2,1)S(1)}, u32[]{:S(2)}, u32[]{:S(2)}) collective-permute-start(bf16[128,768]{1,0:T(8,128)(2,1)} %bitcast.1), channel_id=1, source_target_pairs={{0,1},{1,0},{2,3},{3,2},{4,5},{5,4},{6,7},{7,6},{8,9},{9,8},{10,11... | collective-permute-start | bytes 589832 | tf_op jit(solution)/shard_map/ppermute | solution.py:447
  2.2 1.5 %collective-permute-start.1 = (bf16[128,768]{1,0:T(8,128)(2,1)}, bf16[128,768]{1,0:T(8,128)(2,1)S(1)}, u32[]{:S(2)}, u32[]{:S(2)}) collective-permute-start(bf16[128,768]{1,0:T(8,128)(2,1)} %bitcast.2), channel_id=1, source_target_pairs={{0,2},{1,3},{2,0},{3,1},{4,6},{5,7},{6,4},{7,5},{8,10},{9,11},{10,... | collective-permute-start | bytes 589832 | tf_op jit(solution)/shard_map/ppermute | solution.py:447
  3.7 1.6 %collective-permute-start.2 = (bf16[128,768]{1,0:T(8,128)(2,1)}, bf16[128,768]{1,0:T(8,128)(2,1)S(1)}, u32[]{:S(2)}, u32[]{:S(2)}) collective-permute-start(bf16[128,768]{1,0:T(8,128)(2,1)} %bitcast.3), channel_id=1, source_target_pairs={{0,8},{4,12},{8,16},{12,20},{16,24},{20,28},{24,0},{28,4},{1,9},{5... | collective-permute-start | bytes 589832 | tf_op jit(solution)/shard_map/ppermute | solution.py:453
  5.3 1.2 %collective-permute-start.3 = (bf16[128,768]{1,0:T(8,128)(2,1)}, bf16[128,768]{1,0:T(8,128)(2,1)S(1)}, u32[]{:S(2)}, u32[]{:S(2)}) collective-permute-start(bf16[128,768]{1,0:T(8,128)(2,1)} %bitcast.4), channel_id=1, source_target_pairs={{0,16},{4,20},{8,24},{12,28},{16,0},{20,4},{24,8},{28,12},{1,17},{... | collective-permute-start | bytes 589832 | tf_op jit(solution)/shard_map/ppermute | solution.py:453
  6.5 1.8 %collective-permute-start.4 = (bf16[128,768]{1,0:T(8,128)(2,1)}, bf16[128,768]{1,0:T(8,128)(2,1)S(1)}, u32[]{:S(2)}, u32[]{:S(2)}) collective-permute-start(bf16[128,768]{1,0:T(8,128)(2,1)} %bitcast.5), channel_id=1, source_target_pairs={{0,24},{4,28},{8,0},{12,4},{16,8},{20,12},{24,16},{28,20},{1,25},{... | collective-permute-start | bytes 589832 | tf_op jit(solution)/shard_map/ppermute | solution.py:453
  8.3 1.7 %collective-permute-start.5 = (bf16[128,768]{1,0:T(8,128)(2,1)}, bf16[128,768]{1,0:T(8,128)(2,1)S(1)}, u32[]{:S(2)}, u32[]{:S(2)}) collective-permute-start(bf16[128,768]{1,0:T(8,128)(2,1)} %bitcast.6), channel_id=1, source_target_pairs={{0,3},{1,2},{2,1},{3,0},{4,7},{5,6},{6,5},{7,4},{8,11},{9,10},{10,... | collective-permute-start | bytes 589832 | tf_op jit(solution)/shard_map/ppermute | solution.py:447
  10.0 1.0 %copy-done = bf16[1,128,768]{2,1,0:T(8,128)(2,1)S(1)} copy-done((bf16[1,128,768]{2,1,0:T(8,128)(2,1)S(1)}, bf16[1,128,768]{2,1,0:T(8,128)(2,1)}, u32[]{:S(2)}) %copy-start) | copy-done | bytes 196632
  11.0 1.0 %shifted_copies.4 = (bf16[2048,768]{1,0:T(8,128)(2,1)S(1)}, bf16[128,768]{1,0:T(8,128)(2,1)S(1)}, bf16[128,768]{1,0:T(8,128)(2,1)S(1)}) custom-call(bf16[128,768]{1,0:T(8,128)(2,1)S(1)} %bitcast.7), custom_call_target="tpu_custom_call" | custom-call | bytes 3145728 | tf_op jit(solution)/shard_map/shifted_copies/pallas_call | solution.py:117
  12.6 1.0 %shifted_copies.5 = (bf16[2048,768]{1,0:T(8,128)(2,1)S(1)}, bf16[128,768]{1,0:T(8,128)(2,1)S(1)}) custom-call(bf16[128,768]{1,0:T(8,128)(2,1)S(1)} %collective-permute-done.block_ref), custom_call_target="tpu_custom_call" | custom-call | bytes 3145728 | tf_op jit(solution)/shard_map/shifted_copies/pallas_call | solution.py:117
  13.6 1.0 %shifted_copies.6 = (bf16[2048,768]{1,0:T(8,128)(2,1)S(1)}, bf16[128,768]{1,0:T(8,128)(2,1)S(1)}) custom-call(bf16[128,768]{1,0:T(8,128)(2,1)S(1)} %collective-permute-done.1.block_ref), custom_call_target="tpu_custom_call" | custom-call | bytes 3145728 | tf_op jit(solution)/shard_map/shifted_copies/pallas_call | solution.py:117
  14.6 4.8 %collective-permute-done.2.refs_1_ = bf16[128,768]{1,0:T(8,128)(2,1)S(1)} collective-permute-done((bf16[128,768]{1,0:T(8,128)(2,1)}, bf16[128,768]{1,0:T(8,128)(2,1)S(1)}, u32[]{:S(2)}, u32[]{:S(2)}) %collective-permute-start.2) | collective-permute-done | bytes 196640 | tf_op jit(solution)/shard_map/ppermute | solution.py:453
  19.4 2.5 %collective-permute-done.3.refs_2_ = bf16[128,768]{1,0:T(8,128)(2,1)S(1)} collective-permute-done((bf16[128,768]{1,0:T(8,128)(2,1)}, bf16[128,768]{1,0:T(8,128)(2,1)S(1)}, u32[]{:S(2)}, u32[]{:S(2)}) %collective-permute-start.3) | collective-permute-done | bytes 196640 | tf_op jit(solution)/shard_map/ppermute | solution.py:453
  21.8 1.7 %collective-permute-done.4.refs_3_ = bf16[128,768]{1,0:T(8,128)(2,1)S(1)} collective-permute-done((bf16[128,768]{1,0:T(8,128)(2,1)}, bf16[128,768]{1,0:T(8,128)(2,1)S(1)}, u32[]{:S(2)}, u32[]{:S(2)}) %collective-permute-start.4) | collective-permute-done | bytes 196640 | tf_op jit(solution)/shard_map/ppermute | solution.py:453
  25.6 1.0 %shifted_copies.7 = (bf16[2048,768]{1,0:T(8,128)(2,1)S(1)}, bf16[128,768]{1,0:T(8,128)(2,1)S(1)}) custom-call(bf16[128,768]{1,0:T(8,128)(2,1)S(1)} %collective-permute-done.5.block_ref), custom_call_target="tpu_custom_call" | custom-call | bytes 3145728 | tf_op jit(solution)/shard_map/shifted_copies/pallas_call | solution.py:117
  27.3 1.5 %collective-permute-start.8 = (bf16[128,768]{1,0:T(8,128)(2,1)S(1)}, bf16[128,768]{1,0:T(8,128)(2,1)S(1)}, u32[]{:S(2)}, u32[]{:S(2)}) collective-permute-start(bf16[128,768]{1,0:T(8,128)(2,1)S(1)} %merge.3.aux_ref), channel_id=1, source_target_pairs={{0,1},{1,0},{2,3},{3,2},{4,5},{5,4},{6,7},{7,6},{8,9},{9,8},{10,11... | collective-permute-start | bytes 589832 | tf_op jit(solution)/shard_map/ppermute | solution.py:447
  28.8 1.5 %collective-permute-start.9 = (bf16[128,768]{1,0:T(8,128)(2,1)S(1)}, bf16[128,768]{1,0:T(8,128)(2,1)S(1)}, u32[]{:S(2)}, u32[]{:S(2)}) collective-permute-start(bf16[128,768]{1,0:T(8,128)(2,1)S(1)} %merge.3.aux_ref), channel_id=1, source_target_pairs={{0,2},{1,3},{2,0},{3,1},{4,6},{5,7},{6,4},{7,5},{8,10},{9,11},{10,... | collective-permute-start | bytes 589832 | tf_op jit(solution)/shard_map/ppermute | solution.py:447
  30.3 4.8 %part_first.1.first = f32[4,2048,256]{2,1,0:T(8,128)S(1)} custom-call(bf16[128,768]{1,0:T(8,128)(2,1)S(1)} %merge.3.aux_ref, bf16[128,768]{1,0:T(8,128)(2,1)S(1)} %get-tuple-element.61.own_ref), custom_call_target="tpu_custom_call" | custom-call | flops 2684354560 | bytes 8388608 | tf_op jit(solution)/shard_map/part_first/pallas_call | solution.py:155
  35.1 1.0 %merge.2.partner_ref = bf16[2,128,768]{2,1,0:T(8,128)(2,1)S(1)} custom-call(s32[2,8]{1,0:T(2,128)S(1)} %copy-done.2, bf16[2,128,768]{2,1,0:T(8,128)(2,1)S(1)} %get-tuple-element.54.held_ref, bf16[2,128,768]{2,1,0:T(8,128)(2,1)S(1)} %collective-permute-done.6.got_ref), custom_call_target="tpu_custom_call" | custom-call | bytes 1048576 | tf_op jit(solution)/shard_map/merge/pallas_call | solution.py:91
  36.2 4.2 %pair_first.1.first_ref = f32[4,2048,256]{2,1,0:T(8,128)S(1)} custom-call(bf16[2048,768]{1,0:T(8,128)(2,1)S(1)} %get-tuple-element.60.shifted_ref, bf16[2,128,768]{2,1,0:T(8,128)(2,1)S(1)} %merge.2.partner_ref), custom_call_target="tpu_custom_call" | custom-call | flops 3221225472 | bytes 8388608 | tf_op jit(solution)/shard_map/pair_first/pallas_call | solution.py:376
  41.5 2.4 %collective-permute-start.13 = (bf16[2,128,768]{2,1,0:T(8,128)(2,1)S(1)}, bf16[2,128,768]{2,1,0:T(8,128)(2,1)S(1)}, u32[]{:S(2)}, u32[]{:S(2)}) collective-permute-start(bf16[2,128,768]{2,1,0:T(8,128)(2,1)S(1)} %merge.2.partner_ref), channel_id=1, source_target_pairs={{0,3},{1,2},{2,1},{3,0},{4,7},{5,6},{6,5},{7,4},{8,11},{9,10},{10,... | collective-permute-start | bytes 1179656 | tf_op jit(solution)/shard_map/ppermute | solution.py:447
  44.0 23.7 %coda_coherence.1 = (bf16[128,32,128]{2,1,0:T(8,128)(2,1)}, bf16[128,8,128]{2,1,0:T(8,128)(2,1)S(1)}) custom-call(s32[1,128]{1,0:T(1,128)S(1)} %copy-done.3, s32[1,128]{1,0:T(1,128)S(1)} %copy-done.4, f32[4,2048,256]{2,1,0:T(8,128)S(1)} %part_first.1.first, bf16[128,768]{1,0:T(8,128)(2,1)S(1)} %collective-permute-done.8.refs_0_, ...), custom_call_target="tpu_custom_call" | custom-call | flops 25232932864 | bytes 16777216 | tf_op jit(solution)/shard_map/coda_coherence/pallas_call | solution.py:328
  67.6 1.3 %collective-permute-start.14 = (bf16[128,8,128]{2,1,0:T(8,128)(2,1)S(1)}, bf16[128,8,128]{2,1,0:T(8,128)(2,1)S(1)}, u32[]{:S(2)}, u32[]{:S(2)}) collective-permute-start(bf16[128,8,128]{2,1,0:T(8,128)(2,1)S(1)} %get-tuple-element.79), channel_id=1, source_target_pairs={{3,0},{7,4},{11,8},{15,12},{19,16},{23,20},{27,24},{31,28}} | collective-permute-start | bytes 786440 | tf_op jit(solution)/shard_map/ppermute | solution.py:478
  68.9 1.3 %collective-permute-start.15 = (bf16[128,8,128]{2,1,0:T(8,128)(2,1)S(1)}, bf16[128,8,128]{2,1,0:T(8,128)(2,1)S(1)}, u32[]{:S(2)}, u32[]{:S(2)}) collective-permute-start(bf16[128,8,128]{2,1,0:T(8,128)(2,1)S(1)} %get-tuple-element.79), channel_id=1, source_target_pairs={{2,0},{6,4},{10,8},{14,12},{18,16},{22,20},{26,24},{30,28}} | collective-permute-start | bytes 786440 | tf_op jit(solution)/shard_map/ppermute | solution.py:478
  70.3 11.8 %pair_coherence.1 = bf16[2,128,64,128]{3,2,1,0:T(8,128)(2,1)} custom-call(f32[4,2048,256]{2,1,0:T(8,128)S(1)} %pair_first.1.first_ref, bf16[2048,768]{1,0:T(8,128)(2,1)S(1)} %get-tuple-element.67.refs_0_, bf16[2048,768]{1,0:T(8,128)(2,1)S(1)} %get-tuple-element.68.refs_1_, bf16[2048,768]{1,0:T(8,128)(2,1)S(1)} %get-tuple-element.69.refs_2_, ...), custom_call_target="tpu_custom_call" | custom-call | flops 9663676416 | bytes 16777216 | tf_op jit(solution)/shard_map/pair_coherence/pallas_call | solution.py:424
  (30 shorter events, 5.3 us)
Async XLA Ops:
  0.6 7.7 %collective-permute-start = (bf16[128,768]{1,0:T(8,128)(2,1)}, bf16[128,768]{1,0:T(8,128)(2,1)S(1)}, u32[]{:S(2)}, u32[]{:S(2)}) collective-permute-start(bf16[128,768]{1,0:T(8,128)(2,1)} %bitcast.1), channel_id=1, source_target_pairs={{0,1},{1,0},{2,3},{3,2},{4,5},{5,4},{6,7},{7,6},{8,9},{9,8},{10,11... | collective-permute-start | bytes 589832 | tf_op jit(solution)/shard_map/ppermute | solution.py:447
  2.2 11.4 %collective-permute-start.1 = (bf16[128,768]{1,0:T(8,128)(2,1)}, bf16[128,768]{1,0:T(8,128)(2,1)S(1)}, u32[]{:S(2)}, u32[]{:S(2)}) collective-permute-start(bf16[128,768]{1,0:T(8,128)(2,1)} %bitcast.2), channel_id=1, source_target_pairs={{0,2},{1,3},{2,0},{3,1},{4,6},{5,7},{6,4},{7,5},{8,10},{9,11},{10,... | collective-permute-start | bytes 589832 | tf_op jit(solution)/shard_map/ppermute | solution.py:447
  3.7 15.7 %collective-permute-start.2 = (bf16[128,768]{1,0:T(8,128)(2,1)}, bf16[128,768]{1,0:T(8,128)(2,1)S(1)}, u32[]{:S(2)}, u32[]{:S(2)}) collective-permute-start(bf16[128,768]{1,0:T(8,128)(2,1)} %bitcast.3), channel_id=1, source_target_pairs={{0,8},{4,12},{8,16},{12,20},{16,24},{20,28},{24,0},{28,4},{1,9},{5... | collective-permute-start | bytes 589832 | tf_op jit(solution)/shard_map/ppermute | solution.py:453
  5.3 16.6 %collective-permute-start.3 = (bf16[128,768]{1,0:T(8,128)(2,1)}, bf16[128,768]{1,0:T(8,128)(2,1)S(1)}, u32[]{:S(2)}, u32[]{:S(2)}) collective-permute-start(bf16[128,768]{1,0:T(8,128)(2,1)} %bitcast.4), channel_id=1, source_target_pairs={{0,16},{4,20},{8,24},{12,28},{16,0},{20,4},{24,8},{28,12},{1,17},{... | collective-permute-start | bytes 589832 | tf_op jit(solution)/shard_map/ppermute | solution.py:453
  6.5 17.0 %collective-permute-start.4 = (bf16[128,768]{1,0:T(8,128)(2,1)}, bf16[128,768]{1,0:T(8,128)(2,1)S(1)}, u32[]{:S(2)}, u32[]{:S(2)}) collective-permute-start(bf16[128,768]{1,0:T(8,128)(2,1)} %bitcast.5), channel_id=1, source_target_pairs={{0,24},{4,28},{8,0},{12,4},{16,8},{20,12},{24,16},{28,20},{1,25},{... | collective-permute-start | bytes 589832 | tf_op jit(solution)/shard_map/ppermute | solution.py:453
  8.3 16.7 %collective-permute-start.5 = (bf16[128,768]{1,0:T(8,128)(2,1)}, bf16[128,768]{1,0:T(8,128)(2,1)S(1)}, u32[]{:S(2)}, u32[]{:S(2)}) collective-permute-start(bf16[128,768]{1,0:T(8,128)(2,1)} %bitcast.6), channel_id=1, source_target_pairs={{0,3},{1,2},{2,1},{3,0},{4,7},{5,6},{6,5},{7,4},{8,11},{9,10},{10,... | collective-permute-start | bytes 589832 | tf_op jit(solution)/shard_map/ppermute | solution.py:447
  10.0 1.0 %copy-start = (bf16[1,128,768]{2,1,0:T(8,128)(2,1)S(1)}, bf16[1,128,768]{2,1,0:T(8,128)(2,1)}, u32[]{:S(2)}) copy-start(bf16[1,128,768]{2,1,0:T(8,128)(2,1)} %param.5) | copy-start | bytes 589828
  23.5 0.7 copy-start.1
  25.0 1.6 %collective-permute-start.7 = (bf16[128,768]{1,0:T(8,128)(2,1)S(1)}, bf16[128,768]{1,0:T(8,128)(2,1)S(1)}, u32[]{:S(2)}, u32[]{:S(2)}) collective-permute-start(bf16[128,768]{1,0:T(8,128)(2,1)S(1)} %get-tuple-element.59), channel_id=1, source_target_pairs={{0,4},{4,0},{8,12},{12,8},{16,20},{20,16},{24,28},{28,24},{1,5},{5... | collective-permute-start | bytes 589832 | tf_op jit(solution)/shard_map/ppermute | solution.py:450
  25.1 10.0 %collective-permute-start.6 = (bf16[2,128,768]{2,1,0:T(8,128)(2,1)S(1)}, bf16[2,128,768]{2,1,0:T(8,128)(2,1)S(1)}, u32[]{:S(2)}, u32[]{:S(2)}) collective-permute-start(bf16[2,128,768]{2,1,0:T(8,128)(2,1)S(1)} %get-tuple-element.57), channel_id=1, source_target_pairs={{0,4},{4,0},{8,12},{12,8},{16,20},{20,16},{24,28},{28,24},{1,5},{5... | collective-permute-start | bytes 1179656 | tf_op jit(solution)/shard_map/ppermute | solution.py:450
  26.7 8.4 %copy-start.2 = (s32[2,8]{1,0:T(2,128)S(1)}, s32[2,8]{1,0:T(2,128)}, u32[]{:S(2)}) copy-start(s32[2,8]{1,0:T(2,128)} %scalars_ref.2) | copy-start | bytes 196
  26.7 13.6 %collective-permute-start.10 = (bf16[128,768]{1,0:T(8,128)(2,1)S(1)}, bf16[128,768]{1,0:T(8,128)(2,1)S(1)}, u32[]{:S(2)}, u32[]{:S(2)}) collective-permute-start(bf16[128,768]{1,0:T(8,128)(2,1)S(1)} %merge.3.aux_ref), channel_id=1, source_target_pairs={{0,3},{1,2},{2,1},{3,0},{4,7},{5,6},{6,5},{7,4},{8,11},{9,10},{10,... | collective-permute-start | bytes 589832 | tf_op jit(solution)/shard_map/ppermute | solution.py:447
  27.3 13.1 %collective-permute-start.8 = (bf16[128,768]{1,0:T(8,128)(2,1)S(1)}, bf16[128,768]{1,0:T(8,128)(2,1)S(1)}, u32[]{:S(2)}, u32[]{:S(2)}) collective-permute-start(bf16[128,768]{1,0:T(8,128)(2,1)S(1)} %merge.3.aux_ref), channel_id=1, source_target_pairs={{0,1},{1,0},{2,3},{3,2},{4,5},{5,4},{6,7},{7,6},{8,9},{9,8},{10,11... | collective-permute-start | bytes 589832 | tf_op jit(solution)/shard_map/ppermute | solution.py:447
  28.8 11.6 %collective-permute-start.9 = (bf16[128,768]{1,0:T(8,128)(2,1)S(1)}, bf16[128,768]{1,0:T(8,128)(2,1)S(1)}, u32[]{:S(2)}, u32[]{:S(2)}) collective-permute-start(bf16[128,768]{1,0:T(8,128)(2,1)S(1)} %merge.3.aux_ref), channel_id=1, source_target_pairs={{0,2},{1,3},{2,0},{3,1},{4,6},{5,7},{6,4},{7,5},{8,10},{9,11},{10,... | collective-permute-start | bytes 589832 | tf_op jit(solution)/shard_map/ppermute | solution.py:447
  36.2 7.8 %copy-start.3 = (s32[1,128]{1,0:T(1,128)S(1)}, s32[1,128]{1,0:T(1,128)}, u32[]{:S(2)}) copy-start(s32[1,128]{1,0:T(1,128)} %start_ref.1) | copy-start | bytes 1540
  36.2 7.8 %copy-start.4 = (s32[1,128]{1,0:T(1,128)S(1)}, s32[1,128]{1,0:T(1,128)}, u32[]{:S(2)}) copy-start(s32[1,128]{1,0:T(1,128)} %end_ref.1) | copy-start | bytes 1540
  40.4 29.8 %collective-permute-start.11 = (bf16[2,128,768]{2,1,0:T(8,128)(2,1)S(1)}, bf16[2,128,768]{2,1,0:T(8,128)(2,1)S(1)}, u32[]{:S(2)}, u32[]{:S(2)}) collective-permute-start(bf16[2,128,768]{2,1,0:T(8,128)(2,1)S(1)} %merge.2.partner_ref), channel_id=1, source_target_pairs={{0,1},{1,0},{2,3},{3,2},{4,5},{5,4},{6,7},{7,6},{8,9},{9,8},{10,11... | collective-permute-start | bytes 1179656 | tf_op jit(solution)/shard_map/ppermute | solution.py:447
  41.0 29.2 %collective-permute-start.12 = (bf16[2,128,768]{2,1,0:T(8,128)(2,1)S(1)}, bf16[2,128,768]{2,1,0:T(8,128)(2,1)S(1)}, u32[]{:S(2)}, u32[]{:S(2)}) collective-permute-start(bf16[2,128,768]{2,1,0:T(8,128)(2,1)S(1)} %merge.2.partner_ref), channel_id=1, source_target_pairs={{0,2},{1,3},{2,0},{3,1},{4,6},{5,7},{6,4},{7,5},{8,10},{9,11},{10,... | collective-permute-start | bytes 1179656 | tf_op jit(solution)/shard_map/ppermute | solution.py:447
  41.5 28.7 %collective-permute-start.13 = (bf16[2,128,768]{2,1,0:T(8,128)(2,1)S(1)}, bf16[2,128,768]{2,1,0:T(8,128)(2,1)S(1)}, u32[]{:S(2)}, u32[]{:S(2)}) collective-permute-start(bf16[2,128,768]{2,1,0:T(8,128)(2,1)S(1)} %merge.2.partner_ref), channel_id=1, source_target_pairs={{0,3},{1,2},{2,1},{3,0},{4,7},{5,6},{6,5},{7,4},{8,11},{9,10},{10,... | collective-permute-start | bytes 1179656 | tf_op jit(solution)/shard_map/ppermute | solution.py:447
  67.6 14.5 %collective-permute-start.14 = (bf16[128,8,128]{2,1,0:T(8,128)(2,1)S(1)}, bf16[128,8,128]{2,1,0:T(8,128)(2,1)S(1)}, u32[]{:S(2)}, u32[]{:S(2)}) collective-permute-start(bf16[128,8,128]{2,1,0:T(8,128)(2,1)S(1)} %get-tuple-element.79), channel_id=1, source_target_pairs={{3,0},{7,4},{11,8},{15,12},{19,16},{23,20},{27,24},{31,28}} | collective-permute-start | bytes 786440 | tf_op jit(solution)/shard_map/ppermute | solution.py:478
  68.9 13.7 %collective-permute-start.15 = (bf16[128,8,128]{2,1,0:T(8,128)(2,1)S(1)}, bf16[128,8,128]{2,1,0:T(8,128)(2,1)S(1)}, u32[]{:S(2)}, u32[]{:S(2)}) collective-permute-start(bf16[128,8,128]{2,1,0:T(8,128)(2,1)S(1)} %get-tuple-element.79), channel_id=1, source_target_pairs={{2,0},{6,4},{10,8},{14,12},{18,16},{22,20},{26,24},{30,28}} | collective-permute-start | bytes 786440 | tf_op jit(solution)/shard_map/ppermute | solution.py:478

commit v7 on v6

--- a/solution.py
+++ b/solution.py
@@ -47,8 +47,8 @@
     other = chan + 1 - 2 * (chan % 2)
     aux = owners_ref[0]
     slots = [(out_refs[0], aux), (out_refs[1], aux)]
-    slots += [(out_refs[2].at[r], pairing_ref[r, other]) for r in range(rounds)]
-    slots += [(out_refs[3].at[r], pairing_ref[r, chan]) for r in range(rounds)]
+    slots += [(out_refs[2].at[r], pairing_ref[r * 2 * count + other]) for r in range(rounds)]
+    slots += [(out_refs[3].at[r], pairing_ref[r * 2 * count + chan]) for r in range(rounds)]
     for slot, block in slots:
         distance = (chan - block + 2 * count) % (2 * count) // 2
         for k in range(count):
@@ -60,7 +60,7 @@
 
 def pick(owners, pairing, column):
     block = column[0].shape
-    rounds = pairing.shape[0]
+    rounds = pairing.shape[0] // (2 * len(column))
     shapes = [block, block, (rounds,) + block, (rounds,) + block]
     return pl.pallas_call(
         functools.partial(pick_kernel, rounds),
@@ -441,6 +441,7 @@
     win_size = lax.axis_size("win")
     chan_size = lax.axis_size("chan")
     rounds = pairing.shape[0]
+    pairing = pairing.reshape(-1)
     raw = traces[0]
 
     def exchange(block, k):
@@ -463,7 +464,7 @@
     copies, own_rest = [both[0] for both in shifted], [both[1] for both in shifted]
     aux = merge(lambda ref, chan: [ref[0]], aux_owners, aux_held, cross(aux_sent))
     partners = merge(
-        lambda ref, chan: [ref[r, chan] for r in range(rounds)], pairing, held, cross(sent)
+        lambda ref, chan: [ref[r * chan_size + chan] for r in range(rounds)], pairing, held, cross(sent)
     )
     aux_rest = [exchange(aux, k) for k in range(1, win_size)]
     pair_begun = pair_first(first_copies, partners, LAGS // win_size)

time: 84 us -> 85.9 us (1.023)
  local copies, waits for them, and re-layouts: 1.66 us -> 6.54 us
  waiting for transfers between devices: 9.53 us -> 5.9 us
    unnamed x10 -> x18, local copies, waits for them, and re-layouts: 1.66 us -> 5.78 us
    ppermute x3, waiting for transfers between devices: 8.94 us -> 5.32 us  [per_device(): lax.ppermute(raw, 'chan', [(i, (i + 2 * k) % chan_size) for i in range(ch...]
  transfers between devices with their start and end apart: 16 -> 16, of which waited for: 4 -> 4; matrix products, arithmetic and copies ran while one was open for 0% -> 1% of each run, Pallas kernels for 60% -> 60%
where the time goes in v7:
time: 85.9 us; the launch traced here: 85.4 us
  Pallas kernels  51.7 us (60%)
  starting transfers between devices  19.6 us (23%)
  local copies, waits for them, and re-layouts  6.54 us (8%)
  waiting for transfers between devices  5.9 us (7%)
  between operations  1.65 us (2%)
    pallas_call x1, Pallas kernels, coda_coherence(): pl.pallas_call(functools.partial(coda_kernel, windows), out_shape=[jax.Sh...  23.7 us
    ppermute x9, starting transfers between devices, exchange(): return lax.ppermute(block, 'win', [(i, i ^ k) for i in range(win_size)])  11.9 us
    pallas_call x1, Pallas kernels, pair_coherence(): pl.pallas_call(functools.partial(pair_kernel, windows), out_shape=jax.Sha...  11.8 us
    unnamed x18, local copies, waits for them, and re-layouts  5.78 us
    ppermute x3, waiting for transfers between devices, per_device(): lax.ppermute(raw, 'chan', [(i, (i + 2 * k) % chan_size) for i in range(ch...  5.32 us
    pallas_call x1, Pallas kernels, part_first(): pl.pallas_call(part_first_kernel, out_shape=jax.ShapeDtypeStruct((steps,...  4.82 us
    ppermute x3, starting transfers between devices, per_device(): lax.ppermute(raw, 'chan', [(i, (i + 2 * k) % chan_size) for i in range(ch...  4.61 us
    pallas_call x1, Pallas kernels, pair_first(): pl.pallas_call(pair_first_kernel, out_shape=jax.ShapeDtypeStruct((steps,...  4.19 us
  transfers between devices with their start and end apart: 16, of which 4 were waited for; matrix products, arithmetic and copies ran while one was open for 1% of the time, Pallas kernels for 60%

profile of v7, /device:TPU:8, one launch (start us, length us, event | category | flops | bytes accessed | tf_op | source)
XLA Modules:
  0.0 85.4 jit_solution(14263615642403530949)
XLA Ops:
  0.6 1.6 %collective-permute-start = (bf16[128,768]{1,0:T(8,128)(2,1)}, bf16[128,768]{1,0:T(8,128)(2,1)S(1)}, u32[]{:S(2)}, u32[]{:S(2)}) collective-permute-start(bf16[128,768]{1,0:T(8,128)(2,1)} %bitcast.1), channel_id=1, source_target_pairs={{0,1},{1,0},{2,3},{3,2},{4,5},{5,4},{6,7},{7,6},{8,9},{9,8},{10,11... | collective-permute-start | bytes 589832 | tf_op jit(solution)/shard_map/ppermute | solution.py:448
  2.2 1.5 %collective-permute-start.1 = (bf16[128,768]{1,0:T(8,128)(2,1)}, bf16[128,768]{1,0:T(8,128)(2,1)S(1)}, u32[]{:S(2)}, u32[]{:S(2)}) collective-permute-start(bf16[128,768]{1,0:T(8,128)(2,1)} %bitcast.2), channel_id=1, source_target_pairs={{0,2},{1,3},{2,0},{3,1},{4,6},{5,7},{6,4},{7,5},{8,10},{9,11},{10,... | collective-permute-start | bytes 589832 | tf_op jit(solution)/shard_map/ppermute | solution.py:448
  3.7 1.6 %collective-permute-start.2 = (bf16[128,768]{1,0:T(8,128)(2,1)}, bf16[128,768]{1,0:T(8,128)(2,1)}, u32[]{:S(2)}, u32[]{:S(2)}) collective-permute-start(bf16[128,768]{1,0:T(8,128)(2,1)} %bitcast.3), channel_id=1, source_target_pairs={{0,8},{4,12},{8,16},{12,20},{16,24},{20,28},{24,0},{28,4},{1,9},{5... | collective-permute-start | bytes 589832 | tf_op jit(solution)/shard_map/ppermute | solution.py:454
  5.3 1.2 %collective-permute-start.3 = (bf16[128,768]{1,0:T(8,128)(2,1)}, bf16[128,768]{1,0:T(8,128)(2,1)}, u32[]{:S(2)}, u32[]{:S(2)}) collective-permute-start(bf16[128,768]{1,0:T(8,128)(2,1)} %bitcast.4), channel_id=1, source_target_pairs={{0,16},{4,20},{8,24},{12,28},{16,0},{20,4},{24,8},{28,12},{1,17},{... | collective-permute-start | bytes 589832 | tf_op jit(solution)/shard_map/ppermute | solution.py:454
  6.5 1.8 %collective-permute-start.4 = (bf16[128,768]{1,0:T(8,128)(2,1)}, bf16[128,768]{1,0:T(8,128)(2,1)}, u32[]{:S(2)}, u32[]{:S(2)}) collective-permute-start(bf16[128,768]{1,0:T(8,128)(2,1)} %bitcast.5), channel_id=1, source_target_pairs={{0,24},{4,28},{8,0},{12,4},{16,8},{20,12},{24,16},{28,20},{1,25},{... | collective-permute-start | bytes 589832 | tf_op jit(solution)/shard_map/ppermute | solution.py:454
  9.0 1.7 %collective-permute-start.5 = (bf16[128,768]{1,0:T(8,128)(2,1)}, bf16[128,768]{1,0:T(8,128)(2,1)S(1)}, u32[]{:S(2)}, u32[]{:S(2)}) collective-permute-start(bf16[128,768]{1,0:T(8,128)(2,1)} %bitcast.6), channel_id=1, source_target_pairs={{0,3},{1,2},{2,1},{3,0},{4,7},{5,6},{6,5},{7,4},{8,11},{9,10},{10,... | collective-permute-start | bytes 589832 | tf_op jit(solution)/shard_map/ppermute | solution.py:448
  11.6 1.0 %shifted_copies.4 = (bf16[2048,768]{1,0:T(8,128)(2,1)S(1)}, bf16[128,768]{1,0:T(8,128)(2,1)S(1)}, bf16[128,768]{1,0:T(8,128)(2,1)S(1)}) custom-call(bf16[128,768]{1,0:T(8,128)(2,1)S(1)} %bitcast.7), custom_call_target="tpu_custom_call" | custom-call | bytes 3145728 | tf_op jit(solution)/shard_map/shifted_copies/pallas_call | solution.py:117
  16.3 1.0 %shifted_copies.5 = (bf16[2048,768]{1,0:T(8,128)(2,1)S(1)}, bf16[128,768]{1,0:T(8,128)(2,1)S(1)}) custom-call(bf16[128,768]{1,0:T(8,128)(2,1)S(1)} %copy-done.2), custom_call_target="tpu_custom_call" | custom-call | bytes 3145728 | tf_op jit(solution)/shard_map/shifted_copies/pallas_call | solution.py:117
  17.3 1.0 %shifted_copies.6 = (bf16[2048,768]{1,0:T(8,128)(2,1)S(1)}, bf16[128,768]{1,0:T(8,128)(2,1)S(1)}) custom-call(bf16[128,768]{1,0:T(8,128)(2,1)S(1)} %collective-permute-done.1.block_ref), custom_call_target="tpu_custom_call" | custom-call | bytes 3145728 | tf_op jit(solution)/shard_map/shifted_copies/pallas_call | solution.py:117
  18.3 1.1 %collective-permute-done.2.refs_1_ = bf16[128,768]{1,0:T(8,128)(2,1)} collective-permute-done((bf16[128,768]{1,0:T(8,128)(2,1)}, bf16[128,768]{1,0:T(8,128)(2,1)}, u32[]{:S(2)}, u32[]{:S(2)}) %collective-permute-start.2) | collective-permute-done | bytes 196640 | tf_op jit(solution)/shard_map/ppermute | solution.py:454
  19.4 2.5 %collective-permute-done.3.refs_2_ = bf16[128,768]{1,0:T(8,128)(2,1)} collective-permute-done((bf16[128,768]{1,0:T(8,128)(2,1)}, bf16[128,768]{1,0:T(8,128)(2,1)}, u32[]{:S(2)}, u32[]{:S(2)}) %collective-permute-start.3) | collective-permute-done | bytes 196640 | tf_op jit(solution)/shard_map/ppermute | solution.py:454
  21.8 1.8 %collective-permute-done.4.refs_3_ = bf16[128,768]{1,0:T(8,128)(2,1)} collective-permute-done((bf16[128,768]{1,0:T(8,128)(2,1)}, bf16[128,768]{1,0:T(8,128)(2,1)}, u32[]{:S(2)}, u32[]{:S(2)}) %collective-permute-start.4) | collective-permute-done | bytes 196640 | tf_op jit(solution)/shard_map/ppermute | solution.py:454
  24.5 1.4 %pick.1 = (bf16[128,768]{1,0:T(8,128)(2,1)S(1)}, bf16[128,768]{1,0:T(8,128)(2,1)S(1)}, bf16[2,128,768]{2,1,0:T(8,128)(2,1)S(1)}, bf16[2,128,768]{2,1,0:T(8,128)(2,1)S(1)}) custom-call(s32[1]{0:T(128)S(6)} %copy.9.owners_ref.scalars_ref, s32[16]{0:T(128)S(1)} %reshape.7.pairing_ref.scalars_ref, bf16[128,768]{1,0:T(8,128)(2,1)S(1)} %copy-done.4, ...), custom_call_target="tpu_custom_call" | custom-call | bytes 1048576 | tf_op jit(solution)/shard_map/pick/pallas_call | solution.py:65
  26.5 1.0 %shifted_copies.7 = (bf16[2048,768]{1,0:T(8,128)(2,1)S(1)}, bf16[128,768]{1,0:T(8,128)(2,1)S(1)}) custom-call(bf16[128,768]{1,0:T(8,128)(2,1)S(1)} %collective-permute-done.5.block_ref), custom_call_target="tpu_custom_call" | custom-call | bytes 3145728 | tf_op jit(solution)/shard_map/shifted_copies/pallas_call | solution.py:117
  28.2 1.5 %collective-permute-start.8 = (bf16[128,768]{1,0:T(8,128)(2,1)S(1)}, bf16[128,768]{1,0:T(8,128)(2,1)S(1)}, u32[]{:S(2)}, u32[]{:S(2)}) collective-permute-start(bf16[128,768]{1,0:T(8,128)(2,1)S(1)} %merge.3.aux_ref), channel_id=1, source_target_pairs={{0,1},{1,0},{2,3},{3,2},{4,5},{5,4},{6,7},{7,6},{8,9},{9,8},{10,11... | collective-permute-start | bytes 589832 | tf_op jit(solution)/shard_map/ppermute | solution.py:448
  29.7 1.5 %collective-permute-start.9 = (bf16[128,768]{1,0:T(8,128)(2,1)S(1)}, bf16[128,768]{1,0:T(8,128)(2,1)S(1)}, u32[]{:S(2)}, u32[]{:S(2)}) collective-permute-start(bf16[128,768]{1,0:T(8,128)(2,1)S(1)} %merge.3.aux_ref), channel_id=1, source_target_pairs={{0,2},{1,3},{2,0},{3,1},{4,6},{5,7},{6,4},{7,5},{8,10},{9,11},{10,... | collective-permute-start | bytes 589832 | tf_op jit(solution)/shard_map/ppermute | solution.py:448
  32.1 4.8 %part_first.1.first = f32[4,2048,256]{2,1,0:T(8,128)S(1)} custom-call(bf16[128,768]{1,0:T(8,128)(2,1)S(1)} %merge.3.aux_ref, bf16[128,768]{1,0:T(8,128)(2,1)S(1)} %copy-done.6), custom_call_target="tpu_custom_call" | custom-call | flops 2684354560 | bytes 8388608 | tf_op jit(solution)/shard_map/part_first/pallas_call | solution.py:155
  37.0 1.0 %merge.2.partner_ref = bf16[2,128,768]{2,1,0:T(8,128)(2,1)S(1)} custom-call(s32[16]{0:T(128)S(1)} %reshape.7.pairing_ref.scalars_ref, bf16[2,128,768]{2,1,0:T(8,128)(2,1)S(1)} %get-tuple-element.54.held_ref, bf16[2,128,768]{2,1,0:T(8,128)(2,1)S(1)} %collective-permute-done.6.got_ref), custom_call_target="tpu_custom_call" | custom-call | bytes 1048576 | tf_op jit(solution)/shard_map/merge/pallas_call | solution.py:91
  38.0 4.2 %pair_first.1.first_ref = f32[4,2048,256]{2,1,0:T(8,128)S(1)} custom-call(bf16[2048,768]{1,0:T(8,128)(2,1)S(1)} %get-tuple-element.60.shifted_ref, bf16[2,128,768]{2,1,0:T(8,128)(2,1)S(1)} %merge.2.partner_ref), custom_call_target="tpu_custom_call" | custom-call | flops 3221225472 | bytes 8388608 | tf_op jit(solution)/shard_map/pair_first/pallas_call | solution.py:376
  43.3 2.5 %collective-permute-start.13 = (bf16[2,128,768]{2,1,0:T(8,128)(2,1)S(1)}, bf16[2,128,768]{2,1,0:T(8,128)(2,1)S(1)}, u32[]{:S(2)}, u32[]{:S(2)}) collective-permute-start(bf16[2,128,768]{2,1,0:T(8,128)(2,1)S(1)} %merge.2.partner_ref), channel_id=1, source_target_pairs={{0,3},{1,2},{2,1},{3,0},{4,7},{5,6},{6,5},{7,4},{8,11},{9,10},{10,... | collective-permute-start | bytes 1179656 | tf_op jit(solution)/shard_map/ppermute | solution.py:448
  45.8 23.7 %coda_coherence.1 = (bf16[128,32,128]{2,1,0:T(8,128)(2,1)}, bf16[128,8,128]{2,1,0:T(8,128)(2,1)S(1)}) custom-call(s32[1,128]{1,0:T(1,128)S(1)} %copy-done.7, s32[1,128]{1,0:T(1,128)S(1)} %copy-done.8, f32[4,2048,256]{2,1,0:T(8,128)S(1)} %part_first.1.first, bf16[128,768]{1,0:T(8,128)(2,1)S(1)} %collective-permute-done.8.refs_0_, ...), custom_call_target="tpu_custom_call" | custom-call | flops 25232932864 | bytes 16777216 | tf_op jit(solution)/shard_map/coda_coherence/pallas_call | solution.py:328
  69.5 1.3 %collective-permute-start.14 = (bf16[128,8,128]{2,1,0:T(8,128)(2,1)S(1)}, bf16[128,8,128]{2,1,0:T(8,128)(2,1)S(1)}, u32[]{:S(2)}, u32[]{:S(2)}) collective-permute-start(bf16[128,8,128]{2,1,0:T(8,128)(2,1)S(1)} %get-tuple-element.79), channel_id=1, source_target_pairs={{3,0},{7,4},{11,8},{15,12},{19,16},{23,20},{27,24},{31,28}} | collective-permute-start | bytes 786440 | tf_op jit(solution)/shard_map/ppermute | solution.py:479
  70.8 1.3 %collective-permute-start.15 = (bf16[128,8,128]{2,1,0:T(8,128)(2,1)S(1)}, bf16[128,8,128]{2,1,0:T(8,128)(2,1)S(1)}, u32[]{:S(2)}, u32[]{:S(2)}) collective-permute-start(bf16[128,8,128]{2,1,0:T(8,128)(2,1)S(1)} %get-tuple-element.79), channel_id=1, source_target_pairs={{2,0},{6,4},{10,8},{14,12},{18,16},{22,20},{26,24},{30,28}} | collective-permute-start | bytes 786440 | tf_op jit(solution)/shard_map/ppermute | solution.py:479
  72.1 11.8 %pair_coherence.1 = bf16[2,128,64,128]{3,2,1,0:T(8,128)(2,1)} custom-call(f32[4,2048,256]{2,1,0:T(8,128)S(1)} %pair_first.1.first_ref, bf16[2048,768]{1,0:T(8,128)(2,1)S(1)} %get-tuple-element.67.refs_0_, bf16[2048,768]{1,0:T(8,128)(2,1)S(1)} %get-tuple-element.68.refs_1_, bf16[2048,768]{1,0:T(8,128)(2,1)S(1)} %get-tuple-element.69.refs_2_, ...), custom_call_target="tpu_custom_call" | custom-call | flops 9663676416 | bytes 16777216 | tf_op jit(solution)/shard_map/pair_coherence/pallas_call | solution.py:424
  (39 shorter events, 10.3 us)
Async XLA Ops:
  0.6 7.7 %collective-permute-start = (bf16[128,768]{1,0:T(8,128)(2,1)}, bf16[128,768]{1,0:T(8,128)(2,1)S(1)}, u32[]{:S(2)}, u32[]{:S(2)}) collective-permute-start(bf16[128,768]{1,0:T(8,128)(2,1)} %bitcast.1), channel_id=1, source_target_pairs={{0,1},{1,0},{2,3},{3,2},{4,5},{5,4},{6,7},{7,6},{8,9},{9,8},{10,11... | collective-permute-start | bytes 589832 | tf_op jit(solution)/shard_map/ppermute | solution.py:448
  2.2 15.1 %collective-permute-start.1 = (bf16[128,768]{1,0:T(8,128)(2,1)}, bf16[128,768]{1,0:T(8,128)(2,1)S(1)}, u32[]{:S(2)}, u32[]{:S(2)}) collective-permute-start(bf16[128,768]{1,0:T(8,128)(2,1)} %bitcast.2), channel_id=1, source_target_pairs={{0,2},{1,3},{2,0},{3,1},{4,6},{5,7},{6,4},{7,5},{8,10},{9,11},{10,... | collective-permute-start | bytes 589832 | tf_op jit(solution)/shard_map/ppermute | solution.py:448
  3.7 15.7 %collective-permute-start.2 = (bf16[128,768]{1,0:T(8,128)(2,1)}, bf16[128,768]{1,0:T(8,128)(2,1)}, u32[]{:S(2)}, u32[]{:S(2)}) collective-permute-start(bf16[128,768]{1,0:T(8,128)(2,1)} %bitcast.3), channel_id=1, source_target_pairs={{0,8},{4,12},{8,16},{12,20},{16,24},{20,28},{24,0},{28,4},{1,9},{5... | collective-permute-start | bytes 589832 | tf_op jit(solution)/shard_map/ppermute | solution.py:454
  5.3 16.6 %collective-permute-start.3 = (bf16[128,768]{1,0:T(8,128)(2,1)}, bf16[128,768]{1,0:T(8,128)(2,1)}, u32[]{:S(2)}, u32[]{:S(2)}) collective-permute-start(bf16[128,768]{1,0:T(8,128)(2,1)} %bitcast.4), channel_id=1, source_target_pairs={{0,16},{4,20},{8,24},{12,28},{16,0},{20,4},{24,8},{28,12},{1,17},{... | collective-permute-start | bytes 589832 | tf_op jit(solution)/shard_map/ppermute | solution.py:454
  6.5 17.1 %collective-permute-start.4 = (bf16[128,768]{1,0:T(8,128)(2,1)}, bf16[128,768]{1,0:T(8,128)(2,1)}, u32[]{:S(2)}, u32[]{:S(2)}) collective-permute-start(bf16[128,768]{1,0:T(8,128)(2,1)} %bitcast.5), channel_id=1, source_target_pairs={{0,24},{4,28},{8,0},{12,4},{16,8},{20,12},{24,16},{28,20},{1,25},{... | collective-permute-start | bytes 589832 | tf_op jit(solution)/shard_map/ppermute | solution.py:454
  9.0 16.9 %collective-permute-start.5 = (bf16[128,768]{1,0:T(8,128)(2,1)}, bf16[128,768]{1,0:T(8,128)(2,1)S(1)}, u32[]{:S(2)}, u32[]{:S(2)}) collective-permute-start(bf16[128,768]{1,0:T(8,128)(2,1)} %bitcast.6), channel_id=1, source_target_pairs={{0,3},{1,2},{2,1},{3,0},{4,7},{5,6},{6,5},{7,4},{8,11},{9,10},{10,... | collective-permute-start | bytes 589832 | tf_op jit(solution)/shard_map/ppermute | solution.py:448
  10.7 1.0 %copy-start = (bf16[1,128,768]{2,1,0:T(8,128)(2,1)S(1)}, bf16[1,128,768]{2,1,0:T(8,128)(2,1)}, u32[]{:S(2)}) copy-start(bf16[1,128,768]{2,1,0:T(8,128)(2,1)} %param.5) | copy-start | bytes 589828
  12.6 0.7 copy-start.3
  13.3 0.7 copy-start.5
  15.4 0.9 %copy-start.2 = (bf16[128,768]{1,0:T(8,128)(2,1)S(1)}, bf16[128,768]{1,0:T(8,128)(2,1)}, u32[]{:S(2)}) copy-start(bf16[128,768]{1,0:T(8,128)(2,1)} %copy-done.1) | copy-start | bytes 589828
  23.6 0.9 %copy-start.4 = (bf16[128,768]{1,0:T(8,128)(2,1)S(1)}, bf16[128,768]{1,0:T(8,128)(2,1)}, u32[]{:S(2)}) copy-start(bf16[128,768]{1,0:T(8,128)(2,1)} %copy-done.3) | copy-start | bytes 589828
  25.9 1.6 %collective-permute-start.7 = (bf16[128,768]{1,0:T(8,128)(2,1)S(1)}, bf16[128,768]{1,0:T(8,128)(2,1)S(1)}, u32[]{:S(2)}, u32[]{:S(2)}) collective-permute-start(bf16[128,768]{1,0:T(8,128)(2,1)S(1)} %get-tuple-element.59), channel_id=1, source_target_pairs={{0,4},{4,0},{8,12},{12,8},{16,20},{20,16},{24,28},{28,24},{1,5},{5... | collective-permute-start | bytes 589832 | tf_op jit(solution)/shard_map/ppermute | solution.py:451
  26.0 11.0 %collective-permute-start.6 = (bf16[2,128,768]{2,1,0:T(8,128)(2,1)S(1)}, bf16[2,128,768]{2,1,0:T(8,128)(2,1)S(1)}, u32[]{:S(2)}, u32[]{:S(2)}) collective-permute-start(bf16[2,128,768]{2,1,0:T(8,128)(2,1)S(1)} %get-tuple-element.57), channel_id=1, source_target_pairs={{0,4},{4,0},{8,12},{12,8},{16,20},{20,16},{24,28},{28,24},{1,5},{5... | collective-permute-start | bytes 1179656 | tf_op jit(solution)/shard_map/ppermute | solution.py:451
  27.6 14.6 %collective-permute-start.10 = (bf16[128,768]{1,0:T(8,128)(2,1)S(1)}, bf16[128,768]{1,0:T(8,128)(2,1)S(1)}, u32[]{:S(2)}, u32[]{:S(2)}) collective-permute-start(bf16[128,768]{1,0:T(8,128)(2,1)S(1)} %merge.3.aux_ref), channel_id=1, source_target_pairs={{0,3},{1,2},{2,1},{3,0},{4,7},{5,6},{6,5},{7,4},{8,11},{9,10},{10,... | collective-permute-start | bytes 589832 | tf_op jit(solution)/shard_map/ppermute | solution.py:448
  28.2 14.0 %collective-permute-start.8 = (bf16[128,768]{1,0:T(8,128)(2,1)S(1)}, bf16[128,768]{1,0:T(8,128)(2,1)S(1)}, u32[]{:S(2)}, u32[]{:S(2)}) collective-permute-start(bf16[128,768]{1,0:T(8,128)(2,1)S(1)} %merge.3.aux_ref), channel_id=1, source_target_pairs={{0,1},{1,0},{2,3},{3,2},{4,5},{5,4},{6,7},{7,6},{8,9},{9,8},{10,11... | collective-permute-start | bytes 589832 | tf_op jit(solution)/shard_map/ppermute | solution.py:448
  29.7 12.5 %collective-permute-start.9 = (bf16[128,768]{1,0:T(8,128)(2,1)S(1)}, bf16[128,768]{1,0:T(8,128)(2,1)S(1)}, u32[]{:S(2)}, u32[]{:S(2)}) collective-permute-start(bf16[128,768]{1,0:T(8,128)(2,1)S(1)} %merge.3.aux_ref), channel_id=1, source_target_pairs={{0,2},{1,3},{2,0},{3,1},{4,6},{5,7},{6,4},{7,5},{8,10},{9,11},{10,... | collective-permute-start | bytes 589832 | tf_op jit(solution)/shard_map/ppermute | solution.py:448
  31.2 0.9 %copy-start.6 = (bf16[128,768]{1,0:T(8,128)(2,1)S(1)}, bf16[128,768]{1,0:T(8,128)(2,1)}, u32[]{:S(2)}) copy-start(bf16[128,768]{1,0:T(8,128)(2,1)} %copy-done.5) | copy-start | bytes 589828
  38.0 7.8 %copy-start.7 = (s32[1,128]{1,0:T(1,128)S(1)}, s32[1,128]{1,0:T(1,128)}, u32[]{:S(2)}) copy-start(s32[1,128]{1,0:T(1,128)} %start_ref.1) | copy-start | bytes 1540
  38.0 7.8 %copy-start.8 = (s32[1,128]{1,0:T(1,128)S(1)}, s32[1,128]{1,0:T(1,128)}, u32[]{:S(2)}) copy-start(s32[1,128]{1,0:T(1,128)} %end_ref.1) | copy-start | bytes 1540
  42.2 29.8 %collective-permute-start.11 = (bf16[2,128,768]{2,1,0:T(8,128)(2,1)S(1)}, bf16[2,128,768]{2,1,0:T(8,128)(2,1)S(1)}, u32[]{:S(2)}, u32[]{:S(2)}) collective-permute-start(bf16[2,128,768]{2,1,0:T(8,128)(2,1)S(1)} %merge.2.partner_ref), channel_id=1, source_target_pairs={{0,1},{1,0},{2,3},{3,2},{4,5},{5,4},{6,7},{7,6},{8,9},{9,8},{10,11... | collective-permute-start | bytes 1179656 | tf_op jit(solution)/shard_map/ppermute | solution.py:448
  42.8 29.2 %collective-permute-start.12 = (bf16[2,128,768]{2,1,0:T(8,128)(2,1)S(1)}, bf16[2,128,768]{2,1,0:T(8,128)(2,1)S(1)}, u32[]{:S(2)}, u32[]{:S(2)}) collective-permute-start(bf16[2,128,768]{2,1,0:T(8,128)(2,1)S(1)} %merge.2.partner_ref), channel_id=1, source_target_pairs={{0,2},{1,3},{2,0},{3,1},{4,6},{5,7},{6,4},{7,5},{8,10},{9,11},{10,... | collective-permute-start | bytes 1179656 | tf_op jit(solution)/shard_map/ppermute | solution.py:448
  43.3 28.7 %collective-permute-start.13 = (bf16[2,128,768]{2,1,0:T(8,128)(2,1)S(1)}, bf16[2,128,768]{2,1,0:T(8,128)(2,1)S(1)}, u32[]{:S(2)}, u32[]{:S(2)}) collective-permute-start(bf16[2,128,768]{2,1,0:T(8,128)(2,1)S(1)} %merge.2.partner_ref), channel_id=1, source_target_pairs={{0,3},{1,2},{2,1},{3,0},{4,7},{5,6},{6,5},{7,4},{8,11},{9,10},{10,... | collective-permute-start | bytes 1179656 | tf_op jit(solution)/shard_map/ppermute | solution.py:448
  69.5 14.5 %collective-permute-start.14 = (bf16[128,8,128]{2,1,0:T(8,128)(2,1)S(1)}, bf16[128,8,128]{2,1,0:T(8,128)(2,1)S(1)}, u32[]{:S(2)}, u32[]{:S(2)}) collective-permute-start(bf16[128,8,128]{2,1,0:T(8,128)(2,1)S(1)} %get-tuple-element.79), channel_id=1, source_target_pairs={{3,0},{7,4},{11,8},{15,12},{19,16},{23,20},{27,24},{31,28}} | collective-permute-start | bytes 786440 | tf_op jit(solution)/shard_map/ppermute | solution.py:479
  70.8 13.7 %collective-permute-start.15 = (bf16[128,8,128]{2,1,0:T(8,128)(2,1)S(1)}, bf16[128,8,128]{2,1,0:T(8,128)(2,1)S(1)}, u32[]{:S(2)}, u32[]{:S(2)}) collective-permute-start(bf16[128,8,128]{2,1,0:T(8,128)(2,1)S(1)} %get-tuple-element.79), channel_id=1, source_target_pairs={{2,0},{6,4},{10,8},{14,12},{18,16},{22,20},{26,24},{30,28}} | collective-permute-start | bytes 786440 | tf_op jit(solution)/shard_map/ppermute | solution.py:479
  (1 other events, 0.7 us)
